TPU v7x, 256 devices: a whole 4x4x8 slice. The times are simulated.
256 devices in a mesh: seq: 32 (over z, x_lo, core), chan: 8 (over x_hi, y).
Axes of the slice: x: 4 (x_hi: 2, x_lo: 2; x = x_hi * 2 + x_lo), y: 4, z: 8, core: 2. Of those that a mesh axis runs over, the one named last changes fastest.
Arguments:
- q_gate: float32 [16384, 2048], P('seq', 'chan'), may hold values from -6 to 6
- k_gate: float32 [16384, 2048], P('seq', 'chan'), may hold values from -6 to 6
- values: float32 [16384, 2048], P('seq', 'chan'), may hold values from -6 to 6
- filter_raw: float32 [16384, 128], P('seq'), may hold values from -6 to 6
- grad_out: float32 [16384, 2048], P('seq', 'chan'), may hold values from -6 to 6
Outputs:
- grad_q: float32 [16384, 2048], P('seq', 'chan')
- grad_k: float32 [16384, 2048], P('seq', 'chan')
- grad_v: float32 [16384, 2048], P('seq', 'chan')
- grad_filter: float32 [16384, 128], P('seq')
All inputs are finite; a program needn't handle non-finite values.
Results may differ from a plain program's by a relative error of at most 0.0001.
Values sent between devices are 32-bit elements; how exact they have to be, the bound alone decides.
No kernel may reach another device: no remote copies, remote signals or barrier semaphores. Data moves between devices by JAX's collectives and lax.ppermute only.
A program may use at most 64 MiB of HBM per device.

v0:
```python
import math

import jax
import jax.numpy as jnp
from jax import lax
from jax.sharding import PartitionSpec as P


def product_hi(form, left, right):
    return jnp.einsum(form, left, right, precision=lax.Precision.HIGHEST)


def angle_table(first, second, modulus):
    counts = first[:, None] * second[None, :] % modulus
    angles = counts.astype(jnp.float32) * (2.0 * math.pi / modulus)
    return (jnp.cos(angles), jnp.sin(angles))


def forward_transform(block, shards, offset_base, cos_coarse, sin_coarse, cos_fine, sin_fine):
    seq_len = block.shape[0]
    coarse = 2 * shards
    total = coarse * seq_len
    share = seq_len // shards
    spread = lax.all_to_all(block[None], "seq", split_axis=1, concat_axis=0, tiled=True)
    real_part = product_hi("kn,nbw->kbw", cos_coarse, spread)
    imag_part = -product_hi("kn,nbw->kbw", sin_coarse, spread)
    offsets = offset_base * share + jnp.arange(share, dtype=jnp.int32)
    freq_rows = jnp.arange(coarse, dtype=jnp.int32)
    twist_cos, twist_sin = angle_table(freq_rows, offsets, total)
    twist_cos = twist_cos[:, :, None]
    twist_sin = twist_sin[:, :, None]
    turned_real = real_part * twist_cos + imag_part * twist_sin
    turned_imag = imag_part * twist_cos - real_part * twist_sin
    moved_real, moved_imag = (
        lax.all_to_all(turned_real, "seq", split_axis=0, concat_axis=1, tiled=True),
        lax.all_to_all(turned_imag, "seq", split_axis=0, concat_axis=1, tiled=True),
    )
    spec_real = product_hi("kn,tnw->tkw", cos_fine, moved_real) + product_hi(
        "kn,tnw->tkw", sin_fine, moved_imag
    )
    spec_imag = product_hi("kn,tnw->tkw", cos_fine, moved_imag) - product_hi(
        "kn,tnw->tkw", sin_fine, moved_real
    )
    return (spec_real, spec_imag)


def inverse_transform(spec_real, spec_imag, shards, offset_base, cos_fine, sin_fine):
    seq_len = spec_real.shape[1]
    coarse = 2 * shards
    total = coarse * seq_len
    part_real = product_hi("nk,tkw->tnw", cos_fine, spec_real) - product_hi(
        "nk,tkw->tnw", sin_fine, spec_imag
    )
    part_imag = product_hi("nk,tkw->tnw", cos_fine, spec_imag) + product_hi(
        "nk,tkw->tnw", sin_fine, spec_real
    )
    local_freq = 2 * offset_base + jnp.arange(2, dtype=jnp.int32)
    positions = jnp.arange(seq_len, dtype=jnp.int32)
    twist_cos, twist_sin = angle_table(local_freq, positions, total)
    twist_cos = twist_cos[:, :, None]
    twist_sin = twist_sin[:, :, None]
    turned_real = part_real * twist_cos - part_imag * twist_sin
    turned_imag = part_imag * twist_cos + part_real * twist_sin
    moved_real, moved_imag = (
        lax.all_to_all(turned_real, "seq", split_axis=1, concat_axis=0, tiled=True),
        lax.all_to_all(turned_imag, "seq", split_axis=1, concat_axis=0, tiled=True),
    )
    rows_out = jnp.arange(shards, dtype=jnp.int32)
    freq_rows = jnp.arange(coarse, dtype=jnp.int32)
    back_cos, back_sin = angle_table(rows_out, freq_rows, coarse)
    spatial = (
        product_hi("nk,kbw->nbw", back_cos, moved_real)
        - product_hi("nk,kbw->nbw", back_sin, moved_imag)
    ) * (1.0 / total)
    placed = lax.all_to_all(spatial, "seq", split_axis=0, concat_axis=1, tiled=True)
    return placed[0]


def local(q_gate, k_gate, values, filter_raw, grad_out):
    seq_len = q_gate.shape[0]
    width = q_gate.shape[1]
    nfilt = filter_raw.shape[1]
    shards = lax.axis_size("seq")
    offset_base = lax.axis_index("seq")
    scale = float(seq_len * shards) ** (-0.5)
    coarse_rows = jnp.arange(2 * shards, dtype=jnp.int32)
    cos_coarse, sin_coarse = angle_table(
        coarse_rows, jnp.arange(shards, dtype=jnp.int32), 2 * shards
    )
    fine_rows = jnp.arange(seq_len, dtype=jnp.int32)
    cos_fine, sin_fine = angle_table(fine_rows, fine_rows, seq_len)
    gated = k_gate * values
    grad_conv = grad_out * q_gate
    filt = filter_raw * scale

    def forward(block):
        return forward_transform(
            block, shards, offset_base, cos_coarse, sin_coarse, cos_fine, sin_fine
        )

    def inverse(real_part, imag_part):
        return inverse_transform(real_part, imag_part, shards, offset_base, cos_fine, sin_fine)

    gated_real, gated_imag = forward(gated)
    grad_real, grad_imag = forward(grad_conv)
    filt_real, filt_imag = forward(filt)
    repeats = width // nfilt
    wide_real = jnp.tile(filt_real, (1, 1, repeats))
    wide_imag = jnp.tile(filt_imag, (1, 1, repeats))
    conv_real = wide_real * gated_real - wide_imag * gated_imag
    conv_imag = wide_real * gated_imag + wide_imag * gated_real
    back_real = wide_real * grad_real + wide_imag * grad_imag
    back_imag = wide_real * grad_imag - wide_imag * grad_real
    corr_real = gated_real * grad_real + gated_imag * grad_imag
    corr_imag = gated_real * grad_imag - gated_imag * grad_real
    folded_real = jnp.sum(corr_real.reshape(2, seq_len, repeats, nfilt), axis=2)
    folded_imag = jnp.sum(corr_imag.reshape(2, seq_len, repeats, nfilt), axis=2)
    filter_real, filter_imag = (folded_real, folded_imag)
    conv = inverse(conv_real, conv_imag)
    grad_gated = inverse(back_real, back_imag)
    corr = inverse(filter_real, filter_imag)
    grad_filter = lax.psum(corr, "chan") * scale
    grad_q = grad_out * conv
    grad_k = grad_gated * values
    grad_v = grad_gated * k_gate
    return (grad_q, grad_k, grad_v, grad_filter)


def solution(mesh):
    placed = (
        P("seq", "chan"),
        P("seq", "chan"),
        P("seq", "chan"),
        P("seq", None),
        P("seq", "chan"),
    )
    return jax.shard_map(
        local,
        mesh=mesh,
        in_specs=placed,
        out_specs=(P("seq", "chan"), P("seq", "chan"), P("seq", "chan"), P("seq", None)),
        check_vma=False,
    )
```

profile of v0, /device:TPU:32, one launch (start us, length us, event | category | flops | bytes accessed | tf_op | source)
XLA Modules:
  0.0 699.3 jit_solution(10144373009887755012)
XLA Ops:
  8.9 9.7 %all-to-all-start = ((f32[1,512,128]{2,0,1:T(1,128)}), f32[1,512,128]{2,0,1:T(1,128)S(1)}, u32[]{:S(2)}, u32[]{:S(2)}) async-start(f32[1,512,128]{2,0,1:T(1,128)} %bitcast.3), calls=%async_computation | async-start | bytes 524288 | tf_op jit(solution)/shard_map/all_to_all | solution.py:24
  19.9 10.2 %all-to-all-done = f32[1,512,128]{2,0,1:T(1,128)S(1)} async-done(((f32[1,512,128]{2,0,1:T(1,128)}), f32[1,512,128]{2,0,1:T(1,128)S(1)}, u32[]{:S(2)}, u32[]{:S(2)}) %all-to-all-start) | async-done | bytes 262176 | tf_op jit(solution)/shard_map/all_to_all | solution.py:24
  36.1 15.6 %all-to-all-done.3 = f32[1,512,256]{2,0,1:T(1,128)S(1)} async-done(((f32[1,512,256]{2,0,1:T(1,128)}), f32[1,512,256]{2,0,1:T(1,128)S(1)}, u32[]{:S(2)}, u32[]{:S(2)}) %all-to-all-start.3) | async-done | bytes 524320 | tf_op jit(solution)/shard_map/all_to_all | solution.py:24
  59.5 14.1 %all-to-all-done.9 = f32[1,512,256]{2,0,1:T(1,128)S(1)} async-done(((f32[1,512,256]{2,0,1:T(1,128)}), f32[1,512,256]{2,0,1:T(1,128)S(1)}, u32[]{:S(2)}, u32[]{:S(2)}) %all-to-all-start.9) | async-done | bytes 524320 | tf_op jit(solution)/shard_map/all_to_all | solution.py:24
  79.7 15.7 %all-to-all-done.2 = f32[64,16,128]{2,1,0:T(8,128)S(1)} async-done(((f32[64,16,128]{2,1,0:T(8,128)}), f32[64,16,128]{2,1,0:T(8,128)S(1)}, u32[]{:S(2)}, u32[]{:S(2)}) %all-to-all-start.2) | async-done | bytes 524320 | tf_op jit(solution)/shard_map/all_to_all | solution.py:36
  96.3 5.7 all-to-all-start.1
  109.2 9.6 %all-to-all-done.1 = f32[64,16,128]{2,1,0:T(8,128)} async-done(((f32[64,16,128]{2,1,0:T(8,128)}), f32[64,16,128]{2,1,0:T(8,128)}, u32[]{:S(2)}, u32[]{:S(2)}) %all-to-all-start.1) | async-done | bytes 524320 | tf_op jit(solution)/shard_map/all_to_all | solution.py:35
  118.9 5.9 all-to-all-start.10
  126.3 26.6 %all-to-all-done.10 = f32[64,16,256]{2,1,0:T(8,128)} async-done(((f32[64,16,256]{2,1,0:T(8,128)}), f32[64,16,256]{2,1,0:T(8,128)}, u32[]{:S(2)}, u32[]{:S(2)}) %all-to-all-start.10) | async-done | bytes 1048608 | tf_op jit(solution)/shard_map/all_to_all | solution.py:35
  159.5 26.5 %all-to-all-done.11 = f32[64,16,256]{2,1,0:T(8,128)S(1)} async-done(((f32[64,16,256]{2,1,0:T(8,128)}), f32[64,16,256]{2,1,0:T(8,128)S(1)}, u32[]{:S(2)}, u32[]{:S(2)}) %all-to-all-start.11) | async-done | bytes 1048608 | tf_op jit(solution)/shard_map/all_to_all | solution.py:36
  192.9 26.3 %all-to-all-done.4 = f32[64,16,256]{2,1,0:T(8,128)S(1)} async-done(((f32[64,16,256]{2,1,0:T(8,128)}), f32[64,16,256]{2,1,0:T(8,128)S(1)}, u32[]{:S(2)}, u32[]{:S(2)}) %all-to-all-start.4) | async-done | bytes 1048608 | tf_op jit(solution)/shard_map/all_to_all | solution.py:35
  219.2 5.7 all-to-all-start.5
  224.9 5.8 fusion.46
  231.8 5.8 fusion.50
  237.6 6.4 fusion.4
  244.0 6.7 fusion.5
  252.2 7.5 %fusion.38 = f32[2,256,512]{2,1,0:T(8,128)S(1)} fusion(f32[2,512,256]{2,1,0:T(8,128)S(1)} %bitcast.255), kind=kOutput, calls=%fused_computation.67 | convolution fusion | flops 1614282752 | bytes 2097152 | tf_op jit(solution)/shard_map/kn,tnw->tkw/dot_general | solution.py:10
  259.7 8.0 %fusion.48 = f32[2,256,512]{2,1,0:T(8,128)} fusion(f32[2,512,256]{2,1,0:T(8,128)S(1)} %bitcast.238), kind=kOutput, calls=%fused_computation.77 | convolution fusion | flops 1614282752 | bytes 2097152 | tf_op jit(solution)/shard_map/kn,tnw->tkw/dot_general | solution.py:10
  267.7 8.0 %fusion.36 = f32[2,256,512]{2,1,0:T(8,128)} fusion(f32[2,512,256]{2,1,0:T(8,128)S(1)} %bitcast.257), kind=kOutput, calls=%fused_computation.65 | convolution fusion | flops 1614282752 | bytes 2097152 | tf_op jit(solution)/shard_map/kn,tnw->tkw/dot_general | solution.py:10
  275.7 8.2 %fusion.1 = f32[2,512,256]{1,2,0:T(8,128)} fusion(f32[2,256,512]{2,1,0:T(8,128)S(1)} %fusion.38, f32[2,512,256]{2,1,0:T(8,128)S(1)} %bitcast.258), kind=kOutput, calls=%fused_computation.18 | convolution fusion | flops 1614544896 | bytes 3145728 | tf_op jit(solution)/shard_map/kn,tnw->tkw/dot_general | solution.py:10
  285.2 7.5 %fusion.44 = f32[2,256,512]{2,1,0:T(8,128)S(1)} fusion(f32[2,512,256]{2,1,0:T(8,128)S(1)} %bitcast.259), kind=kOutput, calls=%fused_computation.73 | convolution fusion | flops 1614282752 | bytes 2097152 | tf_op jit(solution)/shard_map/kn,tnw->tkw/dot_general | solution.py:10
  292.7 7.6 %fusion.3 = f32[2,512,256]{1,2,0:T(8,128)S(1)} fusion(f32[2,256,512]{2,1,0:T(8,128)S(1)} %copy-done.28, f32[2,512,256]{2,1,0:T(8,128)S(1)} %bitcast.260), kind=kOutput, calls=%fused_computation.24 | convolution fusion | flops 1614544896 | bytes 3145728 | tf_op jit(solution)/shard_map/kn,tnw->tkw/dot_general | solution.py:10
  300.3 7.8 %fusion = f32[2,512,256]{1,2,0:T(8,128)S(1)} fusion(f32[2,256,512]{2,1,0:T(8,128)S(1)} %copy-done.26, f32[2,512,256]{2,1,0:T(8,128)S(1)} %bitcast.256), kind=kOutput, calls=%fused_computation.16 | convolution fusion | flops 1614544896 | bytes 3145728 | tf_op jit(solution)/shard_map/kn,tnw->tkw/dot_general | solution.py:10
  308.2 11.9 %multiply_add_fusion = (f32[2,512,256]{1,2,0:T(8,128)S(1)}, f32[2,512,256]{1,2,0:T(8,128)S(1)}, f32[2,512,256]{1,2,0:T(8,128)}, f32[2,512,256]{1,2,0:T(8,128)}, ...) fusion(f32[2,512,256]{1,2,0:T(8,128)S(1)} %fusion, f32[2,512,256]{1,2,0:T(8,128)S(1)} %fusion.3, ...), kind=kOutput, calls=%fused_computation.82 | convolution fusion | flops 1619263488 | bytes 12582912 | tf_op jit(solution)/shard_map/kn,tnw->tkw/dot_general | solution.py:10
  320.1 5.3 fusion.28
  325.6 5.7 fusion.30
  331.3 5.3 convolution_add_fusion.4
  336.7 5.4 add_bitcast_fusion.2
  343.1 8.8 %all-to-all-start.15 = ((f32[2,512,128]{2,0,1:T(2,128)}), f32[2,512,128]{2,0,1:T(2,128)S(1)}, u32[]{:S(2)}, u32[]{:S(2)}) async-start(f32[2,512,128]{2,0,1:T(2,128)} %copy.151), calls=%async_computation.15 | async-start | bytes 1048576 | tf_op jit(solution)/shard_map/all_to_all | solution.py:65
  352.9 6.3 fusion.32
  359.2 6.7 fusion.34
  365.9 6.7 convolution_add_fusion
  372.6 8.7 %all-to-all-start.16 = ((f32[2,512,128]{2,0,1:T(2,128)}), f32[2,512,128]{2,0,1:T(2,128)S(1)}, u32[]{:S(2)}, u32[]{:S(2)}) async-start(f32[2,512,128]{2,0,1:T(2,128)} %copy.154), calls=%async_computation.16 | async-start | bytes 1048576 | tf_op jit(solution)/shard_map/all_to_all | solution.py:66
  381.4 6.3 fusion.40
  387.7 6.7 convolution_subtract_fusion
  394.4 6.7 convolution_add_fusion.2
  403.8 8.8 %all-to-all-start.17 = ((f32[32,16,128]{2,1,0:T(8,128)}), f32[32,16,128]{2,1,0:T(8,128)S(1)}, u32[]{:S(2)}, u32[]{:S(2)}) async-start(f32[32,16,128]{2,1,0:T(8,128)} %copy.157), calls=%async_computation.17 | async-start | bytes 524288 | tf_op jit(solution)/shard_map/all_to_all | solution.py:75
  412.7 6.3 fusion.42
  419.0 7.3 %add_bitcast_fusion = (f32[2,512,256]{1,2,0:T(8,128)}, f32[2,512,256]{1,2,0:T(8,128)S(1)}, f32[2,512,256]{1,2,0:T(8,128)}, f32[2,512,256]{1,2,0:T(8,128)S(1)}) fusion(f32[2,256,512]{2,1,0:T(8,128)S(1)} %copy-done.21, f32[2,256,512]{2,1,0:T(8,128)S(1)} %copy-done.20, f32[2,512]{1,0:T(2,128)S(1)} %get-tuple-element.33, f32[2,512]{1,0:T(2,128)S(1)} %get-tuple-element.32, ...), kind=kOutput, calls=%fused_computation.83 | convolution fusion | flops 1617690624 | bytes 9445376 | tf_op jit(solution)/shard_map/nk,tkw->tnw/dot_general | solution.py:10
  428.3 8.3 %all-to-all-start.12 = ((f32[2,512,256]{2,0,1:T(2,128)}), f32[2,512,256]{2,0,1:T(2,128)S(1)}, u32[]{:S(2)}, u32[]{:S(2)}) async-start(f32[2,512,256]{2,0,1:T(2,128)} %copy.144), calls=%async_computation.12 | async-start | bytes 2097152 | tf_op jit(solution)/shard_map/all_to_all | solution.py:65
  437.9 26.7 %all-to-all-done.12 = f32[2,512,256]{2,0,1:T(2,128)S(1)} async-done(((f32[2,512,256]{2,0,1:T(2,128)}), f32[2,512,256]{2,0,1:T(2,128)S(1)}, u32[]{:S(2)}, u32[]{:S(2)}) %all-to-all-start.12) | async-done | bytes 1048608 | tf_op jit(solution)/shard_map/all_to_all | solution.py:65
  471.3 25.8 %all-to-all-done.13 = f32[2,512,256]{2,0,1:T(2,128)S(1)} async-done(((f32[2,512,256]{2,0,1:T(2,128)}), f32[2,512,256]{2,0,1:T(2,128)S(1)}, u32[]{:S(2)}, u32[]{:S(2)}) %all-to-all-start.13) | async-done | bytes 1048608 | tf_op jit(solution)/shard_map/all_to_all | solution.py:66
  504.5 26.8 %all-to-all-done.6 = f32[2,512,256]{2,0,1:T(2,128)S(1)} async-done(((f32[2,512,256]{2,0,1:T(2,128)}), f32[2,512,256]{2,0,1:T(2,128)S(1)}, u32[]{:S(2)}, u32[]{:S(2)}) %all-to-all-start.6) | async-done | bytes 1048608 | tf_op jit(solution)/shard_map/all_to_all | solution.py:65
  531.3 5.3 all-to-all-start.7
  549.4 15.2 %all-to-all-done.7 = f32[2,512,256]{2,0,1:T(2,128)S(1)} async-done(((f32[2,512,256]{2,0,1:T(2,128)}), f32[2,512,256]{2,0,1:T(2,128)S(1)}, u32[]{:S(2)}, u32[]{:S(2)}) %all-to-all-start.7) | async-done | bytes 1048608 | tf_op jit(solution)/shard_map/all_to_all | solution.py:66
  564.6 5.6 all-to-all-start.14
  576.0 11.2 %all-to-all-done.14 = f32[32,16,256]{2,1,0:T(8,128)} async-done(((f32[32,16,256]{2,1,0:T(8,128)}), f32[32,16,256]{2,1,0:T(8,128)}, u32[]{:S(2)}, u32[]{:S(2)}) %all-to-all-start.14) | async-done | bytes 524320 | tf_op jit(solution)/shard_map/all_to_all | solution.py:75
  593.1 94.4 %all-reduce.2.cloned.1.call-done = f32[512,128]{1,0:T(8,128)} async-done(((f32[512,128]{1,0:T(8,128)}), f32[512,128]{1,0:T(8,128)}) %all-reduce.2.cloned.1.call-update) | async-done | bytes 262160 | tf_op jit(solution)/shard_map/psum | solution.py:122
  (138 shorter events, 101.1 us)
Async XLA Ops:
  7.2 11.4 %copy-start.6 = (f32[512,256]{1,0:T(8,128)S(1)}, f32[512,256]{1,0:T(8,128)}, u32[]{:S(2)}) copy-start(f32[512,256]{1,0:T(8,128)} %param.6) | copy-start | bytes 1572868
  7.2 11.4 %copy-start.8 = (f32[512,256]{1,0:T(8,128)S(1)}, f32[512,256]{1,0:T(8,128)}, u32[]{:S(2)}) copy-start(f32[512,256]{1,0:T(8,128)} %param.7) | copy-start | bytes 1572868
  8.9 21.1 %all-to-all-start = ((f32[1,512,128]{2,0,1:T(1,128)}), f32[1,512,128]{2,0,1:T(1,128)S(1)}, u32[]{:S(2)}, u32[]{:S(2)}) async-start(f32[1,512,128]{2,0,1:T(1,128)} %bitcast.3), calls=%async_computation | async-start | bytes 524288 | tf_op jit(solution)/shard_map/all_to_all | solution.py:24
  19.9 14.9 %copy-start.10 = (f32[512,256]{1,0:T(8,128)S(1)}, f32[512,256]{1,0:T(8,128)}, u32[]{:S(2)}) copy-start(f32[512,256]{1,0:T(8,128)} %param.9) | copy-start | bytes 1572868
  19.9 14.9 %copy-start.23 = (f32[512,256]{1,0:T(8,128)S(1)}, f32[512,256]{1,0:T(8,128)}, u32[]{:S(2)}) copy-start(f32[512,256]{1,0:T(8,128)} %param.5) | copy-start | bytes 1572868
  30.0 21.6 %all-to-all-start.3 = ((f32[1,512,256]{2,0,1:T(1,128)}), f32[1,512,256]{2,0,1:T(1,128)S(1)}, u32[]{:S(2)}, u32[]{:S(2)}) async-start(f32[1,512,256]{2,0,1:T(1,128)} %broadcast_in_dim.7), calls=%async_computation.3 | async-start | bytes 1048576 | tf_op jit(solution)/shard_map/all_to_all | solution.py:24
  51.7 21.9 %all-to-all-start.9 = ((f32[1,512,256]{2,0,1:T(1,128)}), f32[1,512,256]{2,0,1:T(1,128)S(1)}, u32[]{:S(2)}, u32[]{:S(2)}) async-start(f32[1,512,256]{2,0,1:T(1,128)} %broadcast_in_dim.8), calls=%async_computation.9 | async-start | bytes 1048576 | tf_op jit(solution)/shard_map/all_to_all | solution.py:24
  73.6 21.9 %all-to-all-start.2 = ((f32[64,16,128]{2,1,0:T(8,128)}), f32[64,16,128]{2,1,0:T(8,128)S(1)}, u32[]{:S(2)}, u32[]{:S(2)}) async-start(f32[64,16,128]{2,1,0:T(8,128)} %copy.112), calls=%async_computation.2 | async-start | bytes 1048576 | tf_op jit(solution)/shard_map/all_to_all | solution.py:36
  95.5 0.8 copy-start.12
  96.3 22.6 %all-to-all-start.1 = ((f32[64,16,128]{2,1,0:T(8,128)}), f32[64,16,128]{2,1,0:T(8,128)}, u32[]{:S(2)}, u32[]{:S(2)}) async-start(f32[64,16,128]{2,1,0:T(8,128)} %copy.109), calls=%async_computation.1 | async-start | bytes 1048576 | tf_op jit(solution)/shard_map/all_to_all | solution.py:35
  118.9 34.1 %all-to-all-start.10 = ((f32[64,16,256]{2,1,0:T(8,128)}), f32[64,16,256]{2,1,0:T(8,128)}, u32[]{:S(2)}, u32[]{:S(2)}) async-start(f32[64,16,256]{2,1,0:T(8,128)} %copy.136), calls=%async_computation.10 | async-start | bytes 2097152 | tf_op jit(solution)/shard_map/all_to_all | solution.py:35
  152.9 33.1 %all-to-all-start.11 = ((f32[64,16,256]{2,1,0:T(8,128)}), f32[64,16,256]{2,1,0:T(8,128)S(1)}, u32[]{:S(2)}, u32[]{:S(2)}) async-start(f32[64,16,256]{2,1,0:T(8,128)} %copy.139), calls=%async_computation.11 | async-start | bytes 2097152 | tf_op jit(solution)/shard_map/all_to_all | solution.py:36
  186.0 33.1 %all-to-all-start.4 = ((f32[64,16,256]{2,1,0:T(8,128)}), f32[64,16,256]{2,1,0:T(8,128)S(1)}, u32[]{:S(2)}, u32[]{:S(2)}) async-start(f32[64,16,256]{2,1,0:T(8,128)} %copy.117), calls=%async_computation.4 | async-start | bytes 2097152 | tf_op jit(solution)/shard_map/all_to_all | solution.py:35
  191.2 1.6 copy-start.13
  219.2 64.7 %all-to-all-start.5 = ((f32[64,16,256]{2,1,0:T(8,128)}), f32[64,16,256]{2,1,0:T(8,128)}, u32[]{:S(2)}, u32[]{:S(2)}) async-start(f32[64,16,256]{2,1,0:T(8,128)} %copy.120), calls=%async_computation.5 | async-start | bytes 2097152 | tf_op jit(solution)/shard_map/all_to_all | solution.py:36
  285.2 7.5 %copy-start.28 = (f32[2,256,512]{2,1,0:T(8,128)S(1)}, f32[2,256,512]{2,1,0:T(8,128)}, u32[]{:S(2)}) copy-start(f32[2,256,512]{2,1,0:T(8,128)} %fusion.48) | copy-start | bytes 3145732
  292.7 7.6 %copy-start.26 = (f32[2,256,512]{2,1,0:T(8,128)S(1)}, f32[2,256,512]{2,1,0:T(8,128)}, u32[]{:S(2)}) copy-start(f32[2,256,512]{2,1,0:T(8,128)} %fusion.36) | copy-start | bytes 3145732
  300.3 7.8 %copy-start.18 = (f32[2,512,256]{1,2,0:T(8,128)S(1)}, f32[2,512,256]{1,2,0:T(8,128)}, u32[]{:S(2)}) copy-start(f32[2,512,256]{1,2,0:T(8,128)} %fusion.1) | copy-start | bytes 3145732
  300.3 7.8 %copy-start.24 = (f32[2,512,128]{1,2,0:T(8,128)S(1)}, f32[2,512,128]{1,2,0:T(8,128)}, u32[]{:S(2)}) copy-start(f32[2,512,128]{1,2,0:T(8,128)} %fusion.4) | copy-start | bytes 1572868
  300.3 7.8 %copy-start.25 = (f32[2,512,128]{1,2,0:T(8,128)S(1)}, f32[2,512,128]{1,2,0:T(8,128)}, u32[]{:S(2)}) copy-start(f32[2,512,128]{1,2,0:T(8,128)} %fusion.5) | copy-start | bytes 1572868
  343.1 9.8 %copy-start.15 = (f32[2,512,256]{1,2,0:T(8,128)S(1)}, f32[2,512,256]{1,2,0:T(8,128)}, u32[]{:S(2)}) copy-start(f32[2,512,256]{1,2,0:T(8,128)} %get-tuple-element.18) | copy-start | bytes 3145732
  343.1 29.5 %all-to-all-start.15 = ((f32[2,512,128]{2,0,1:T(2,128)}), f32[2,512,128]{2,0,1:T(2,128)S(1)}, u32[]{:S(2)}, u32[]{:S(2)}) async-start(f32[2,512,128]{2,0,1:T(2,128)} %copy.151), calls=%async_computation.15 | async-start | bytes 1048576 | tf_op jit(solution)/shard_map/all_to_all | solution.py:65
  352.8 6.3 copy-start.17
  372.6 8.7 %copy-start.4 = (f32[2,512,256]{1,2,0:T(8,128)S(1)}, f32[2,512,256]{1,2,0:T(8,128)}, u32[]{:S(2)}) copy-start(f32[2,512,256]{1,2,0:T(8,128)} %get-tuple-element.20) | copy-start | bytes 3145732
  372.6 29.5 %all-to-all-start.16 = ((f32[2,512,128]{2,0,1:T(2,128)}), f32[2,512,128]{2,0,1:T(2,128)S(1)}, u32[]{:S(2)}, u32[]{:S(2)}) async-start(f32[2,512,128]{2,0,1:T(2,128)} %copy.154), calls=%async_computation.16 | async-start | bytes 1048576 | tf_op jit(solution)/shard_map/all_to_all | solution.py:66
  381.3 6.4 copy-start.16
  381.3 6.4 copy-start.27
  387.7 6.7 copy-start.14
  403.8 23.8 %all-to-all-start.17 = ((f32[32,16,128]{2,1,0:T(8,128)}), f32[32,16,128]{2,1,0:T(8,128)S(1)}, u32[]{:S(2)}, u32[]{:S(2)}) async-start(f32[32,16,128]{2,1,0:T(8,128)} %copy.157), calls=%async_computation.17 | async-start | bytes 524288 | tf_op jit(solution)/shard_map/all_to_all | solution.py:75
  412.6 6.4 copy-start.20
  412.6 6.4 copy-start.21
  412.7 6.4 copy-start.22
  427.6 9.0 %copy-start.5 = (f32[2,512,256]{1,2,0:T(8,128)S(1)}, f32[2,512,256]{1,2,0:T(8,128)}, u32[]{:S(2)}) copy-start(f32[2,512,256]{1,2,0:T(8,128)} %get-tuple-element.14) | copy-start | bytes 3145732
  427.6 0.7 copy-start.19
  428.3 36.3 %all-to-all-start.12 = ((f32[2,512,256]{2,0,1:T(2,128)}), f32[2,512,256]{2,0,1:T(2,128)S(1)}, u32[]{:S(2)}, u32[]{:S(2)}) async-start(f32[2,512,256]{2,0,1:T(2,128)} %copy.144), calls=%async_computation.12 | async-start | bytes 2097152 | tf_op jit(solution)/shard_map/all_to_all | solution.py:65
  464.6 32.5 %all-to-all-start.13 = ((f32[2,512,256]{2,0,1:T(2,128)}), f32[2,512,256]{2,0,1:T(2,128)S(1)}, u32[]{:S(2)}, u32[]{:S(2)}) async-start(f32[2,512,256]{2,0,1:T(2,128)} %copy.147), calls=%async_computation.13 | async-start | bytes 2097152 | tf_op jit(solution)/shard_map/all_to_all | solution.py:66
  497.2 1.0 copy-start
  498.2 33.1 %all-to-all-start.6 = ((f32[2,512,256]{2,0,1:T(2,128)}), f32[2,512,256]{2,0,1:T(2,128)S(1)}, u32[]{:S(2)}, u32[]{:S(2)}) async-start(f32[2,512,256]{2,0,1:T(2,128)} %copy.127), calls=%async_computation.6 | async-start | bytes 2097152 | tf_op jit(solution)/shard_map/all_to_all | solution.py:65
  531.3 33.3 %all-to-all-start.7 = ((f32[2,512,256]{2,0,1:T(2,128)}), f32[2,512,256]{2,0,1:T(2,128)S(1)}, u32[]{:S(2)}, u32[]{:S(2)}) async-start(f32[2,512,256]{2,0,1:T(2,128)} %copy.130), calls=%async_computation.7 | async-start | bytes 2097152 | tf_op jit(solution)/shard_map/all_to_all | solution.py:66
  538.5 3.0 copy-start.1
  543.4 3.0 copy-start.2
  546.4 1.2 copy-start.3
  564.6 22.6 %all-to-all-start.14 = ((f32[32,16,256]{2,1,0:T(8,128)}), f32[32,16,256]{2,1,0:T(8,128)}, u32[]{:S(2)}, u32[]{:S(2)}) async-start(f32[32,16,256]{2,1,0:T(8,128)} %copy.150), calls=%async_computation.14 | async-start | bytes 1048576 | tf_op jit(solution)/shard_map/all_to_all | solution.py:75
  587.2 102.0 %copy-start.9 = (f32[512,256]{1,0:T(8,128)S(1)}, f32[512,256]{1,0:T(8,128)}, u32[]{:S(2)}) copy-start(f32[512,256]{1,0:T(8,128)} %param.7) | copy-start | bytes 1572868
  587.2 104.2 %all-to-all-start.8 = ((f32[32,16,256]{2,1,0:T(8,128)}), f32[32,16,256]{2,1,0:T(8,128)S(1)}, u32[]{:S(2)}, u32[]{:S(2)}) async-start(f32[32,16,256]{2,1,0:T(8,128)} %copy.133), calls=%async_computation.8 | async-start | bytes 1048576 | tf_op jit(solution)/shard_map/all_to_all | solution.py:75
  592.3 96.9 %copy-start.7 = (f32[512,256]{1,0:T(8,128)S(1)}, f32[512,256]{1,0:T(8,128)}, u32[]{:S(2)}) copy-start(f32[512,256]{1,0:T(8,128)} %param.6) | copy-start | bytes 1572868
  592.3 95.2 %all-reduce.2.cloned.1.call-start = ((), (), s32[]{:S(2)}) async-start(), calls=%async_computation.18 | async-start | bytes 524288 | tf_op jit(solution)/shard_map/psum | solution.py:122
  689.2 2.2 copy-start.11
Sparse Core Ops, SparseCore 0:
  596.3 91.1 all-reduce.1
where the time goes:
time: 710 us; the launch traced here: 699 us
  waiting for transfers between devices  345 us (49%)
  matrix products  177 us (25%)
  starting transfers between devices  112 us (16%)
  local copies, waits for them, and re-layouts  43.1 us (6%)
  between operations  15.1 us (2%)
    dot_general x36, matrix products, product_hi(): return jnp.einsum(form, left, right, precision=lax.Precision.HIGHEST)  177 us
    psum x1, waiting for transfers between devices, local(): grad_filter = lax.psum(corr, 'chan') * scale  94.4 us
    all_to_all x3, waiting for transfers between devices, forward_transform(): lax.all_to_all(turned_real, 'seq', split_axis=0, concat_axis=1, tiled=True)  62.5 us
    all_to_all x3, waiting for transfers between devices, inverse_transform(): lax.all_to_all(turned_real, 'seq', split_axis=1, concat_axis=0, tiled=True)  53.5 us
    all_to_all x3, waiting for transfers between devices, forward_transform(): lax.all_to_all(turned_imag, 'seq', split_axis=0, concat_axis=1, tiled=True)  42.3 us
    all_to_all x3, waiting for transfers between devices, inverse_transform(): lax.all_to_all(turned_imag, 'seq', split_axis=1, concat_axis=0, tiled=True)  41 us
    all_to_all x3, waiting for transfers between devices, forward_transform(): lax.all_to_all(block[None], 'seq', split_axis=1, concat_axis=0, tiled=True)  39.9 us
    all_to_all x3, starting transfers between devices, inverse_transform(): lax.all_to_all(turned_real, 'seq', split_axis=1, concat_axis=0, tiled=True)  22 us
  transfers between devices with their start and end apart: 19, of which 14 were waited for; matrix products, arithmetic and copies ran while one was open for 22% of the time, Pallas kernels for 0%

commit v1 on v0

v1 whole, which is shorter than its diff:
```python
import functools

import jax
import jax.numpy as jnp
import numpy as np
from jax import lax
from jax.experimental import pallas as pl
from jax.experimental.pallas import tpu as pltpu
from jax.sharding import PartitionSpec as P


SIDE = 128
HALVES = 2
GROUP = 4
QUARTERS = 4
BF = jnp.bfloat16
F32 = jnp.float32


def split_np(table):
    high = table.astype(np.float32).astype(BF)
    low = (table - high.astype(np.float64)).astype(np.float32).astype(BF)
    return high, low


def tables(shards, factor):
    total = SIDE * SIDE
    index = np.arange(SIDE)
    quarter, source = np.divmod(index, shards)
    first = source * QUARTERS + quarter
    coarse = 2.0 * np.pi * np.outer(index + 0.25, first) / SIDE
    high, low = split_np(np.concatenate([np.cos(coarse), -np.sin(coarse)], axis=0))
    into = np.concatenate([high, low, high], axis=1)
    high, low = split_np(np.concatenate([np.cos(coarse.T), -np.sin(coarse.T)], axis=1) * factor)
    back = np.concatenate([high, low, high], axis=1)
    fine = 2.0 * np.pi * (np.outer(index, index) % SIDE) / SIDE
    cos, sin = np.cos(fine), np.sin(fine)
    high, low = split_np(np.block([[cos, -sin], [sin, cos]]))
    ahead = np.concatenate([high, high, low], axis=0)
    high, low = split_np(np.block([[cos, sin], [-sin, cos]]))
    behind = np.concatenate([high, high, low], axis=0)
    turn = 2.0 * np.pi * np.outer(index + 0.25, index) / total
    twist = np.concatenate([np.cos(turn), np.sin(turn)], axis=1).astype(np.float32)
    return into, back, ahead, behind, twist


def halves(value):
    high = value.astype(BF)
    return high, (value - high.astype(F32)).astype(BF)


def dot(left, right):
    return jnp.dot(left, right, preferred_element_type=F32)


def ahead_pair(one, two, into, ahead, twist):
    high, low = halves(jnp.concatenate([one, two], axis=1))
    coarse = dot(into, jnp.concatenate([high, high, low], axis=0))
    cos, sin = twist[:, :SIDE], twist[:, SIDE:]
    rows = []
    for side in range(2):
        real = coarse[:SIDE, side * SIDE : (side + 1) * SIDE]
        imag = coarse[SIDE:, side * SIDE : (side + 1) * SIDE]
        rows.append(
            jnp.concatenate([real * cos + imag * sin, imag * cos - real * sin], axis=1)
        )
    high, low = halves(jnp.concatenate(rows, axis=0))
    return dot(jnp.concatenate([high, low, high], axis=1), ahead)


def behind_pair(spec, back, behind, twist):
    high, low = halves(spec)
    fine = dot(jnp.concatenate([high, low, high], axis=1), behind)
    cos, sin = twist[:, :SIDE], twist[:, SIDE:]
    reals, imags = [], []
    for side in range(2):
        real = fine[side * SIDE : (side + 1) * SIDE, :SIDE]
        imag = fine[side * SIDE : (side + 1) * SIDE, SIDE:]
        reals.append(real * cos - imag * sin)
        imags.append(imag * cos + real * sin)
    turned = jnp.concatenate(
        [jnp.concatenate(reals, axis=1), jnp.concatenate(imags, axis=1)], axis=0
    )
    high, low = halves(turned)
    return dot(back, jnp.concatenate([high, high, low], axis=0))


def product(left, right, conjugate):
    lr, li = left[:, :SIDE], left[:, SIDE:]
    rr, ri = right[:, :SIDE], right[:, SIDE:]
    if conjugate:
        return lr * rr + li * ri, lr * ri - li * rr
    return lr * rr - li * ri, lr * ri + li * rr


def gather_rows(ref, base, step, shards, pitch):
    return jnp.concatenate(
        [ref[pl.ds(base + q * step, shards, stride=pitch), :] for q in range(QUARTERS)], axis=0
    )


def pack_kernel(shards, pitch, k_ref, v_ref, g_ref, q_ref, f_ref, out_ref):
    for q in range(QUARTERS):
        rows = slice(q * SIDE, (q + 1) * SIDE)
        for h in range(HALVES):
            cols = slice(h * SIDE, (h + 1) * SIDE)
            gated = (k_ref[rows, cols] * v_ref[rows, cols]).T
            grad = (g_ref[rows, cols] * q_ref[rows, cols]).T
            for j in range(GROUP):
                own = slice(j * shards, (j + 1) * shards)
                at = q * 8 + h * GROUP + j
                out_ref[pl.ds(at, shards, stride=pitch), :] = gated[own]
                out_ref[pl.ds(32 + at, shards, stride=pitch), :] = grad[own]
        filt = f_ref[rows, :].T
        for j in range(GROUP):
            own = slice(j * shards, (j + 1) * shards)
            out_ref[pl.ds(64 + q * GROUP + j, shards, stride=pitch), :] = filt[own]


def conv_kernel(
    shards, pitch, in_ref, into_ref, back_ref, ahead_ref, behind_ref, twist_ref,
    out_ref, gated_ref, filt_ref,
):
    into, ahead, twist = into_ref[...], ahead_ref[...], twist_ref[...]
    back, behind = back_ref[...], behind_ref[...]
    for pair in range(GROUP // 2):
        slabs = [
            gather_rows(in_ref, 64 + 2 * pair + j, GROUP, shards, pitch) for j in range(2)
        ]
        filt_ref[pl.ds(pair * 2 * SIDE, 2 * SIDE), :] = ahead_pair(*slabs, into, ahead, twist)
    for j in range(GROUP):
        slabs = [gather_rows(in_ref, h * GROUP + j, 8, shards, pitch) for h in range(HALVES)]
        spec = ahead_pair(*slabs, into, ahead, twist)
        gated_ref[pl.ds(j * 2 * SIDE, 2 * SIDE), :] = spec
        filt = filt_ref[pl.ds(j * SIDE, SIDE), :]
        both = [
            jnp.concatenate(product(filt, spec[h * SIDE : (h + 1) * SIDE], False), axis=1)
            for h in range(HALVES)
        ]
        conv = behind_pair(jnp.concatenate(both, axis=0), back, behind, twist)
        for h in range(HALVES):
            for q in range(QUARTERS):
                out_ref[pl.ds(q * 8 + h * GROUP + j, shards, stride=32), :] = conv[
                    q * shards : (q + 1) * shards, h * SIDE : (h + 1) * SIDE
                ]


def corr_kernel(
    shards, pitch, in_ref, gated_ref, into_ref, back_ref, ahead_ref, behind_ref, twist_ref,
    out_ref, grad_ref,
):
    into, ahead, twist = into_ref[...], ahead_ref[...], twist_ref[...]
    back, behind = back_ref[...], behind_ref[...]
    for pair in range(GROUP // 2):
        sums = []
        for j in (2 * pair, 2 * pair + 1):
            slabs = [
                gather_rows(in_ref, 32 + h * GROUP + j, 8, shards, pitch) for h in range(HALVES)
            ]
            spec = ahead_pair(*slabs, into, ahead, twist)
            grad_ref[pl.ds(j * 2 * SIDE, 2 * SIDE), :] = spec
            gated = gated_ref[pl.ds(j * 2 * SIDE, 2 * SIDE), :]
            lower = product(gated[:SIDE], spec[:SIDE], True)
            upper = product(gated[SIDE:], spec[SIDE:], True)
            sums.append(
                jnp.concatenate([lower[0] + upper[0], lower[1] + upper[1]], axis=1)
            )
        corr = behind_pair(jnp.concatenate(sums, axis=0), back, behind, twist)
        for j in range(2):
            for q in range(QUARTERS):
                out_ref[pl.ds((q * 2 + pair) * 2 * shards + j, shards, stride=2), :] = corr[
                    q * shards : (q + 1) * shards, j * SIDE : (j + 1) * SIDE
                ]


def back_kernel(shards, grad_ref, filt_ref, back_ref, behind_ref, twist_ref, out_ref):
    twist, back, behind = twist_ref[...], back_ref[...], behind_ref[...]
    for j in range(GROUP):
        spec = grad_ref[pl.ds(j * 2 * SIDE, 2 * SIDE), :]
        filt = filt_ref[pl.ds(j * SIDE, SIDE), :]
        both = [
            jnp.concatenate(product(filt, spec[h * SIDE : (h + 1) * SIDE], True), axis=1)
            for h in range(HALVES)
        ]
        grad = behind_pair(jnp.concatenate(both, axis=0), back, behind, twist)
        for h in range(HALVES):
            for q in range(QUARTERS):
                out_ref[pl.ds(q * 8 + h * GROUP + j, shards, stride=32), :] = grad[
                    q * shards : (q + 1) * shards, h * SIDE : (h + 1) * SIDE
                ]


def unpack_kernel(shards, in_ref, *refs):
    count = len(refs) // 2
    for q in range(QUARTERS):
        rows = slice(q * SIDE, (q + 1) * SIDE)
        for h in range(HALVES):
            cols = slice(h * SIDE, (h + 1) * SIDE)
            slab = gather_rows(in_ref, q * 8 + h * GROUP, 1, shards, 32).T
            for weight_ref, out_ref in zip(refs[:count], refs[count:]):
                out_ref[rows, cols] = slab * weight_ref[rows, cols]


def filter_kernel(shards, in_ref, out_ref):
    for q in range(QUARTERS):
        slab = jnp.concatenate(
            [
                in_ref[pl.ds((q * 2 + j // 2) * 2 * shards + j % 2, shards, stride=2), :]
                for j in range(GROUP)
            ],
            axis=0,
        )
        out_ref[q * SIDE : (q + 1) * SIDE, :] = slab.T


def call(kernel, outs, args, name, flops=0):
    shapes = [jax.ShapeDtypeStruct(shape, F32) for shape in outs]
    moved = sum(4 * int(np.prod(shape)) for shape in outs) + sum(a.size * a.dtype.itemsize for a in args)
    return pl.pallas_call(
        kernel,
        out_shape=shapes,
        in_specs=[pl.BlockSpec(memory_space=pltpu.VMEM)] * len(args),
        out_specs=[pl.BlockSpec(memory_space=pltpu.VMEM)] * len(outs),
        name=name,
        compiler_params=pltpu.CompilerParams(vmem_limit_bytes=40 * 1024 * 1024),
        cost_estimate=pl.CostEstimate(flops=flops, bytes_accessed=moved, transcendentals=0),
    )(*args)


def exchange(block, axis, members):
    rows = block.shape[0] // members
    parted = block.reshape(members, rows, block.shape[1])
    return lax.all_to_all(parted, axis, 0, 0, tiled=True).reshape(block.shape)


def local(q_gate, k_gate, values, filter_raw, grad_out):
    shards = lax.axis_size("seq")
    members = lax.axis_size("chan")
    total = SIDE * SIDE
    into, back, ahead, behind, twist = (
        jnp.asarray(t) for t in tables(shards, total ** (-0.5) / total)
    )
    pitch = 80
    rows = 32 * shards
    packed = call(
        functools.partial(pack_kernel, shards, pitch),
        [(pitch * shards, SIDE)],
        (k_gate, values, grad_out, q_gate, filter_raw),
        "pack",
    )[0]
    spread = exchange(packed, "seq", shards)
    heavy = 6 * 10**9
    conv_out, gated_spec, filt_spec = call(
        functools.partial(conv_kernel, shards, pitch),
        [(rows, SIDE), (8 * SIDE, 2 * SIDE), (GROUP * SIDE, 2 * SIDE)],
        (spread, into, back, ahead, behind, twist),
        "conv",
        heavy,
    )
    conv = exchange(conv_out, "seq", shards)
    corr_out, grad_spec = call(
        functools.partial(corr_kernel, shards, pitch),
        [(8 * 2 * shards, SIDE), (8 * SIDE, 2 * SIDE)],
        (spread, gated_spec, into, back, ahead, behind, twist),
        "corr",
        heavy,
    )
    back_out = call(
        functools.partial(back_kernel, shards),
        [(rows, SIDE)],
        (grad_spec, filt_spec, back, behind, twist),
        "back",
        heavy,
    )[0]
    chunk = 2 * shards
    me = lax.axis_index("chan")
    parts = corr_out.reshape(members, chunk, SIDE)
    ring = [[(i, (i + d) % members) for i in range(members)] for d in range(members)]
    pieces = [lax.dynamic_index_in_dim(parts, me, 0, keepdims=False)]
    for d in range(1, members):
        piece = lax.dynamic_index_in_dim(parts, (me + d) % members, 0, keepdims=False)
        pieces.append(lax.ppermute(piece, "chan", ring[d]))
    summed = functools.reduce(jnp.add, pieces)
    summed, conv = lax.optimization_barrier((summed, conv))
    placed = exchange(summed, "seq", shards)
    placed, back_out = lax.optimization_barrier((placed, back_out))
    grad_gated = exchange(back_out, "seq", shards)
    wide = lax.all_to_all(
        jnp.broadcast_to(placed, (members, chunk, SIDE)), "chan", 0, 0, tiled=True
    ).reshape(members * chunk, SIDE)
    block = q_gate.shape
    grad_q = call(functools.partial(unpack_kernel, shards), [block], (conv, grad_out), "unpack_q")[0]
    grad_k, grad_v = call(
        functools.partial(unpack_kernel, shards),
        [block, block],
        (grad_gated, values, k_gate),
        "unpack_kv",
    )
    grad_filter = call(
        functools.partial(filter_kernel, shards), [filter_raw.shape], (wide,), "unpack_f"
    )[0]
    return grad_q, grad_k, grad_v, grad_filter


def solution(mesh):
    placed = (
        P("seq", "chan"),
        P("seq", "chan"),
        P("seq", "chan"),
        P("seq", None),
        P("seq", "chan"),
    )
    return jax.shard_map(
        local,
        mesh=mesh,
        in_specs=placed,
        out_specs=(P("seq", "chan"), P("seq", "chan"), P("seq", "chan"), P("seq", None)),
        check_vma=False,
    )
```

time: 710 us -> 142 us (0.20)
  the two profiles are of different devices: /device:TPU:32 before, /device:TPU:1 now
where the time goes in v1:
time: 142 us; the launch traced here: 141 us
  blocking collectives  56.1 us (40%)
  starting transfers between devices  34.2 us (24%)
  waiting for transfers between devices  24.2 us (17%)
  Pallas kernels  13.6 us (10%)
  local copies, waits for them, and re-layouts  11.4 us (8%)
    all_to_all x1, blocking collectives, exchange(): return lax.all_to_all(parted, axis, 0, 0, tiled=True).reshape(block.shape)  45 us
    all_to_all x3, starting transfers between devices, exchange(): return lax.all_to_all(parted, axis, 0, 0, tiled=True).reshape(block.shape)  21.8 us
    all_to_all x3, waiting for transfers between devices, exchange(): return lax.all_to_all(parted, axis, 0, 0, tiled=True).reshape(block.shape)  17.5 us
    pallas_call x7, Pallas kernels, call(): pl.pallas_call(kernel, out_shape=shapes, in_specs=[pl.BlockSpec(memory_sp...  13.6 us
    ppermute x7, starting transfers between devices, local(): pieces.append(lax.ppermute(piece, 'chan', ring[d]))  12.3 us
    unnamed x38, local copies, waits for them, and re-layouts  11.4 us
    all_to_all x1, blocking collectives, local(): lax.all_to_all(jnp.broadcast_to(placed, (members, chunk, SIDE)), 'chan',...  11.1 us
    ppermute x7, waiting for transfers between devices, local(): pieces.append(lax.ppermute(piece, 'chan', ring[d]))  6.71 us
  transfers between devices with their start and end apart: 10, of which 5 were waited for; matrix products, arithmetic and copies ran while one was open for 0% of the time, Pallas kernels for 5%

profile of v1, /device:TPU:1, one launch (start us, length us, event | category | flops | bytes accessed | tf_op | source)
XLA Modules:
  0.0 141.0 jit_solution(9466834018766050704)
XLA Ops:
  0.6 0.0 copy-start
  0.6 1.0 copy-done
  1.7 1.0 copy-done.2
  2.7 1.0 copy-done.4
  3.8 1.0 copy-done.6
  4.8 0.9 copy-done.7
  5.8 0.6 pack.1
  6.4 0.0 copy-start.8
  6.4 0.0 copy-start.9
  6.4 0.0 copy-start.10
  6.4 0.0 copy-start.11
  6.4 0.0 copy-start.12
  6.4 45.0 %all_to_all.25 = f32[32,80,128]{2,1,0:T(8,128)S(1)} all-to-all(f32[32,80,128]{2,1,0:T(8,128)S(1)} %bitcast.38), channel_id=1, replica_groups=mesh['seq'=32,'chan'=8] {'seq'}, dimensions={0} | all-to-all | bytes 2621440 | tf_op jit(solution)/shard_map/all_to_all | solution.py:233
  51.4 4.4 %conv.1 = (f32[1024,128]{1,0:T(8,128)}, f32[1024,256]{1,0:T(8,128)S(1)}, f32[512,256]{1,0:T(8,128)S(1)}) custom-call(f32[2560,128]{1,0:T(8,128)S(1)} %bitcast.41, bf16[256,384]{1,0:T(8,128)(2,1)S(1)} %copy-done.11, bf16[128,768]{1,0:T(8,128)(2,1)S(1)} %copy-done.10, bf16[768,256]{1,0:T(8,128)(2,1)S(1)} %copy-done.9, bf16[768,256]{1,0:T(8,128)(2,1)S(1)} %copy-done.8, ...), custom_call_target="tpu_custom_call" | custom-call | flops 6000000000 | bytes 4718592 | tf_op jit(solution)/shard_map/conv/pallas_call | solution.py:219
  55.9 1.0 copy-done.13
  56.8 0.8 copy-done.17
  57.6 4.4 %all-to-all-start.1 = ((f32[32,32,128]{2,1,0:T(8,128)}), f32[32,32,128]{2,1,0:T(8,128)S(1)}, u32[]{:S(2)}, u32[]{:S(2)}) async-start(f32[32,32,128]{2,1,0:T(8,128)} %bitcast.11), calls=%async_computation.1 | async-start | bytes 1048576 | tf_op jit(solution)/shard_map/all_to_all | solution.py:233
  62.1 1.2 copy-done.14
  63.4 2.3 %corr.1 = (f32[512,128]{1,0:T(8,128)S(1)}, f32[1024,256]{1,0:T(8,128)S(1)}) custom-call(f32[2560,128]{1,0:T(8,128)S(1)} %bitcast.42, f32[1024,256]{1,0:T(8,128)S(1)} %copy-done.14, bf16[256,384]{1,0:T(8,128)(2,1)S(1)} %copy-done.11, bf16[128,768]{1,0:T(8,128)(2,1)S(1)} %copy-done.10, bf16[768,256]{1,0:T(8,128)(2,1)S(1)} %copy-done.9, ...), custom_call_target="tpu_custom_call" | custom-call | flops 6000000000 | bytes 4980736 | tf_op jit(solution)/shard_map/corr/pallas_call | solution.py:219
  65.7 1.0 copy-done.15
  66.7 5.0 %collective-permute-start.6 = (f32[64,128]{1,0:T(8,128)S(1)}, f32[64,128]{1,0:T(8,128)S(1)}, u32[]{:S(2)}, u32[]{:S(2)}) collective-permute-start(f32[64,128]{1,0:T(8,128)S(1)} %get-tuple-element.27), channel_id=1, source_target_pairs={{0,7},{1,0},{2,1},{3,2},{4,3},{5,4},{6,5},{7,6},{8,15},{9,8},{10,9... | collective-permute-start | bytes 98312 | tf_op jit(solution)/shard_map/ppermute | solution.py:282
  71.7 0.3 collective-permute-start.5
  72.0 0.9 collective-permute-start.4
  73.0 2.5 %collective-permute-start.3 = (f32[64,128]{1,0:T(8,128)S(1)}, f32[64,128]{1,0:T(8,128)S(1)}, u32[]{:S(2)}, u32[]{:S(2)}) collective-permute-start(f32[64,128]{1,0:T(8,128)S(1)} %get-tuple-element.30), channel_id=1, source_target_pairs={{0,4},{1,5},{2,6},{3,7},{4,0},{5,1},{6,2},{7,3},{8,12},{9,13},{10,... | collective-permute-start | bytes 98312 | tf_op jit(solution)/shard_map/ppermute | solution.py:282
  75.4 0.0 collective-permute-start.2
  75.4 0.0 collective-permute-done.6
  75.4 3.6 %collective-permute-start.1 = (f32[64,128]{1,0:T(8,128)S(1)}, f32[64,128]{1,0:T(8,128)S(1)}, u32[]{:S(2)}, u32[]{:S(2)}) collective-permute-start(f32[64,128]{1,0:T(8,128)S(1)} %get-tuple-element.32), channel_id=1, source_target_pairs={{0,2},{1,3},{2,4},{3,5},{4,6},{5,7},{6,0},{7,1},{8,10},{9,11},{10,... | collective-permute-start | bytes 98312 | tf_op jit(solution)/shard_map/ppermute | solution.py:282
  79.1 0.0 collective-permute-done.5
  79.1 0.0 collective-permute-start
  79.1 0.0 collective-permute-done.4
  79.1 0.0 collective-permute-done.3
  79.1 1.6 %collective-permute-done.2 = f32[64,128]{1,0:T(8,128)S(1)} collective-permute-done((f32[64,128]{1,0:T(8,128)S(1)}, f32[64,128]{1,0:T(8,128)S(1)}, u32[]{:S(2)}, u32[]{:S(2)}) %collective-permute-start.2) | collective-permute-done | bytes 32800 | tf_op jit(solution)/shard_map/ppermute | solution.py:282
  80.7 2.3 %collective-permute-done.1 = f32[64,128]{1,0:T(8,128)S(1)} collective-permute-done((f32[64,128]{1,0:T(8,128)S(1)}, f32[64,128]{1,0:T(8,128)S(1)}, u32[]{:S(2)}, u32[]{:S(2)}) %collective-permute-start.1) | collective-permute-done | bytes 32800 | tf_op jit(solution)/shard_map/ppermute | solution.py:282
  83.0 2.8 %collective-permute-done = f32[64,128]{1,0:T(8,128)S(1)} collective-permute-done((f32[64,128]{1,0:T(8,128)S(1)}, f32[64,128]{1,0:T(8,128)S(1)}, u32[]{:S(2)}, u32[]{:S(2)}) %collective-permute-start) | collective-permute-done | bytes 32800 | tf_op jit(solution)/shard_map/ppermute | solution.py:282
  85.8 0.6 fusion.5
  86.4 10.9 %all-to-all-start.2 = ((f32[32,2,128]{2,1,0:T(2,128)}), f32[32,2,128]{2,1,0:T(2,128)S(1)}, u32[]{:S(2)}, u32[]{:S(2)}) async-start(f32[32,2,128]{2,1,0:T(2,128)} %bitcast.13), calls=%async_computation.2 | async-start | bytes 65536 | tf_op jit(solution)/shard_map/all_to_all | solution.py:233
  97.3 1.2 copy-done.16
  98.5 1.0 copy-done.18
  99.6 2.9 %back.1 = f32[1024,128]{1,0:T(8,128)} custom-call(f32[1024,256]{1,0:T(8,128)S(1)} %copy-done.16, f32[512,256]{1,0:T(8,128)S(1)} %copy-done.18, bf16[128,768]{1,0:T(8,128)(2,1)S(1)} %copy-done.10, bf16[768,256]{1,0:T(8,128)(2,1)S(1)} %copy-done.8, f32[128,256]{1,0:T(8,128)S(1)} %copy-done.12), custom_call_target="tpu_custom_call" | custom-call | flops 6000000000 | bytes 2818048 | tf_op jit(solution)/shard_map/back/pallas_call | solution.py:219
  102.5 2.9 %all-to-all-done.2 = f32[32,2,128]{2,1,0:T(2,128)S(1)} async-done(((f32[32,2,128]{2,1,0:T(2,128)}), f32[32,2,128]{2,1,0:T(2,128)S(1)}, u32[]{:S(2)}, u32[]{:S(2)}) %all-to-all-start.2) | async-done | bytes 32800 | tf_op jit(solution)/shard_map/all_to_all | solution.py:233
  105.4 11.1 %all_to_all.26 = f32[8,64,128]{2,1,0:T(8,128)S(1)} all-to-all(f32[8,64,128]{2,1,0:T(8,128)S(1)} %broadcast_in_dim.3), channel_id=1, replica_groups=mesh['seq'=32,'chan'=8] {'chan'}, dimensions={0} | all-to-all | bytes 524288 | tf_op jit(solution)/shard_map/all_to_all | solution.py:288
  116.5 6.6 %all-to-all-start.3 = ((f32[32,32,128]{2,1,0:T(8,128)}), f32[32,32,128]{2,1,0:T(8,128)S(1)}, u32[]{:S(2)}, u32[]{:S(2)}) async-start(f32[32,32,128]{2,1,0:T(8,128)} %bitcast.15), calls=%async_computation.3 | async-start | bytes 1048576 | tf_op jit(solution)/shard_map/all_to_all | solution.py:233
  123.1 0.0 copy-start.3
  123.1 0.0 copy-start.5
  123.2 1.2 unpack_q.1
  124.3 0.8 unpack_f.1
  125.1 14.5 %all-to-all-done.3 = f32[32,32,128]{2,1,0:T(8,128)S(1)} async-done(((f32[32,32,128]{2,1,0:T(8,128)}), f32[32,32,128]{2,1,0:T(8,128)S(1)}, u32[]{:S(2)}, u32[]{:S(2)}) %all-to-all-start.3) | async-done | bytes 524320 | tf_op jit(solution)/shard_map/all_to_all | solution.py:233
  139.7 1.3 unpack_kv.1
  (22 shorter events, 0.1 us)
Async XLA Ops:
  0.6 1.0 copy-start
  1.7 1.0 copy-start.2
  2.7 1.0 copy-start.4
  3.8 1.0 copy-start.6
  4.8 0.9 copy-start.7
  6.4 45.0 %copy-start.8 = (bf16[768,256]{1,0:T(8,128)(2,1)S(1)}, bf16[768,256]{1,0:T(8,128)(2,1)}, u32[]{:S(2)}) copy-start(bf16[768,256]{1,0:T(8,128)(2,1)} %constant.85.clone.behind_ref) | copy-start | bytes 1179652
  6.4 45.0 %copy-start.9 = (bf16[768,256]{1,0:T(8,128)(2,1)S(1)}, bf16[768,256]{1,0:T(8,128)(2,1)}, u32[]{:S(2)}) copy-start(bf16[768,256]{1,0:T(8,128)(2,1)} %constant.84.clone.ahead_ref) | copy-start | bytes 1179652
  6.4 45.0 %copy-start.10 = (bf16[128,768]{1,0:T(8,128)(2,1)S(1)}, bf16[128,768]{1,0:T(8,128)(2,1)}, u32[]{:S(2)}) copy-start(bf16[128,768]{1,0:T(8,128)(2,1)} %constant.83.clone.back_ref) | copy-start | bytes 589828
  6.4 45.0 %copy-start.11 = (bf16[256,384]{1,0:T(8,128)(2,1)S(1)}, bf16[256,384]{1,0:T(8,128)(2,1)}, u32[]{:S(2)}) copy-start(bf16[256,384]{1,0:T(8,128)(2,1)} %constant.82.clone.into_ref) | copy-start | bytes 589828
  6.4 45.0 %copy-start.12 = (f32[128,256]{1,0:T(8,128)S(1)}, f32[128,256]{1,0:T(8,128)}, u32[]{:S(2)}) copy-start(f32[128,256]{1,0:T(8,128)} %constant.86.clone.twist_ref) | copy-start | bytes 393220
  55.9 1.0 copy-start.13
  56.8 0.8 copy-start.17
  57.6 28.8 %all-to-all-start.1 = ((f32[32,32,128]{2,1,0:T(8,128)}), f32[32,32,128]{2,1,0:T(8,128)S(1)}, u32[]{:S(2)}, u32[]{:S(2)}) async-start(f32[32,32,128]{2,1,0:T(8,128)} %bitcast.11), calls=%async_computation.1 | async-start | bytes 1048576 | tf_op jit(solution)/shard_map/all_to_all | solution.py:233
  62.1 1.2 copy-start.14
  65.7 1.0 copy-start.15
  66.7 8.7 %collective-permute-start.6 = (f32[64,128]{1,0:T(8,128)S(1)}, f32[64,128]{1,0:T(8,128)S(1)}, u32[]{:S(2)}, u32[]{:S(2)}) collective-permute-start(f32[64,128]{1,0:T(8,128)S(1)} %get-tuple-element.27), channel_id=1, source_target_pairs={{0,7},{1,0},{2,1},{3,2},{4,3},{5,4},{6,5},{7,6},{8,15},{9,8},{10,9... | collective-permute-start | bytes 98312 | tf_op jit(solution)/shard_map/ppermute | solution.py:282
  71.7 7.4 %collective-permute-start.5 = (f32[64,128]{1,0:T(8,128)S(1)}, f32[64,128]{1,0:T(8,128)S(1)}, u32[]{:S(2)}, u32[]{:S(2)}) collective-permute-start(f32[64,128]{1,0:T(8,128)S(1)} %get-tuple-element.28), channel_id=1, source_target_pairs={{0,6},{1,7},{2,0},{3,1},{4,2},{5,3},{6,4},{7,5},{8,14},{9,15},{10,... | collective-permute-start | bytes 98312 | tf_op jit(solution)/shard_map/ppermute | solution.py:282
  72.0 7.0 %collective-permute-start.4 = (f32[64,128]{1,0:T(8,128)S(1)}, f32[64,128]{1,0:T(8,128)S(1)}, u32[]{:S(2)}, u32[]{:S(2)}) collective-permute-start(f32[64,128]{1,0:T(8,128)S(1)} %get-tuple-element.29), channel_id=1, source_target_pairs={{0,5},{1,6},{2,7},{3,0},{4,1},{5,2},{6,3},{7,4},{8,13},{9,14},{10,... | collective-permute-start | bytes 98312 | tf_op jit(solution)/shard_map/ppermute | solution.py:282
  73.0 6.1 %collective-permute-start.3 = (f32[64,128]{1,0:T(8,128)S(1)}, f32[64,128]{1,0:T(8,128)S(1)}, u32[]{:S(2)}, u32[]{:S(2)}) collective-permute-start(f32[64,128]{1,0:T(8,128)S(1)} %get-tuple-element.30), channel_id=1, source_target_pairs={{0,4},{1,5},{2,6},{3,7},{4,0},{5,1},{6,2},{7,3},{8,12},{9,13},{10,... | collective-permute-start | bytes 98312 | tf_op jit(solution)/shard_map/ppermute | solution.py:282
  75.4 5.3 %collective-permute-start.2 = (f32[64,128]{1,0:T(8,128)S(1)}, f32[64,128]{1,0:T(8,128)S(1)}, u32[]{:S(2)}, u32[]{:S(2)}) collective-permute-start(f32[64,128]{1,0:T(8,128)S(1)} %get-tuple-element.31), channel_id=1, source_target_pairs={{0,3},{1,4},{2,5},{3,6},{4,7},{5,0},{6,1},{7,2},{8,11},{9,12},{10,... | collective-permute-start | bytes 98312 | tf_op jit(solution)/shard_map/ppermute | solution.py:282
  75.4 7.5 %collective-permute-start.1 = (f32[64,128]{1,0:T(8,128)S(1)}, f32[64,128]{1,0:T(8,128)S(1)}, u32[]{:S(2)}, u32[]{:S(2)}) collective-permute-start(f32[64,128]{1,0:T(8,128)S(1)} %get-tuple-element.32), channel_id=1, source_target_pairs={{0,2},{1,3},{2,4},{3,5},{4,6},{5,7},{6,0},{7,1},{8,10},{9,11},{10,... | collective-permute-start | bytes 98312 | tf_op jit(solution)/shard_map/ppermute | solution.py:282
  79.1 6.7 %collective-permute-start = (f32[64,128]{1,0:T(8,128)S(1)}, f32[64,128]{1,0:T(8,128)S(1)}, u32[]{:S(2)}, u32[]{:S(2)}) collective-permute-start(f32[64,128]{1,0:T(8,128)S(1)} %get-tuple-element.26), channel_id=1, source_target_pairs={{0,1},{1,2},{2,3},{3,4},{4,5},{5,6},{6,7},{7,0},{8,9},{9,10},{10,1... | collective-permute-start | bytes 98312 | tf_op jit(solution)/shard_map/ppermute | solution.py:282
  86.4 19.0 %all-to-all-start.2 = ((f32[32,2,128]{2,1,0:T(2,128)}), f32[32,2,128]{2,1,0:T(2,128)S(1)}, u32[]{:S(2)}, u32[]{:S(2)}) async-start(f32[32,2,128]{2,1,0:T(2,128)} %bitcast.13), calls=%async_computation.2 | async-start | bytes 65536 | tf_op jit(solution)/shard_map/all_to_all | solution.py:233
  97.3 1.2 copy-start.16
  98.5 1.0 copy-start.18
  102.5 20.6 %copy-start.1 = (f32[512,256]{1,0:T(8,128)S(1)}, f32[512,256]{1,0:T(8,128)}, u32[]{:S(2)}) copy-start(f32[512,256]{1,0:T(8,128)} %refs_0_.2) | copy-start | bytes 1572868
  116.5 23.1 %all-to-all-start.3 = ((f32[32,32,128]{2,1,0:T(8,128)}), f32[32,32,128]{2,1,0:T(8,128)S(1)}, u32[]{:S(2)}, u32[]{:S(2)}) async-start(f32[32,32,128]{2,1,0:T(8,128)} %bitcast.15), calls=%async_computation.3 | async-start | bytes 1048576 | tf_op jit(solution)/shard_map/all_to_all | solution.py:233
  123.1 16.6 %copy-start.3 = (f32[512,256]{1,0:T(8,128)S(1)}, f32[512,256]{1,0:T(8,128)}, u32[]{:S(2)}) copy-start(f32[512,256]{1,0:T(8,128)} %refs_1_.1) | copy-start | bytes 1572868
  123.1 16.5 %copy-start.5 = (f32[512,256]{1,0:T(8,128)S(1)}, f32[512,256]{1,0:T(8,128)}, u32[]{:S(2)}) copy-start(f32[512,256]{1,0:T(8,128)} %refs_0_.3) | copy-start | bytes 1572868

commit v2 on v1

v2 whole, which is shorter than its diff:
```python
import functools

import jax
import jax.numpy as jnp
import numpy as np
from jax import lax
from jax.experimental import pallas as pl
from jax.experimental.pallas import tpu as pltpu
from jax.sharding import Mesh
from jax.sharding import PartitionSpec as P


SIDE = 128
HALVES = 2
BLOCKS = 4
QUARTERS = 4
IN_ROWS = 17
OUT_ROWS = 20
BF = jnp.bfloat16
F32 = jnp.float32


def split_np(table):
    high = table.astype(np.float32).astype(BF)
    low = (table - high.astype(np.float64)).astype(np.float32).astype(BF)
    return high, low


def tables(shards, factor):
    total = SIDE * SIDE
    index = np.arange(SIDE)
    quarter, source = np.divmod(index, shards)
    first = source * QUARTERS + quarter
    coarse = 2.0 * np.pi * np.outer(index + 0.25, first) / SIDE
    high, low = split_np(np.concatenate([np.cos(coarse), -np.sin(coarse)], axis=0))
    into = np.concatenate([high, low, high], axis=1)
    high, low = split_np(np.concatenate([np.cos(coarse.T), -np.sin(coarse.T)], axis=1) * factor)
    back = np.concatenate([high, low, high], axis=1)
    fine = 2.0 * np.pi * (np.outer(index, index) % SIDE) / SIDE
    cos, sin = np.cos(fine), np.sin(fine)
    high, low = split_np(np.block([[cos, -sin], [sin, cos]]))
    ahead = np.concatenate([high, high, low], axis=0)
    high, low = split_np(np.block([[cos, sin], [-sin, cos]]))
    behind = np.concatenate([high, high, low], axis=0)
    turn = 2.0 * np.pi * np.outer(index + 0.25, index) / total
    twist = np.concatenate([np.cos(turn), np.sin(turn)], axis=1).astype(np.float32)
    return into, back, ahead, behind, twist


def halves(value):
    high = value.astype(BF)
    return high, (value - high.astype(F32)).astype(BF)


def dot(left, right):
    return jnp.dot(left, right, preferred_element_type=F32)


def transform(slabs, into, ahead, twist):
    high, low = halves(jnp.concatenate(slabs, axis=1))
    coarse = dot(into, jnp.concatenate([high, high, low], axis=0))
    cos, sin = twist[:, :SIDE], twist[:, SIDE:]
    rows = []
    for at in range(len(slabs)):
        real = coarse[:SIDE, at * SIDE : (at + 1) * SIDE]
        imag = coarse[SIDE:, at * SIDE : (at + 1) * SIDE]
        rows.append(
            jnp.concatenate([real * cos + imag * sin, imag * cos - real * sin], axis=1)
        )
    high, low = halves(jnp.concatenate(rows, axis=0))
    return dot(jnp.concatenate([high, low, high], axis=1), ahead)


def inverse(specs, back, behind, twist):
    high, low = halves(jnp.concatenate(specs, axis=0))
    fine = dot(jnp.concatenate([high, low, high], axis=1), behind)
    cos, sin = twist[:, :SIDE], twist[:, SIDE:]
    reals, imags = [], []
    for at in range(len(specs)):
        real = fine[at * SIDE : (at + 1) * SIDE, :SIDE]
        imag = fine[at * SIDE : (at + 1) * SIDE, SIDE:]
        reals.append(real * cos - imag * sin)
        imags.append(imag * cos + real * sin)
    turned = jnp.concatenate(
        [jnp.concatenate(reals, axis=1), jnp.concatenate(imags, axis=1)], axis=0
    )
    high, low = halves(turned)
    return dot(back, jnp.concatenate([high, high, low], axis=0))


def product(left, right):
    lr, li = left[:, :SIDE], left[:, SIDE:]
    rr, ri = right[:, :SIDE], right[:, SIDE:]
    return jnp.concatenate([lr * rr - li * ri, lr * ri + li * rr], axis=1)


def turned_product(left, right):
    lr, li = left[:, :SIDE], left[:, SIDE:]
    rr, ri = right[:, :SIDE], right[:, SIDE:]
    return jnp.concatenate([lr * rr + li * ri, lr * ri - li * rr], axis=1)


def gather_rows(ref, base, step, shards, pitch):
    return jnp.concatenate(
        [ref[pl.ds(base + q * step, shards, stride=pitch), :] for q in range(QUARTERS)], axis=0
    )


def pack_kernel(
    members, near_ref, k_hbm, v_hbm, g_hbm, q_hbm, f_hbm, out_ref,
    k_ref, v_ref, g_ref, q_ref, f_ref, sems,
):
    copies = []
    for q in range(QUARTERS):
        rows = pl.ds(q * SIDE, SIDE)
        pairs = ((k_hbm, k_ref), (v_hbm, v_ref), (g_hbm, g_ref), (q_hbm, q_ref))
        for at, (source, target) in enumerate(pairs):
            copy = pltpu.make_async_copy(source.at[rows], target.at[rows], sems.at[q * 4 + at])
            copy.start()
            copies.append(copy)
    start = pl.multiple_of(near_ref[0] * SIDE, SIDE)
    last = pltpu.make_async_copy(f_hbm.at[pl.ds(start, SIDE)], f_ref, sems.at[16])
    last.start()
    for q in range(QUARTERS):
        for at in range(4):
            copies[q * 4 + at].wait()
        rows = slice(q * SIDE, (q + 1) * SIDE)
        for h in range(HALVES):
            cols = slice(h * SIDE, (h + 1) * SIDE)
            at = h * QUARTERS + q
            out_ref[pl.ds(at, members, stride=IN_ROWS), :] = (
                k_ref[rows, cols] * v_ref[rows, cols]
            ).T
            out_ref[pl.ds(8 + at, members, stride=IN_ROWS), :] = (
                g_ref[rows, cols] * q_ref[rows, cols]
            ).T
    last.wait()
    out_ref[pl.ds(16, members, stride=IN_ROWS), :] = f_ref[...].T


def ahead_kernel(
    shards, in_ref, into_ref, back_ref, ahead_ref, behind_ref, twist_ref,
    corr_ref, gated_ref, grad_ref,
):
    into, ahead, twist = into_ref[...], ahead_ref[...], twist_ref[...]
    pitch = BLOCKS * IN_ROWS
    total = None
    for block in range(BLOCKS):
        specs = []
        for array, out_ref in enumerate((gated_ref, grad_ref)):
            slabs = [
                gather_rows(
                    in_ref, block * IN_ROWS + array * 8 + h * QUARTERS, 1, shards, pitch
                )
                for h in range(HALVES)
            ]
            spec = transform(slabs, into, ahead, twist)
            out_ref[pl.ds(block * 2 * SIDE, 2 * SIDE), :] = spec
            specs.append(spec)
        term = turned_product(*specs)
        term = term[:SIDE] + term[SIDE:]
        total = term if total is None else total + term
    corr_ref[...] = inverse([total], back_ref[...], behind_ref[...], twist)


def behind_kernel(
    shards, in_ref, gated_ref, grad_ref, into_ref, back_ref, ahead_ref, behind_ref, twist_ref,
    out_ref,
):
    twist, back, behind = twist_ref[...], back_ref[...], behind_ref[...]
    pitch = BLOCKS * OUT_ROWS
    slab = gather_rows(in_ref, 16, IN_ROWS, shards, BLOCKS * IN_ROWS)
    filt = transform([slab], into_ref[...], ahead_ref[...], twist)
    for block in range(BLOCKS):
        for array, spec_ref in enumerate((gated_ref, grad_ref)):
            combine = turned_product if array else product
            specs = [
                combine(filt, spec_ref[pl.ds((block * 2 + h) * SIDE, SIDE), :])
                for h in range(HALVES)
            ]
            result = inverse(specs, back, behind, twist)
            for h in range(HALVES):
                for q in range(QUARTERS):
                    at = block * OUT_ROWS + array * 8 + h * QUARTERS + q
                    out_ref[pl.ds(at, shards, stride=pitch), :] = result[
                        q * shards : (q + 1) * shards, h * SIDE : (h + 1) * SIDE
                    ]


def sum_kernel(shards, own_ref, other_ref, _, out_ref):
    total = own_ref[...] + other_ref[...]
    for block in range(BLOCKS):
        for q in range(QUARTERS):
            at = block * OUT_ROWS + 16 + q
            out_ref[pl.ds(at, shards, stride=BLOCKS * OUT_ROWS), :] = total[
                q * shards : (q + 1) * shards
            ]


def unpack_kernel(
    members, in_ref, g_ref, v_ref, k_ref, gq_hbm, gk_hbm, gv_hbm, gf_hbm,
    gq_ref, gk_ref, gv_ref, gf_ref, sems,
):
    copies = []
    for q in range(QUARTERS):
        rows = slice(q * SIDE, (q + 1) * SIDE)
        for h in range(HALVES):
            cols = slice(h * SIDE, (h + 1) * SIDE)
            at = h * QUARTERS + q
            conv = in_ref[pl.ds(at, members, stride=OUT_ROWS), :].T
            gq_ref[rows, cols] = conv * g_ref[rows, cols]
            back = in_ref[pl.ds(8 + at, members, stride=OUT_ROWS), :].T
            gk_ref[rows, cols] = back * v_ref[rows, cols]
            gv_ref[rows, cols] = back * k_ref[rows, cols]
        gf_ref[rows, :] = in_ref[pl.ds(16 + q, members, stride=OUT_ROWS), :].T
        pairs = ((gq_ref, gq_hbm), (gk_ref, gk_hbm), (gv_ref, gv_hbm), (gf_ref, gf_hbm))
        for at, (source, target) in enumerate(pairs):
            part = pl.ds(q * SIDE, SIDE)
            copy = pltpu.make_async_copy(source.at[part], target.at[part], sems.at[q * 4 + at])
            copy.start()
            copies.append(copy)
    for copy in copies:
        copy.wait()


VMEM = pl.BlockSpec(memory_space=pltpu.VMEM)
HBM = pl.BlockSpec(memory_space=pltpu.HBM)
SMEM = pl.BlockSpec(memory_space=pltpu.SMEM)
LIMIT = 24 * 1024 * 1024


def call(kernel, outs, args, name, ins=None, out_spec=VMEM, scratch=(), flops=0, aliases=None):
    moved = sum(4 * int(np.prod(shape)) for shape in outs)
    moved += sum(a.size * a.dtype.itemsize for a in args)
    return pl.pallas_call(
        kernel,
        out_shape=[jax.ShapeDtypeStruct(shape, F32) for shape in outs],
        in_specs=ins or [VMEM] * len(args),
        out_specs=[out_spec] * len(outs),
        scratch_shapes=list(scratch),
        input_output_aliases=aliases or {},
        name=name,
        compiler_params=pltpu.CompilerParams(vmem_limit_bytes=LIMIT),
        cost_estimate=pl.CostEstimate(flops=flops, bytes_accessed=moved, transcendentals=0),
    )(*args)


def exchange(block, inner):
    parted = block.reshape(block.shape[0] // int(np.prod(inner)), *inner, SIDE)
    return lax.all_to_all(parted, ("seq", "near"), 0, 0, tiled=True).reshape(block.shape)


def local(q_gate, k_gate, values, filter_raw, grad_out):
    shards = lax.axis_size("seq")
    members = shards * lax.axis_size("near")
    total = SIDE * SIDE
    into, back, ahead, behind, twist = (
        jnp.asarray(t) for t in tables(shards, total ** (-0.5) / total)
    )
    block = q_gate.shape
    wide = pltpu.VMEM(block, F32)
    near = lax.axis_index("near").astype(jnp.int32).reshape(1)
    packed = call(
        functools.partial(pack_kernel, members),
        [(IN_ROWS * members, SIDE)],
        (near, *(pltpu.with_memory_space_constraint(a, pltpu.HBM) for a in (k_gate, values, grad_out, q_gate, filter_raw))),
        "pack",
        ins=[SMEM] + [HBM] * 5,
        scratch=[wide] * 4 + [pltpu.VMEM((SIDE, SIDE), F32), pltpu.SemaphoreType.DMA((17,))],
    )[0]
    spread = exchange(packed, (17, 1))
    corr, gated_spec, grad_spec = call(
        functools.partial(ahead_kernel, shards),
        [(SIDE, SIDE), (8 * SIDE, 2 * SIDE), (8 * SIDE, 2 * SIDE)],
        (spread, into, back, ahead, behind, twist),
        "ahead",
        flops=10**9,
    )
    other = lax.ppermute(corr, "far", [(0, 1), (1, 0)])
    results = call(
        functools.partial(behind_kernel, shards),
        [(OUT_ROWS * members, SIDE)],
        (spread, gated_spec, grad_spec, into, back, ahead, behind, twist),
        "behind",
        flops=10**9,
    )[0]
    results = call(
        functools.partial(sum_kernel, shards),
        [(OUT_ROWS * members, SIDE)],
        (corr, other, results),
        "sum",
        ins=[VMEM] * 3,
        aliases={2: 0},
    )[0]
    placed = exchange(results, (5, 4))
    grad_q, grad_k, grad_v, grad_filter = call(
        functools.partial(unpack_kernel, members),
        [block, block, block, filter_raw.shape],
        (placed, grad_out, values, k_gate),
        "unpack",
        out_spec=HBM,
        scratch=[wide] * 3 + [pltpu.VMEM(filter_raw.shape, F32), pltpu.SemaphoreType.DMA((16,))],
    )
    return grad_q, grad_k, grad_v, grad_filter


def solution(mesh):
    shards, groups = mesh.devices.shape
    parted = Mesh(
        mesh.devices.reshape(shards, groups // BLOCKS, BLOCKS), ("seq", "far", "near")
    )
    whole, filters = P("seq", ("far", "near")), P("seq", None)
    return jax.shard_map(
        local,
        mesh=parted,
        in_specs=(whole, whole, whole, filters, whole),
        out_specs=(whole, whole, whole, filters),
        check_vma=False,
    )
```

time: 142 us -> 101 us (0.71)
  blocking collectives: 56.1 us -> 87.8 us
  starting transfers between devices: 34.2 us -> 2.54 us
  waiting for transfers between devices: 24.2 us -> 0.01 us
  local copies, waits for them, and re-layouts: 11.4 us -> 0.05 us
  Pallas kernels: 13.6 us -> 10.1 us
    all_to_all x2, blocking collectives: 56.1 us -> 87.8 us  [exchange(): lax.all_to_all(parted, ('seq', 'near'), 0, 0, tiled=True)]
    all_to_all x3 -> x0, starting transfers between devices: 21.8 us -> none  [exchange(): return lax.all_to_all(parted, axis, 0, 0, tiled=True).reshape(block.shape)]
    all_to_all x3 -> x0, waiting for transfers between devices: 17.5 us -> none  [exchange(): return lax.all_to_all(parted, axis, 0, 0, tiled=True).reshape(block.shape)]
    unnamed x38 -> x16, local copies, waits for them, and re-layouts: 11.4 us -> 0.05 us
    ppermute x7 -> x1, starting transfers between devices: 12.3 us -> 2.54 us  [local(): other = lax.ppermute(corr, 'far', [(0, 1), (1, 0)])]
    ppermute x7 -> x1, waiting for transfers between devices: 6.71 us -> 0.01 us  [local(): other = lax.ppermute(corr, 'far', [(0, 1), (1, 0)])]
    pallas_call x7 -> x5, Pallas kernels: 13.6 us -> 10.1 us  [call(): pl.pallas_call(kernel, out_shape=[jax.ShapeDtypeStruct(shape, F32) for sh...]
  transfers between devices with their start and end apart: 10 -> 1, of which waited for: 5 -> 0; matrix products, arithmetic and copies ran while one was open for 0% -> 0% of each run, Pallas kernels for 5% -> 4%
where the time goes in v2:
time: 101 us
  blocking collectives  87.8 us (87%)
  Pallas kernels  10.1 us (10%)
  starting transfers between devices  2.54 us (3%)
    all_to_all x2, blocking collectives, exchange(): lax.all_to_all(parted, ('seq', 'near'), 0, 0, tiled=True)  87.8 us
    pallas_call x5, Pallas kernels, call(): pl.pallas_call(kernel, out_shape=[jax.ShapeDtypeStruct(shape, F32) for sh...  10.1 us
    ppermute x1, starting transfers between devices, local(): other = lax.ppermute(corr, 'far', [(0, 1), (1, 0)])  2.54 us
  transfers between devices with their start and end apart: 1, of which 0 were waited for; matrix products, arithmetic and copies ran while one was open for 0% of the time, Pallas kernels for 4%

profile of v2, /device:TPU:1, one launch (start us, length us, event | category | flops | bytes accessed | tf_op | source)
XLA Modules:
  0.0 101.3 jit_solution(7786360770680565659)
XLA Ops:
  0.6 2.0 %pack.1 = f32[2176,128]{1,0:T(8,128)S(1)} custom-call(s32[1]{0:T(128)} %bitcast.near_ref, f32[512,256]{1,0:T(8,128)} %k_ref.1, f32[512,256]{1,0:T(8,128)} %v_ref.1, f32[512,256]{1,0:T(8,128)} %g_ref.1, f32[512,256]{1,0:T(8,128)} %q_hbm.1, f32[512,128]{1,0:T(8,128)} %f_hbm.1), custom_call_target="tpu_custom_call" | custom-call | bytes 3473412 | tf_op jit(solution)/shard_map/pack/pallas_call | solution.py:235
  2.6 0.0 copy-start.3
  2.6 0.0 copy-start.4
  2.7 0.0 copy-start.5
  2.7 0.0 copy-start.6
  2.7 0.0 copy-start.7
  2.7 45.8 %all_to_all.10 = f32[128,17,1,128]{3,2,1,0:T(1,128)S(1)} all-to-all(f32[128,17,1,128]{3,2,1,0:T(1,128)S(1)} %bitcast.9), channel_id=1, replica_groups=mesh['seq'=32,'far'=2,'near'=4] {'seq','near'}, dimensions={0} | all-to-all | bytes 2228224 | tf_op jit(solution)/shard_map/all_to_all | solution.py:250
  48.5 0.0 copy-done.3
  48.5 0.0 copy-done.4
  48.5 0.0 copy-done.5
  48.5 0.0 copy-done.6
  48.6 0.0 copy-done.7
  48.6 2.5 %ahead.1 = (f32[128,128]{1,0:T(8,128)S(1)}, f32[1024,256]{1,0:T(8,128)S(1)}, f32[1024,256]{1,0:T(8,128)S(1)}) custom-call(f32[2176,128]{1,0:T(8,128)S(1)} %bitcast.7, bf16[256,384]{1,0:T(8,128)(2,1)S(1)} %copy-done.6, bf16[128,768]{1,0:T(8,128)(2,1)S(1)} %copy-done.5, bf16[768,256]{1,0:T(8,128)(2,1)S(1)} %copy-done.4, bf16[768,256]{1,0:T(8,128)(2,1)S(1)} %copy-done.3, ...), custom_call_target="tpu_custom_call" | custom-call | flops 1000000000 | bytes 4587520 | tf_op jit(solution)/shard_map/ahead/pallas_call | solution.py:235
  51.1 2.5 %collective-permute-start = (f32[128,128]{1,0:T(8,128)S(1)}, f32[128,128]{1,0:T(8,128)S(1)}, u32[]{:S(2)}, u32[]{:S(2)}) collective-permute-start(f32[128,128]{1,0:T(8,128)S(1)} %get-tuple-element.7.own_ref), channel_id=1, source_target_pairs={{0,4},{4,0},{1,5},{5,1},{2,6},{6,2},{3,7},{7,3},{8,12},{12,8},{9,1... | collective-permute-start | bytes 196616 | tf_op jit(solution)/shard_map/ppermute | solution.py:279
  53.6 4.1 %behind.1._ = f32[2560,128]{1,0:T(8,128)S(1)} custom-call(f32[2176,128]{1,0:T(8,128)S(1)} %bitcast.8, f32[1024,256]{1,0:T(8,128)S(1)} %get-tuple-element.8.gated_ref, f32[1024,256]{1,0:T(8,128)S(1)} %get-tuple-element.9.grad_ref, bf16[256,384]{1,0:T(8,128)(2,1)S(1)} %copy-done.6, bf16[128,768]{1,0:T(8,128)(2,1)S(1)} %copy-done.5, ...), custom_call_target="tpu_custom_call" | custom-call | flops 1000000000 | bytes 5832704 | tf_op jit(solution)/shard_map/behind/pallas_call | solution.py:235
  57.7 0.0 collective-permute-done.other_ref
  57.7 0.1 sum.1
  57.8 0.0 copy-start
  57.8 0.0 copy-start.1
  57.8 0.0 copy-start.2
  57.8 42.0 %all_to_all.11 = f32[128,5,4,128]{3,2,1,0:T(4,128)S(1)} all-to-all(f32[128,5,4,128]{3,2,1,0:T(4,128)S(1)} %bitcast.5), channel_id=1, replica_groups=mesh['seq'=32,'far'=2,'near'=4] {'seq','near'}, dimensions={0} | all-to-all | bytes 2621440 | tf_op jit(solution)/shard_map/all_to_all | solution.py:250
  99.8 0.0 copy-done
  99.8 0.0 copy-done.1
  99.8 0.0 copy-done.2
  99.8 1.5 %unpack.1 = (f32[512,256]{1,0:T(8,128)}, f32[512,256]{1,0:T(8,128)}, f32[512,256]{1,0:T(8,128)}, f32[512,128]{1,0:T(8,128)}) custom-call(f32[2560,128]{1,0:T(8,128)S(1)} %bitcast.6, f32[512,256]{1,0:T(8,128)S(1)} %copy-done.2, f32[512,256]{1,0:T(8,128)S(1)} %copy-done.1, f32[512,256]{1,0:T(8,128)S(1)} %copy-done), custom_call_target="tpu_custom_call" | custom-call | bytes 4718592 | tf_op jit(solution)/shard_map/unpack/pallas_call | solution.py:235
Async XLA Ops:
  2.6 45.9 %copy-start.3 = (bf16[768,256]{1,0:T(8,128)(2,1)S(1)}, bf16[768,256]{1,0:T(8,128)(2,1)}, u32[]{:S(2)}) copy-start(bf16[768,256]{1,0:T(8,128)(2,1)} %constant.17.clone.behind_ref) | copy-start | bytes 1179652
  2.6 45.9 %copy-start.4 = (bf16[768,256]{1,0:T(8,128)(2,1)S(1)}, bf16[768,256]{1,0:T(8,128)(2,1)}, u32[]{:S(2)}) copy-start(bf16[768,256]{1,0:T(8,128)(2,1)} %constant.16.clone.ahead_ref) | copy-start | bytes 1179652
  2.7 45.9 %copy-start.5 = (bf16[128,768]{1,0:T(8,128)(2,1)S(1)}, bf16[128,768]{1,0:T(8,128)(2,1)}, u32[]{:S(2)}) copy-start(bf16[128,768]{1,0:T(8,128)(2,1)} %constant.15.clone.back_ref) | copy-start | bytes 589828
  2.7 45.9 %copy-start.6 = (bf16[256,384]{1,0:T(8,128)(2,1)S(1)}, bf16[256,384]{1,0:T(8,128)(2,1)}, u32[]{:S(2)}) copy-start(bf16[256,384]{1,0:T(8,128)(2,1)} %constant.14.clone.into_ref) | copy-start | bytes 589828
  2.7 45.9 %copy-start.7 = (f32[128,256]{1,0:T(8,128)S(1)}, f32[128,256]{1,0:T(8,128)}, u32[]{:S(2)}) copy-start(f32[128,256]{1,0:T(8,128)} %constant.18.clone.twist_ref) | copy-start | bytes 393220
  51.1 6.6 %collective-permute-start = (f32[128,128]{1,0:T(8,128)S(1)}, f32[128,128]{1,0:T(8,128)S(1)}, u32[]{:S(2)}, u32[]{:S(2)}) collective-permute-start(f32[128,128]{1,0:T(8,128)S(1)} %get-tuple-element.7.own_ref), channel_id=1, source_target_pairs={{0,4},{4,0},{1,5},{5,1},{2,6},{6,2},{3,7},{7,3},{8,12},{12,8},{9,1... | collective-permute-start | bytes 196616 | tf_op jit(solution)/shard_map/ppermute | solution.py:279
  57.8 42.0 %copy-start = (f32[512,256]{1,0:T(8,128)S(1)}, f32[512,256]{1,0:T(8,128)}, u32[]{:S(2)}) copy-start(f32[512,256]{1,0:T(8,128)} %k_ref.1) | copy-start | bytes 1572868
  57.8 42.0 %copy-start.1 = (f32[512,256]{1,0:T(8,128)S(1)}, f32[512,256]{1,0:T(8,128)}, u32[]{:S(2)}) copy-start(f32[512,256]{1,0:T(8,128)} %v_ref.1) | copy-start | bytes 1572868
  57.8 42.0 %copy-start.2 = (f32[512,256]{1,0:T(8,128)S(1)}, f32[512,256]{1,0:T(8,128)}, u32[]{:S(2)}) copy-start(f32[512,256]{1,0:T(8,128)} %g_ref.1) | copy-start | bytes 1572868

commit v3 on v2

--- a/solution.py
+++ b/solution.py
@@ -35,7 +35,7 @@
     high, low = split_np(np.concatenate([np.cos(coarse), -np.sin(coarse)], axis=0))
     into = np.concatenate([high, low, high], axis=1)
     high, low = split_np(np.concatenate([np.cos(coarse.T), -np.sin(coarse.T)], axis=1) * factor)
-    back = np.concatenate([high, low, high], axis=1)
+    back = np.concatenate([high, low], axis=0)
     fine = 2.0 * np.pi * (np.outer(index, index) % SIDE) / SIDE
     cos, sin = np.cos(fine), np.sin(fine)
     high, low = split_np(np.block([[cos, -sin], [sin, cos]]))
@@ -56,36 +56,56 @@
     return jnp.dot(left, right, preferred_element_type=F32)
 
 
-def transform(slabs, into, ahead, twist):
+def coarse_stage(slabs, into, twist, high_ref, low_ref, row):
     high, low = halves(jnp.concatenate(slabs, axis=1))
     coarse = dot(into, jnp.concatenate([high, high, low], axis=0))
     cos, sin = twist[:, :SIDE], twist[:, SIDE:]
-    rows = []
     for at in range(len(slabs)):
         real = coarse[:SIDE, at * SIDE : (at + 1) * SIDE]
         imag = coarse[SIDE:, at * SIDE : (at + 1) * SIDE]
-        rows.append(
-            jnp.concatenate([real * cos + imag * sin, imag * cos - real * sin], axis=1)
+        store_halves(
+            jnp.concatenate([real * cos + imag * sin, imag * cos - real * sin], axis=1),
+            high_ref, low_ref, row + at * SIDE,
         )
-    high, low = halves(jnp.concatenate(rows, axis=0))
-    return dot(jnp.concatenate([high, low, high], axis=1), ahead)
-
-
-def inverse(specs, back, behind, twist):
-    high, low = halves(jnp.concatenate(specs, axis=0))
-    fine = dot(jnp.concatenate([high, low, high], axis=1), behind)
+
+
+def store_halves(value, high_ref, low_ref, row):
+    high, low = halves(value)
+    rows = slice(row, row + value.shape[0])
+    high_ref[rows, :] = high
+    low_ref[rows, :] = low
+
+
+def fine_stage(high_ref, low_ref, row, count, matrix, pieces=2):
+    size = count // pieces
+    results = []
+    for at in range(pieces):
+        rows = slice(row + at * size, row + (at + 1) * size)
+        high, low = high_ref[rows, :], low_ref[rows, :]
+        results.append(dot(jnp.concatenate([high, low, high], axis=1), matrix))
+    return results
+
+
+def last_stage(fine, back, twist):
     cos, sin = twist[:, :SIDE], twist[:, SIDE:]
-    reals, imags = [], []
-    for at in range(len(specs)):
-        real = fine[at * SIDE : (at + 1) * SIDE, :SIDE]
-        imag = fine[at * SIDE : (at + 1) * SIDE, SIDE:]
-        reals.append(real * cos - imag * sin)
-        imags.append(imag * cos + real * sin)
-    turned = jnp.concatenate(
-        [jnp.concatenate(reals, axis=1), jnp.concatenate(imags, axis=1)], axis=0
-    )
-    high, low = halves(turned)
-    return dot(back, jnp.concatenate([high, high, low], axis=0))
+    split = []
+    for at in range(0, len(fine), 2):
+        reals, imags = [], []
+        for slab in fine[at : at + 2]:
+            real, imag = slab[:, :SIDE], slab[:, SIDE:]
+            reals.append(real * cos - imag * sin)
+            imags.append(imag * cos + real * sin)
+        turned = jnp.concatenate(
+            [jnp.concatenate(reals, axis=1), jnp.concatenate(imags, axis=1)], axis=0
+        )
+        split.append(halves(turned))
+    both = [dot(back, high) for high, _ in split]
+    rest = [dot(back[:SIDE], low) for _, low in split]
+    return [b[:SIDE] + b[SIDE:] + r for b, r in zip(both, rest)]
+
+
+def slabs_of(parts):
+    return [part[at : at + SIDE] for part in parts for at in range(0, part.shape[0], SIDE)]
 
 
 def product(left, right):
@@ -118,72 +138,90 @@
             copy = pltpu.make_async_copy(source.at[rows], target.at[rows], sems.at[q * 4 + at])
             copy.start()
             copies.append(copy)
-    start = pl.multiple_of(near_ref[0] * SIDE, SIDE)
-    last = pltpu.make_async_copy(f_hbm.at[pl.ds(start, SIDE)], f_ref, sems.at[16])
-    last.start()
+        if q == 0:
+            start = pl.multiple_of(near_ref[0] * SIDE, SIDE)
+            own = pltpu.make_async_copy(f_hbm.at[pl.ds(start, SIDE)], f_ref, sems.at[16])
+            own.start()
     for q in range(QUARTERS):
-        for at in range(4):
-            copies[q * 4 + at].wait()
         rows = slice(q * SIDE, (q + 1) * SIDE)
-        for h in range(HALVES):
-            cols = slice(h * SIDE, (h + 1) * SIDE)
-            at = h * QUARTERS + q
-            out_ref[pl.ds(at, members, stride=IN_ROWS), :] = (
-                k_ref[rows, cols] * v_ref[rows, cols]
-            ).T
-            out_ref[pl.ds(8 + at, members, stride=IN_ROWS), :] = (
-                g_ref[rows, cols] * q_ref[rows, cols]
-            ).T
-    last.wait()
-    out_ref[pl.ds(16, members, stride=IN_ROWS), :] = f_ref[...].T
+        for array, (left, right) in enumerate(((k_ref, v_ref), (g_ref, q_ref))):
+            copies[q * 4 + array * 2].wait()
+            copies[q * 4 + array * 2 + 1].wait()
+            for h in range(HALVES):
+                cols = slice(h * SIDE, (h + 1) * SIDE)
+                at = array * 8 + h * QUARTERS + q
+                out_ref[pl.ds(at, members, stride=IN_ROWS), :] = (
+                    left[rows, cols] * right[rows, cols]
+                ).T
+        if q == 0:
+            own.wait()
+            out_ref[pl.ds(16, members, stride=IN_ROWS), :] = f_ref[...].T
 
 
 def ahead_kernel(
     shards, in_ref, into_ref, back_ref, ahead_ref, behind_ref, twist_ref,
-    corr_ref, gated_ref, grad_ref,
+    corr_ref, gated_ref, grad_ref, high_ref, low_ref,
 ):
-    into, ahead, twist = into_ref[...], ahead_ref[...], twist_ref[...]
+    into, twist = into_ref[...], twist_ref[...]
     pitch = BLOCKS * IN_ROWS
+    span = BLOCKS * HALVES * SIDE
+    half = span // 2
     total = None
-    for block in range(BLOCKS):
-        specs = []
-        for array, out_ref in enumerate((gated_ref, grad_ref)):
+    for part in range(2):
+        for array in range(2):
             slabs = [
                 gather_rows(
                     in_ref, block * IN_ROWS + array * 8 + h * QUARTERS, 1, shards, pitch
                 )
+                for block in (part * 2, part * 2 + 1)
                 for h in range(HALVES)
             ]
-            spec = transform(slabs, into, ahead, twist)
-            out_ref[pl.ds(block * 2 * SIDE, 2 * SIDE), :] = spec
-            specs.append(spec)
-        term = turned_product(*specs)
-        term = term[:SIDE] + term[SIDE:]
-        total = term if total is None else total + term
-    corr_ref[...] = inverse([total], back_ref[...], behind_ref[...], twist)
+            coarse_stage(slabs, into, twist, high_ref, low_ref, part * span + array * half)
+    for part in range(2):
+        both = fine_stage(high_ref, low_ref, part * span, span, ahead_ref[...], 1)[0]
+        both = (both[:half], both[half:])
+        rows = slice(part * half, (part + 1) * half)
+        gated_ref[rows, :] = both[0]
+        grad_ref[rows, :] = both[1]
+        for at in range(0, half, SIDE):
+            term = turned_product(both[0][at : at + SIDE], both[1][at : at + SIDE])
+            total = term if total is None else total + term
+    store_halves(total, high_ref, low_ref, 2 * span)
+    fine = fine_stage(high_ref, low_ref, 2 * span, SIDE, behind_ref[...], 1)
+    corr_ref[...] = last_stage([jnp.concatenate(fine, axis=0)], back_ref[...], twist)[0]
 
 
 def behind_kernel(
     shards, in_ref, gated_ref, grad_ref, into_ref, back_ref, ahead_ref, behind_ref, twist_ref,
-    out_ref,
+    out_ref, high_ref, low_ref,
 ):
-    twist, back, behind = twist_ref[...], back_ref[...], behind_ref[...]
+    twist, back = twist_ref[...], back_ref[...]
     pitch = BLOCKS * OUT_ROWS
+    group = 2 * HALVES * SIDE
+    spare = BLOCKS * group
     slab = gather_rows(in_ref, 16, IN_ROWS, shards, BLOCKS * IN_ROWS)
-    filt = transform([slab], into_ref[...], ahead_ref[...], twist)
+    coarse_stage([slab], into_ref[...], twist, high_ref, low_ref, spare)
+    filt = jnp.concatenate(fine_stage(high_ref, low_ref, spare, SIDE, ahead_ref[...]), axis=0)
     for block in range(BLOCKS):
         for array, spec_ref in enumerate((gated_ref, grad_ref)):
             combine = turned_product if array else product
-            specs = [
-                combine(filt, spec_ref[pl.ds((block * 2 + h) * SIDE, SIDE), :])
-                for h in range(HALVES)
-            ]
-            result = inverse(specs, back, behind, twist)
             for h in range(HALVES):
+                spec = spec_ref[pl.ds((block * 2 + h) * SIDE, SIDE), :]
+                row = block * group + (array * HALVES + h) * SIDE
+                store_halves(combine(filt, spec), high_ref, low_ref, row)
+    for part in range(2):
+        fine = slabs_of(
+            fine_stage(high_ref, low_ref, part * 2 * group, 2 * group, behind_ref[...])
+        )
+        for near in range(2):
+            block = part * 2 + near
+            results = last_stage(fine[near * 4 : near * 4 + 4], back, twist)
+            for at in range(2 * HALVES):
+                column = at % 2 * SIDE
                 for q in range(QUARTERS):
-                    at = block * OUT_ROWS + array * 8 + h * QUARTERS + q
-                    out_ref[pl.ds(at, shards, stride=pitch), :] = result[
-                        q * shards : (q + 1) * shards, h * SIDE : (h + 1) * SIDE
+                    row = block * OUT_ROWS + at * QUARTERS + q
+                    out_ref[pl.ds(row, shards, stride=pitch), :] = results[at // 2][
+                        q * shards : (q + 1) * shards, column : column + SIDE
                     ]
 
 
@@ -247,19 +285,20 @@
 
 def exchange(block, inner):
     parted = block.reshape(block.shape[0] // int(np.prod(inner)), *inner, SIDE)
-    return lax.all_to_all(parted, ("seq", "near"), 0, 0, tiled=True).reshape(block.shape)
+    return lax.all_to_all(parted, ("seq", "far", "mid"), 0, 0, tiled=True).reshape(block.shape)
 
 
 def local(q_gate, k_gate, values, filter_raw, grad_out):
     shards = lax.axis_size("seq")
-    members = shards * lax.axis_size("near")
+    members = shards * BLOCKS
     total = SIDE * SIDE
     into, back, ahead, behind, twist = (
         jnp.asarray(t) for t in tables(shards, total ** (-0.5) / total)
     )
     block = q_gate.shape
     wide = pltpu.VMEM(block, F32)
-    near = lax.axis_index("near").astype(jnp.int32).reshape(1)
+    split = [pltpu.VMEM((17 * SIDE, 2 * SIDE), BF)] * 2
+    near = lax.axis_index(("far", "mid")).astype(jnp.int32).reshape(1)
     packed = call(
         functools.partial(pack_kernel, members),
         [(IN_ROWS * members, SIDE)],
@@ -274,14 +313,16 @@
         [(SIDE, SIDE), (8 * SIDE, 2 * SIDE), (8 * SIDE, 2 * SIDE)],
         (spread, into, back, ahead, behind, twist),
         "ahead",
+        scratch=split,
         flops=10**9,
     )
-    other = lax.ppermute(corr, "far", [(0, 1), (1, 0)])
+    other = lax.ppermute(corr, "pair", [(0, 1), (1, 0)])
     results = call(
         functools.partial(behind_kernel, shards),
         [(OUT_ROWS * members, SIDE)],
         (spread, gated_spec, grad_spec, into, back, ahead, behind, twist),
         "behind",
+        scratch=split,
         flops=10**9,
     )[0]
     results = call(
@@ -307,9 +348,9 @@
 def solution(mesh):
     shards, groups = mesh.devices.shape
     parted = Mesh(
-        mesh.devices.reshape(shards, groups // BLOCKS, BLOCKS), ("seq", "far", "near")
-    )
-    whole, filters = P("seq", ("far", "near")), P("seq", None)
+        mesh.devices.reshape(shards, 2, groups // 4, 2), ("seq", "far", "mid", "pair")
+    )
+    whole, filters = P("seq", ("far", "mid", "pair")), P("seq", None)
     return jax.shard_map(
         local,
         mesh=parted,

time: 101 us -> 103 us (1.020)
  blocking collectives: 87.8 us -> 92.7 us
  Pallas kernels: 10.1 us -> 7.91 us
  starting transfers between devices: 2.54 us -> 0.48 us
    all_to_all x2, blocking collectives: 87.8 us -> 92.7 us  [exchange(): lax.all_to_all(parted, ('seq', 'far', 'mid'), 0, 0, tiled=True)]
    pallas_call x5, Pallas kernels: 10.1 us -> 7.91 us  [call(): pl.pallas_call(kernel, out_shape=[jax.ShapeDtypeStruct(shape, F32) for sh...]
    ppermute x1, starting transfers between devices: 2.54 us -> 0.48 us  [local(): other = lax.ppermute(corr, 'pair', [(0, 1), (1, 0)])]
  transfers between devices with their start and end apart: 1 -> 1, of which waited for: 0 -> 1; matrix products, arithmetic and copies ran while one was open for 0% -> 0% of each run, Pallas kernels for 4% -> 2%
where the time goes in v3:
time: 103 us; the launch traced here: 102 us
  blocking collectives  92.7 us (90%)
  Pallas kernels  7.91 us (8%)
    all_to_all x2, blocking collectives, exchange(): lax.all_to_all(parted, ('seq', 'far', 'mid'), 0, 0, tiled=True)  92.7 us
    pallas_call x5, Pallas kernels, call(): pl.pallas_call(kernel, out_shape=[jax.ShapeDtypeStruct(shape, F32) for sh...  7.91 us
  transfers between devices with their start and end apart: 1, of which 1 were waited for; matrix products, arithmetic and copies ran while one was open for 0% of the time, Pallas kernels for 2%

profile of v3, /device:TPU:1, one launch (start us, length us, event | category | flops | bytes accessed | tf_op | source)
XLA Modules:
  0.0 102.5 jit_solution(9729352332752811336)
XLA Ops:
  0.6 2.1 %pack.1 = f32[2176,128]{1,0:T(8,128)S(1)} custom-call(s32[1]{0:T(128)} %bitcast.near_ref, f32[512,256]{1,0:T(8,128)} %k_ref.1, f32[512,256]{1,0:T(8,128)} %v_ref.1, f32[512,256]{1,0:T(8,128)} %g_ref.1, f32[512,256]{1,0:T(8,128)} %q_hbm.1, f32[512,128]{1,0:T(8,128)} %f_hbm.1), custom_call_target="tpu_custom_call" | custom-call | bytes 3473412 | tf_op jit(solution)/shard_map/pack/pallas_call | solution.py:273
  2.7 0.0 copy-start.3
  2.7 0.0 copy-start.4
  2.7 0.0 copy-start.5
  2.8 0.0 copy-start.6
  2.8 0.0 copy-start.7
  2.8 48.4 %all_to_all.10 = f32[128,17,1,128]{3,2,1,0:T(1,128)S(1)} all-to-all(f32[128,17,1,128]{3,2,1,0:T(1,128)S(1)} %bitcast.9), channel_id=1, replica_groups=mesh['seq'=32,'far'=2,'mid'=2,'pair'=2] {'seq','far','mid'}, dimensions={0} | all-to-all | bytes 2228224 | tf_op jit(solution)/shard_map/all_to_all | solution.py:288
  51.2 0.0 copy-done.3
  51.2 0.0 copy-done.4
  51.2 0.0 copy-done.5
  51.2 0.0 copy-done.6
  51.2 0.0 copy-done.7
  51.3 2.1 %ahead.1 = (f32[128,128]{1,0:T(8,128)S(1)}, f32[1024,256]{1,0:T(8,128)S(1)}, f32[1024,256]{1,0:T(8,128)S(1)}) custom-call(f32[2176,128]{1,0:T(8,128)S(1)} %bitcast.7, bf16[256,384]{1,0:T(8,128)(2,1)S(1)} %copy-done.5, bf16[256,256]{1,0:T(8,128)(2,1)S(1)} %copy-done.7, bf16[768,256]{1,0:T(8,128)(2,1)S(1)} %copy-done.4, bf16[768,256]{1,0:T(8,128)(2,1)S(1)} %copy-done.3, ...), custom_call_target="tpu_custom_call" | custom-call | flops 1000000000 | bytes 4521984 | tf_op jit(solution)/shard_map/ahead/pallas_call | solution.py:273
  53.4 0.5 collective-permute-start
  53.9 2.2 %behind.1._ = f32[2560,128]{1,0:T(8,128)S(1)} custom-call(f32[2176,128]{1,0:T(8,128)S(1)} %bitcast.8, f32[1024,256]{1,0:T(8,128)S(1)} %get-tuple-element.8.gated_ref, f32[1024,256]{1,0:T(8,128)S(1)} %get-tuple-element.9.grad_ref, bf16[256,384]{1,0:T(8,128)(2,1)S(1)} %copy-done.5, bf16[256,256]{1,0:T(8,128)(2,1)S(1)} %copy-done.7, ...), custom_call_target="tpu_custom_call" | custom-call | flops 1000000000 | bytes 5767168 | tf_op jit(solution)/shard_map/behind/pallas_call | solution.py:273
  56.0 0.6 collective-permute-done.other_ref
  56.6 0.1 sum.1
  56.7 0.0 copy-start
  56.7 0.0 copy-start.1
  56.7 0.0 copy-start.2
  56.7 44.3 %all_to_all.11 = f32[128,5,4,128]{3,2,1,0:T(4,128)S(1)} all-to-all(f32[128,5,4,128]{3,2,1,0:T(4,128)S(1)} %bitcast.5), channel_id=1, replica_groups=mesh['seq'=32,'far'=2,'mid'=2,'pair'=2] {'seq','far','mid'}, dimensions={0} | all-to-all | bytes 2621440 | tf_op jit(solution)/shard_map/all_to_all | solution.py:288
  101.0 0.0 copy-done
  101.0 0.0 copy-done.1
  101.0 0.0 copy-done.2
  101.0 1.5 %unpack.1 = (f32[512,256]{1,0:T(8,128)}, f32[512,256]{1,0:T(8,128)}, f32[512,256]{1,0:T(8,128)}, f32[512,128]{1,0:T(8,128)}) custom-call(f32[2560,128]{1,0:T(8,128)S(1)} %bitcast.6, f32[512,256]{1,0:T(8,128)S(1)} %copy-done.2, f32[512,256]{1,0:T(8,128)S(1)} %copy-done.1, f32[512,256]{1,0:T(8,128)S(1)} %copy-done), custom_call_target="tpu_custom_call" | custom-call | bytes 4718592 | tf_op jit(solution)/shard_map/unpack/pallas_call | solution.py:273
Async XLA Ops:
  2.7 48.5 %copy-start.3 = (bf16[768,256]{1,0:T(8,128)(2,1)S(1)}, bf16[768,256]{1,0:T(8,128)(2,1)}, u32[]{:S(2)}) copy-start(bf16[768,256]{1,0:T(8,128)(2,1)} %constant.23.clone.behind_ref) | copy-start | bytes 1179652
  2.7 48.5 %copy-start.4 = (bf16[768,256]{1,0:T(8,128)(2,1)S(1)}, bf16[768,256]{1,0:T(8,128)(2,1)}, u32[]{:S(2)}) copy-start(bf16[768,256]{1,0:T(8,128)(2,1)} %constant.22.clone.ahead_ref) | copy-start | bytes 1179652
  2.7 48.5 %copy-start.5 = (bf16[256,384]{1,0:T(8,128)(2,1)S(1)}, bf16[256,384]{1,0:T(8,128)(2,1)}, u32[]{:S(2)}) copy-start(bf16[256,384]{1,0:T(8,128)(2,1)} %constant.20.clone.into_ref) | copy-start | bytes 589828
  2.8 48.5 %copy-start.6 = (f32[128,256]{1,0:T(8,128)S(1)}, f32[128,256]{1,0:T(8,128)}, u32[]{:S(2)}) copy-start(f32[128,256]{1,0:T(8,128)} %constant.24.clone.twist_ref) | copy-start | bytes 393220
  2.8 48.5 %copy-start.7 = (bf16[256,256]{1,0:T(8,128)(2,1)S(1)}, bf16[256,256]{1,0:T(8,128)(2,1)}, u32[]{:S(2)}) copy-start(bf16[256,256]{1,0:T(8,128)(2,1)} %constant.21.clone.back_ref) | copy-start | bytes 393220
  53.4 3.2 %collective-permute-start = (f32[128,128]{1,0:T(8,128)S(1)}, f32[128,128]{1,0:T(8,128)S(1)}, u32[]{:S(2)}, u32[]{:S(2)}) collective-permute-start(f32[128,128]{1,0:T(8,128)S(1)} %get-tuple-element.7.own_ref), channel_id=1, source_target_pairs={{0,1},{1,0},{2,3},{3,2},{4,5},{5,4},{6,7},{7,6},{8,9},{9,8},{10,11... | collective-permute-start | bytes 196616 | tf_op jit(solution)/shard_map/ppermute | solution.py:319
  56.7 44.3 %copy-start = (f32[512,256]{1,0:T(8,128)S(1)}, f32[512,256]{1,0:T(8,128)}, u32[]{:S(2)}) copy-start(f32[512,256]{1,0:T(8,128)} %k_ref.1) | copy-start | bytes 1572868
  56.7 44.3 %copy-start.1 = (f32[512,256]{1,0:T(8,128)S(1)}, f32[512,256]{1,0:T(8,128)}, u32[]{:S(2)}) copy-start(f32[512,256]{1,0:T(8,128)} %v_ref.1) | copy-start | bytes 1572868
  56.7 44.3 %copy-start.2 = (f32[512,256]{1,0:T(8,128)S(1)}, f32[512,256]{1,0:T(8,128)}, u32[]{:S(2)}) copy-start(f32[512,256]{1,0:T(8,128)} %g_ref.1) | copy-start | bytes 1572868

commit v4 on v3

--- a/solution.py
+++ b/solution.py
@@ -285,12 +285,12 @@
 
 def exchange(block, inner):
     parted = block.reshape(block.shape[0] // int(np.prod(inner)), *inner, SIDE)
-    return lax.all_to_all(parted, ("seq", "far", "mid"), 0, 0, tiled=True).reshape(block.shape)
+    return lax.all_to_all(parted, ("seq", "near"), 0, 0, tiled=True).reshape(block.shape)
 
 
 def local(q_gate, k_gate, values, filter_raw, grad_out):
     shards = lax.axis_size("seq")
-    members = shards * BLOCKS
+    members = shards * lax.axis_size("near")
     total = SIDE * SIDE
     into, back, ahead, behind, twist = (
         jnp.asarray(t) for t in tables(shards, total ** (-0.5) / total)
@@ -298,7 +298,7 @@
     block = q_gate.shape
     wide = pltpu.VMEM(block, F32)
     split = [pltpu.VMEM((17 * SIDE, 2 * SIDE), BF)] * 2
-    near = lax.axis_index(("far", "mid")).astype(jnp.int32).reshape(1)
+    near = lax.axis_index("near").astype(jnp.int32).reshape(1)
     packed = call(
         functools.partial(pack_kernel, members),
         [(IN_ROWS * members, SIDE)],
@@ -316,7 +316,7 @@
         scratch=split,
         flops=10**9,
     )
-    other = lax.ppermute(corr, "pair", [(0, 1), (1, 0)])
+    other = lax.ppermute(corr, "far", [(0, 1), (1, 0)])
     results = call(
         functools.partial(behind_kernel, shards),
         [(OUT_ROWS * members, SIDE)],
@@ -348,9 +348,9 @@
 def solution(mesh):
     shards, groups = mesh.devices.shape
     parted = Mesh(
-        mesh.devices.reshape(shards, 2, groups // 4, 2), ("seq", "far", "mid", "pair")
-    )
-    whole, filters = P("seq", ("far", "mid", "pair")), P("seq", None)
+        mesh.devices.reshape(shards, groups // BLOCKS, BLOCKS), ("seq", "far", "near")
+    )
+    whole, filters = P("seq", ("far", "near")), P("seq", None)
     return jax.shard_map(
         local,
         mesh=parted,

time: 103 us -> 100 us (0.971)
  blocking collectives: 92.7 us -> 88.7 us
  starting transfers between devices: 0.48 us -> 2.55 us
    all_to_all x2, blocking collectives: 92.7 us -> 88.7 us  [exchange(): lax.all_to_all(parted, ('seq', 'near'), 0, 0, tiled=True)]
    ppermute x1, starting transfers between devices: 0.48 us -> 2.55 us  [local(): other = lax.ppermute(corr, 'far', [(0, 1), (1, 0)])]
  transfers between devices with their start and end apart: 1 -> 1, of which waited for: 1 -> 0; matrix products, arithmetic and copies ran while one was open for 0% -> 0% of each run, Pallas kernels for 2% -> 2%
where the time goes in v4:
time: 100 us; the launch traced here: 99.9 us
  blocking collectives  88.7 us (89%)
  Pallas kernels  7.91 us (8%)
  starting transfers between devices  2.55 us (3%)
    all_to_all x2, blocking collectives, exchange(): lax.all_to_all(parted, ('seq', 'near'), 0, 0, tiled=True)  88.7 us
    pallas_call x5, Pallas kernels, call(): pl.pallas_call(kernel, out_shape=[jax.ShapeDtypeStruct(shape, F32) for sh...  7.91 us
    ppermute x1, starting transfers between devices, local(): other = lax.ppermute(corr, 'far', [(0, 1), (1, 0)])  2.55 us
  transfers between devices with their start and end apart: 1, of which 0 were waited for; matrix products, arithmetic and copies ran while one was open for 0% of the time, Pallas kernels for 2%

profile of v4, /device:TPU:1, one launch (start us, length us, event | category | flops | bytes accessed | tf_op | source)
XLA Modules:
  0.0 99.9 jit_solution(12291621524766910228)
XLA Ops:
  0.6 2.1 %pack.1 = f32[2176,128]{1,0:T(8,128)S(1)} custom-call(s32[1]{0:T(128)} %bitcast.near_ref, f32[512,256]{1,0:T(8,128)} %k_ref.1, f32[512,256]{1,0:T(8,128)} %v_ref.1, f32[512,256]{1,0:T(8,128)} %g_ref.1, f32[512,256]{1,0:T(8,128)} %q_hbm.1, f32[512,128]{1,0:T(8,128)} %f_hbm.1), custom_call_target="tpu_custom_call" | custom-call | bytes 3473412 | tf_op jit(solution)/shard_map/pack/pallas_call | solution.py:273
  2.7 0.0 copy-start.3
  2.7 0.0 copy-start.4
  2.7 0.0 copy-start.5
  2.8 0.0 copy-start.6
  2.8 0.0 copy-start.7
  2.8 45.8 %all_to_all.10 = f32[128,17,1,128]{3,2,1,0:T(1,128)S(1)} all-to-all(f32[128,17,1,128]{3,2,1,0:T(1,128)S(1)} %bitcast.9), channel_id=1, replica_groups=mesh['seq'=32,'far'=2,'near'=4] {'seq','near'}, dimensions={0} | all-to-all | bytes 2228224 | tf_op jit(solution)/shard_map/all_to_all | solution.py:288
  48.6 0.0 copy-done.3
  48.6 0.0 copy-done.4
  48.6 0.0 copy-done.5
  48.6 0.0 copy-done.6
  48.6 0.0 copy-done.7
  48.7 2.1 %ahead.1 = (f32[128,128]{1,0:T(8,128)S(1)}, f32[1024,256]{1,0:T(8,128)S(1)}, f32[1024,256]{1,0:T(8,128)S(1)}) custom-call(f32[2176,128]{1,0:T(8,128)S(1)} %bitcast.7, bf16[256,384]{1,0:T(8,128)(2,1)S(1)} %copy-done.5, bf16[256,256]{1,0:T(8,128)(2,1)S(1)} %copy-done.7, bf16[768,256]{1,0:T(8,128)(2,1)S(1)} %copy-done.4, bf16[768,256]{1,0:T(8,128)(2,1)S(1)} %copy-done.3, ...), custom_call_target="tpu_custom_call" | custom-call | flops 1000000000 | bytes 4521984 | tf_op jit(solution)/shard_map/ahead/pallas_call | solution.py:273
  50.8 2.5 %collective-permute-start = (f32[128,128]{1,0:T(8,128)S(1)}, f32[128,128]{1,0:T(8,128)S(1)}, u32[]{:S(2)}, u32[]{:S(2)}) collective-permute-start(f32[128,128]{1,0:T(8,128)S(1)} %get-tuple-element.7.own_ref), channel_id=1, source_target_pairs={{0,4},{4,0},{1,5},{5,1},{2,6},{6,2},{3,7},{7,3},{8,12},{12,8},{9,1... | collective-permute-start | bytes 196616 | tf_op jit(solution)/shard_map/ppermute | solution.py:319
  53.3 2.2 %behind.1._ = f32[2560,128]{1,0:T(8,128)S(1)} custom-call(f32[2176,128]{1,0:T(8,128)S(1)} %bitcast.8, f32[1024,256]{1,0:T(8,128)S(1)} %get-tuple-element.8.gated_ref, f32[1024,256]{1,0:T(8,128)S(1)} %get-tuple-element.9.grad_ref, bf16[256,384]{1,0:T(8,128)(2,1)S(1)} %copy-done.5, bf16[256,256]{1,0:T(8,128)(2,1)S(1)} %copy-done.7, ...), custom_call_target="tpu_custom_call" | custom-call | flops 1000000000 | bytes 5767168 | tf_op jit(solution)/shard_map/behind/pallas_call | solution.py:273
  55.5 0.0 collective-permute-done.other_ref
  55.5 0.1 sum.1
  55.6 0.0 copy-start
  55.6 0.0 copy-start.1
  55.6 0.0 copy-start.2
  55.6 42.8 %all_to_all.11 = f32[128,5,4,128]{3,2,1,0:T(4,128)S(1)} all-to-all(f32[128,5,4,128]{3,2,1,0:T(4,128)S(1)} %bitcast.5), channel_id=1, replica_groups=mesh['seq'=32,'far'=2,'near'=4] {'seq','near'}, dimensions={0} | all-to-all | bytes 2621440 | tf_op jit(solution)/shard_map/all_to_all | solution.py:288
  98.4 0.0 copy-done
  98.4 0.0 copy-done.1
  98.4 0.0 copy-done.2
  98.5 1.5 %unpack.1 = (f32[512,256]{1,0:T(8,128)}, f32[512,256]{1,0:T(8,128)}, f32[512,256]{1,0:T(8,128)}, f32[512,128]{1,0:T(8,128)}) custom-call(f32[2560,128]{1,0:T(8,128)S(1)} %bitcast.6, f32[512,256]{1,0:T(8,128)S(1)} %copy-done.2, f32[512,256]{1,0:T(8,128)S(1)} %copy-done.1, f32[512,256]{1,0:T(8,128)S(1)} %copy-done), custom_call_target="tpu_custom_call" | custom-call | bytes 4718592 | tf_op jit(solution)/shard_map/unpack/pallas_call | solution.py:273
Async XLA Ops:
  2.7 45.9 %copy-start.3 = (bf16[768,256]{1,0:T(8,128)(2,1)S(1)}, bf16[768,256]{1,0:T(8,128)(2,1)}, u32[]{:S(2)}) copy-start(bf16[768,256]{1,0:T(8,128)(2,1)} %constant.17.clone.behind_ref) | copy-start | bytes 1179652
  2.7 45.9 %copy-start.4 = (bf16[768,256]{1,0:T(8,128)(2,1)S(1)}, bf16[768,256]{1,0:T(8,128)(2,1)}, u32[]{:S(2)}) copy-start(bf16[768,256]{1,0:T(8,128)(2,1)} %constant.16.clone.ahead_ref) | copy-start | bytes 1179652
  2.7 45.9 %copy-start.5 = (bf16[256,384]{1,0:T(8,128)(2,1)S(1)}, bf16[256,384]{1,0:T(8,128)(2,1)}, u32[]{:S(2)}) copy-start(bf16[256,384]{1,0:T(8,128)(2,1)} %constant.14.clone.into_ref) | copy-start | bytes 589828
  2.8 45.9 %copy-start.6 = (f32[128,256]{1,0:T(8,128)S(1)}, f32[128,256]{1,0:T(8,128)}, u32[]{:S(2)}) copy-start(f32[128,256]{1,0:T(8,128)} %constant.18.clone.twist_ref) | copy-start | bytes 393220
  2.8 45.9 %copy-start.7 = (bf16[256,256]{1,0:T(8,128)(2,1)S(1)}, bf16[256,256]{1,0:T(8,128)(2,1)}, u32[]{:S(2)}) copy-start(bf16[256,256]{1,0:T(8,128)(2,1)} %constant.15.clone.back_ref) | copy-start | bytes 393220
  50.8 4.7 %collective-permute-start = (f32[128,128]{1,0:T(8,128)S(1)}, f32[128,128]{1,0:T(8,128)S(1)}, u32[]{:S(2)}, u32[]{:S(2)}) collective-permute-start(f32[128,128]{1,0:T(8,128)S(1)} %get-tuple-element.7.own_ref), channel_id=1, source_target_pairs={{0,4},{4,0},{1,5},{5,1},{2,6},{6,2},{3,7},{7,3},{8,12},{12,8},{9,1... | collective-permute-start | bytes 196616 | tf_op jit(solution)/shard_map/ppermute | solution.py:319
  55.6 42.9 %copy-start = (f32[512,256]{1,0:T(8,128)S(1)}, f32[512,256]{1,0:T(8,128)}, u32[]{:S(2)}) copy-start(f32[512,256]{1,0:T(8,128)} %k_ref.1) | copy-start | bytes 1572868
  55.6 42.8 %copy-start.1 = (f32[512,256]{1,0:T(8,128)S(1)}, f32[512,256]{1,0:T(8,128)}, u32[]{:S(2)}) copy-start(f32[512,256]{1,0:T(8,128)} %v_ref.1) | copy-start | bytes 1572868
  55.6 42.8 %copy-start.2 = (f32[512,256]{1,0:T(8,128)S(1)}, f32[512,256]{1,0:T(8,128)}, u32[]{:S(2)}) copy-start(f32[512,256]{1,0:T(8,128)} %g_ref.1) | copy-start | bytes 1572868

commit v5 on v4

--- a/solution.py
+++ b/solution.py
@@ -163,7 +163,7 @@
     corr_ref, gated_ref, grad_ref, high_ref, low_ref,
 ):
     into, twist = into_ref[...], twist_ref[...]
-    pitch = BLOCKS * IN_ROWS
+    pitch = shards * IN_ROWS
     span = BLOCKS * HALVES * SIDE
     half = span // 2
     total = None
@@ -171,7 +171,7 @@
         for array in range(2):
             slabs = [
                 gather_rows(
-                    in_ref, block * IN_ROWS + array * 8 + h * QUARTERS, 1, shards, pitch
+                    in_ref, block * pitch + array * 8 + h * QUARTERS, 1, shards, IN_ROWS
                 )
                 for block in (part * 2, part * 2 + 1)
                 for h in range(HALVES)
@@ -196,10 +196,10 @@
     out_ref, high_ref, low_ref,
 ):
     twist, back = twist_ref[...], back_ref[...]
-    pitch = BLOCKS * OUT_ROWS
+    pitch = shards * OUT_ROWS
     group = 2 * HALVES * SIDE
     spare = BLOCKS * group
-    slab = gather_rows(in_ref, 16, IN_ROWS, shards, BLOCKS * IN_ROWS)
+    slab = gather_rows(in_ref, 16, shards * IN_ROWS, shards, IN_ROWS)
     coarse_stage([slab], into_ref[...], twist, high_ref, low_ref, spare)
     filt = jnp.concatenate(fine_stage(high_ref, low_ref, spare, SIDE, ahead_ref[...]), axis=0)
     for block in range(BLOCKS):
@@ -219,8 +219,8 @@
             for at in range(2 * HALVES):
                 column = at % 2 * SIDE
                 for q in range(QUARTERS):
-                    row = block * OUT_ROWS + at * QUARTERS + q
-                    out_ref[pl.ds(row, shards, stride=pitch), :] = results[at // 2][
+                    row = block * pitch + at * QUARTERS + q
+                    out_ref[pl.ds(row, shards, stride=OUT_ROWS), :] = results[at // 2][
                         q * shards : (q + 1) * shards, column : column + SIDE
                     ]
 
@@ -229,8 +229,8 @@
     total = own_ref[...] + other_ref[...]
     for block in range(BLOCKS):
         for q in range(QUARTERS):
-            at = block * OUT_ROWS + 16 + q
-            out_ref[pl.ds(at, shards, stride=BLOCKS * OUT_ROWS), :] = total[
+            at = block * shards * OUT_ROWS + 16 + q
+            out_ref[pl.ds(at, shards, stride=OUT_ROWS), :] = total[
                 q * shards : (q + 1) * shards
             ]
 
@@ -285,7 +285,7 @@
 
 def exchange(block, inner):
     parted = block.reshape(block.shape[0] // int(np.prod(inner)), *inner, SIDE)
-    return lax.all_to_all(parted, ("seq", "near"), 0, 0, tiled=True).reshape(block.shape)
+    return lax.all_to_all(parted, ("near", "seq"), 0, 0, tiled=True).reshape(block.shape)
 
 
 def local(q_gate, k_gate, values, filter_raw, grad_out):

time: 100 us -> 99.6 us (level)
  blocking collectives: 88.7 us -> 87.4 us
    all_to_all x2, blocking collectives: 88.7 us -> 87.4 us  [exchange(): lax.all_to_all(parted, ('near', 'seq'), 0, 0, tiled=True)]
  transfers between devices with their start and end apart: 1 -> 1, of which waited for: 0 -> 1; matrix products, arithmetic and copies ran while one was open for 0% -> 0% of each run, Pallas kernels for 2% -> 2%
where the time goes in v5:
time: 99.6 us; the launch traced here: 98.6 us
  blocking collectives  87.4 us (88%)
  Pallas kernels  7.78 us (8%)
  starting transfers between devices  2.53 us (3%)
    all_to_all x2, blocking collectives, exchange(): lax.all_to_all(parted, ('near', 'seq'), 0, 0, tiled=True)  87.4 us
    pallas_call x5, Pallas kernels, call(): pl.pallas_call(kernel, out_shape=[jax.ShapeDtypeStruct(shape, F32) for sh...  7.78 us
    ppermute x1, starting transfers between devices, local(): other = lax.ppermute(corr, 'far', [(0, 1), (1, 0)])  2.53 us
  transfers between devices with their start and end apart: 1, of which 1 were waited for; matrix products, arithmetic and copies ran while one was open for 0% of the time, Pallas kernels for 2%

profile of v5, /device:TPU:1, one launch (start us, length us, event | category | flops | bytes accessed | tf_op | source)
XLA Modules:
  0.0 98.6 jit_solution(405491604709900901)
XLA Ops:
  0.6 2.1 %pack.1 = f32[2176,128]{1,0:T(8,128)S(1)} custom-call(s32[1]{0:T(128)} %bitcast.near_ref, f32[512,256]{1,0:T(8,128)} %k_ref.1, f32[512,256]{1,0:T(8,128)} %v_ref.1, f32[512,256]{1,0:T(8,128)} %g_ref.1, f32[512,256]{1,0:T(8,128)} %q_hbm.1, f32[512,128]{1,0:T(8,128)} %f_hbm.1), custom_call_target="tpu_custom_call" | custom-call | bytes 3473412 | tf_op jit(solution)/shard_map/pack/pallas_call | solution.py:273
  2.7 0.0 copy-start.3
  2.7 0.0 copy-start.4
  2.7 0.0 copy-start.5
  2.8 0.0 copy-start.6
  2.8 0.0 copy-start.7
  2.8 44.3 %all_to_all.10 = f32[128,17,1,128]{3,2,1,0:T(1,128)S(1)} all-to-all(f32[128,17,1,128]{3,2,1,0:T(1,128)S(1)} %bitcast.9), channel_id=1, replica_groups=mesh['seq'=32,'far'=2,'near'=4] {'near','seq'}, dimensions={0} | all-to-all | bytes 2228224 | tf_op jit(solution)/shard_map/all_to_all | solution.py:288
  47.1 0.0 copy-done.3
  47.1 0.0 copy-done.4
  47.1 0.0 copy-done.5
  47.1 0.0 copy-done.6
  47.1 0.0 copy-done.7
  47.2 2.1 %ahead.1 = (f32[128,128]{1,0:T(8,128)S(1)}, f32[1024,256]{1,0:T(8,128)S(1)}, f32[1024,256]{1,0:T(8,128)S(1)}) custom-call(f32[2176,128]{1,0:T(8,128)S(1)} %bitcast.7, bf16[256,384]{1,0:T(8,128)(2,1)S(1)} %copy-done.5, bf16[256,256]{1,0:T(8,128)(2,1)S(1)} %copy-done.7, bf16[768,256]{1,0:T(8,128)(2,1)S(1)} %copy-done.4, bf16[768,256]{1,0:T(8,128)(2,1)S(1)} %copy-done.3, ...), custom_call_target="tpu_custom_call" | custom-call | flops 1000000000 | bytes 4521984 | tf_op jit(solution)/shard_map/ahead/pallas_call | solution.py:273
  49.3 2.5 %collective-permute-start = (f32[128,128]{1,0:T(8,128)S(1)}, f32[128,128]{1,0:T(8,128)S(1)}, u32[]{:S(2)}, u32[]{:S(2)}) collective-permute-start(f32[128,128]{1,0:T(8,128)S(1)} %get-tuple-element.7.own_ref), channel_id=1, source_target_pairs={{0,4},{4,0},{1,5},{5,1},{2,6},{6,2},{3,7},{7,3},{8,12},{12,8},{9,1... | collective-permute-start | bytes 196616 | tf_op jit(solution)/shard_map/ppermute | solution.py:319
  51.8 2.1 %behind.1._ = f32[2560,128]{1,0:T(8,128)S(1)} custom-call(f32[2176,128]{1,0:T(8,128)S(1)} %bitcast.8, f32[1024,256]{1,0:T(8,128)S(1)} %get-tuple-element.8.gated_ref, f32[1024,256]{1,0:T(8,128)S(1)} %get-tuple-element.9.grad_ref, bf16[256,384]{1,0:T(8,128)(2,1)S(1)} %copy-done.5, bf16[256,256]{1,0:T(8,128)(2,1)S(1)} %copy-done.7, ...), custom_call_target="tpu_custom_call" | custom-call | flops 1000000000 | bytes 5767168 | tf_op jit(solution)/shard_map/behind/pallas_call | solution.py:273
  53.9 0.1 collective-permute-done.other_ref
  54.0 0.0 copy-start
  54.0 0.0 copy-start.1
  54.0 0.0 copy-start.2
  54.1 43.0 %all_to_all.11 = f32[128,5,4,128]{3,2,1,0:T(4,128)S(1)} all-to-all(f32[128,5,4,128]{3,2,1,0:T(4,128)S(1)} %bitcast.5), channel_id=1, replica_groups=mesh['seq'=32,'far'=2,'near'=4] {'near','seq'}, dimensions={0} | all-to-all | bytes 2621440 | tf_op jit(solution)/shard_map/all_to_all | solution.py:288
  97.1 0.0 copy-done
  97.1 0.0 copy-done.1
  97.1 0.0 copy-done.2
  97.1 1.5 %unpack.1 = (f32[512,256]{1,0:T(8,128)}, f32[512,256]{1,0:T(8,128)}, f32[512,256]{1,0:T(8,128)}, f32[512,128]{1,0:T(8,128)}) custom-call(f32[2560,128]{1,0:T(8,128)S(1)} %bitcast.6, f32[512,256]{1,0:T(8,128)S(1)} %copy-done.2, f32[512,256]{1,0:T(8,128)S(1)} %copy-done.1, f32[512,256]{1,0:T(8,128)S(1)} %copy-done), custom_call_target="tpu_custom_call" | custom-call | bytes 4718592 | tf_op jit(solution)/shard_map/unpack/pallas_call | solution.py:273
  (1 shorter events, 0.0 us)
Async XLA Ops:
  2.7 44.4 %copy-start.3 = (bf16[768,256]{1,0:T(8,128)(2,1)S(1)}, bf16[768,256]{1,0:T(8,128)(2,1)}, u32[]{:S(2)}) copy-start(bf16[768,256]{1,0:T(8,128)(2,1)} %constant.17.clone.behind_ref) | copy-start | bytes 1179652
  2.7 44.4 %copy-start.4 = (bf16[768,256]{1,0:T(8,128)(2,1)S(1)}, bf16[768,256]{1,0:T(8,128)(2,1)}, u32[]{:S(2)}) copy-start(bf16[768,256]{1,0:T(8,128)(2,1)} %constant.16.clone.ahead_ref) | copy-start | bytes 1179652
  2.7 44.4 %copy-start.5 = (bf16[256,384]{1,0:T(8,128)(2,1)S(1)}, bf16[256,384]{1,0:T(8,128)(2,1)}, u32[]{:S(2)}) copy-start(bf16[256,384]{1,0:T(8,128)(2,1)} %constant.14.clone.into_ref) | copy-start | bytes 589828
  2.8 44.4 %copy-start.6 = (f32[128,256]{1,0:T(8,128)S(1)}, f32[128,256]{1,0:T(8,128)}, u32[]{:S(2)}) copy-start(f32[128,256]{1,0:T(8,128)} %constant.18.clone.twist_ref) | copy-start | bytes 393220
  2.8 44.4 %copy-start.7 = (bf16[256,256]{1,0:T(8,128)(2,1)S(1)}, bf16[256,256]{1,0:T(8,128)(2,1)}, u32[]{:S(2)}) copy-start(bf16[256,256]{1,0:T(8,128)(2,1)} %constant.15.clone.back_ref) | copy-start | bytes 393220
  49.3 4.7 %collective-permute-start = (f32[128,128]{1,0:T(8,128)S(1)}, f32[128,128]{1,0:T(8,128)S(1)}, u32[]{:S(2)}, u32[]{:S(2)}) collective-permute-start(f32[128,128]{1,0:T(8,128)S(1)} %get-tuple-element.7.own_ref), channel_id=1, source_target_pairs={{0,4},{4,0},{1,5},{5,1},{2,6},{6,2},{3,7},{7,3},{8,12},{12,8},{9,1... | collective-permute-start | bytes 196616 | tf_op jit(solution)/shard_map/ppermute | solution.py:319
  54.0 43.1 %copy-start = (f32[512,256]{1,0:T(8,128)S(1)}, f32[512,256]{1,0:T(8,128)}, u32[]{:S(2)}) copy-start(f32[512,256]{1,0:T(8,128)} %k_ref.1) | copy-start | bytes 1572868
  54.0 43.1 %copy-start.1 = (f32[512,256]{1,0:T(8,128)S(1)}, f32[512,256]{1,0:T(8,128)}, u32[]{:S(2)}) copy-start(f32[512,256]{1,0:T(8,128)} %v_ref.1) | copy-start | bytes 1572868
  54.0 43.0 %copy-start.2 = (f32[512,256]{1,0:T(8,128)S(1)}, f32[512,256]{1,0:T(8,128)}, u32[]{:S(2)}) copy-start(f32[512,256]{1,0:T(8,128)} %g_ref.1) | copy-start | bytes 1572868

commit v6 on v5

--- a/solution.py
+++ b/solution.py
@@ -127,7 +127,7 @@
 
 
 def pack_kernel(
-    members, near_ref, k_hbm, v_hbm, g_hbm, q_hbm, f_hbm, out_ref,
+    members, place_ref, k_hbm, v_hbm, g_hbm, q_hbm, f_hbm, own_ref, other_ref,
     k_ref, v_ref, g_ref, q_ref, f_ref, sems,
 ):
     copies = []
@@ -139,9 +139,19 @@
             copy.start()
             copies.append(copy)
         if q == 0:
-            start = pl.multiple_of(near_ref[0] * SIDE, SIDE)
-            own = pltpu.make_async_copy(f_hbm.at[pl.ds(start, SIDE)], f_ref, sems.at[16])
-            own.start()
+            start = pl.multiple_of(place_ref[0] * SIDE, SIDE)
+            part = pltpu.make_async_copy(f_hbm.at[pl.ds(start, SIDE)], f_ref, sems.at[16])
+            part.start()
+    core = place_ref[1]
+    first = core == 0
+
+    def put(slab, at):
+        lower, upper = slab[:members], slab[members:]
+        own_ref[pl.ds(core * IN_ROWS + at, members, stride=2 * IN_ROWS), :] = jnp.where(
+            first, lower, upper
+        )
+        other_ref[pl.ds(at, members, stride=IN_ROWS), :] = jnp.where(first, upper, lower)
+
     for q in range(QUARTERS):
         rows = slice(q * SIDE, (q + 1) * SIDE)
         for array, (left, right) in enumerate(((k_ref, v_ref), (g_ref, q_ref))):
@@ -149,13 +159,18 @@
             copies[q * 4 + array * 2 + 1].wait()
             for h in range(HALVES):
                 cols = slice(h * SIDE, (h + 1) * SIDE)
-                at = array * 8 + h * QUARTERS + q
-                out_ref[pl.ds(at, members, stride=IN_ROWS), :] = (
-                    left[rows, cols] * right[rows, cols]
-                ).T
+                put((left[rows, cols] * right[rows, cols]).T, array * 8 + h * QUARTERS + q)
         if q == 0:
-            own.wait()
-            out_ref[pl.ds(16, members, stride=IN_ROWS), :] = f_ref[...].T
+            part.wait()
+            put(f_ref[...].T, 16)
+
+
+def merge_kernel(members, place_ref, other_ref, _, out_ref):
+    start = (1 - place_ref[1]) * IN_ROWS
+    for at in range(IN_ROWS):
+        out_ref[pl.ds(start + at, members, stride=2 * IN_ROWS), :] = other_ref[
+            pl.ds(at, members, stride=IN_ROWS), :
+        ]
 
 
 def ahead_kernel(
@@ -239,18 +254,24 @@
     members, in_ref, g_ref, v_ref, k_ref, gq_hbm, gk_hbm, gv_hbm, gf_hbm,
     gq_ref, gk_ref, gv_ref, gf_ref, sems,
 ):
+    def get(at):
+        parts = [
+            in_ref[pl.ds(core * OUT_ROWS + at, members, stride=2 * OUT_ROWS), :]
+            for core in range(2)
+        ]
+        return jnp.concatenate(parts, axis=0).T
+
     copies = []
     for q in range(QUARTERS):
         rows = slice(q * SIDE, (q + 1) * SIDE)
         for h in range(HALVES):
             cols = slice(h * SIDE, (h + 1) * SIDE)
             at = h * QUARTERS + q
-            conv = in_ref[pl.ds(at, members, stride=OUT_ROWS), :].T
-            gq_ref[rows, cols] = conv * g_ref[rows, cols]
-            back = in_ref[pl.ds(8 + at, members, stride=OUT_ROWS), :].T
+            gq_ref[rows, cols] = get(at) * g_ref[rows, cols]
+            back = get(8 + at)
             gk_ref[rows, cols] = back * v_ref[rows, cols]
             gv_ref[rows, cols] = back * k_ref[rows, cols]
-        gf_ref[rows, :] = in_ref[pl.ds(16 + q, members, stride=OUT_ROWS), :].T
+        gf_ref[rows, :] = get(16 + q)
         pairs = ((gq_ref, gq_hbm), (gk_ref, gk_hbm), (gv_ref, gv_hbm), (gf_ref, gf_hbm))
         for at, (source, target) in enumerate(pairs):
             part = pl.ds(q * SIDE, SIDE)
@@ -283,14 +304,14 @@
     )(*args)
 
 
-def exchange(block, inner):
+def exchange(block, inner, axes):
     parted = block.reshape(block.shape[0] // int(np.prod(inner)), *inner, SIDE)
-    return lax.all_to_all(parted, ("near", "seq"), 0, 0, tiled=True).reshape(block.shape)
+    return lax.all_to_all(parted, axes, 0, 0, tiled=True).reshape(block.shape)
 
 
 def local(q_gate, k_gate, values, filter_raw, grad_out):
-    shards = lax.axis_size("seq")
-    members = shards * lax.axis_size("near")
+    members = lax.axis_size("line") * lax.axis_size("near")
+    shards = lax.axis_size("line") * lax.axis_size("core")
     total = SIDE * SIDE
     into, back, ahead, behind, twist = (
         jnp.asarray(t) for t in tables(shards, total ** (-0.5) / total)
@@ -298,16 +319,26 @@
     block = q_gate.shape
     wide = pltpu.VMEM(block, F32)
     split = [pltpu.VMEM((17 * SIDE, 2 * SIDE), BF)] * 2
-    near = lax.axis_index("near").astype(jnp.int32).reshape(1)
-    packed = call(
+    place = jnp.stack([lax.axis_index("near"), lax.axis_index("core")]).astype(jnp.int32)
+    swap = [(0, 1), (1, 0)]
+    inputs = (k_gate, values, grad_out, q_gate, filter_raw)
+    packed, other = call(
         functools.partial(pack_kernel, members),
-        [(IN_ROWS * members, SIDE)],
-        (near, *(pltpu.with_memory_space_constraint(a, pltpu.HBM) for a in (k_gate, values, grad_out, q_gate, filter_raw))),
+        [(2 * IN_ROWS * members, SIDE), (IN_ROWS * members, SIDE)],
+        (place, *(pltpu.with_memory_space_constraint(a, pltpu.HBM) for a in inputs)),
         "pack",
         ins=[SMEM] + [HBM] * 5,
         scratch=[wide] * 4 + [pltpu.VMEM((SIDE, SIDE), F32), pltpu.SemaphoreType.DMA((17,))],
+    )
+    packed = call(
+        functools.partial(merge_kernel, members),
+        [(2 * IN_ROWS * members, SIDE)],
+        (place, lax.ppermute(other, "core", swap), packed),
+        "merge",
+        ins=[SMEM, VMEM, VMEM],
+        aliases={2: 0},
     )[0]
-    spread = exchange(packed, (17, 1))
+    spread = exchange(packed, (17, 2), ("near", "line"))
     corr, gated_spec, grad_spec = call(
         functools.partial(ahead_kernel, shards),
         [(SIDE, SIDE), (8 * SIDE, 2 * SIDE), (8 * SIDE, 2 * SIDE)],
@@ -316,10 +347,10 @@
         scratch=split,
         flops=10**9,
     )
-    other = lax.ppermute(corr, "far", [(0, 1), (1, 0)])
+    other = lax.ppermute(corr, "far", swap)
     results = call(
         functools.partial(behind_kernel, shards),
-        [(OUT_ROWS * members, SIDE)],
+        [(2 * OUT_ROWS * members, SIDE)],
         (spread, gated_spec, grad_spec, into, back, ahead, behind, twist),
         "behind",
         scratch=split,
@@ -327,13 +358,13 @@
     )[0]
     results = call(
         functools.partial(sum_kernel, shards),
-        [(OUT_ROWS * members, SIDE)],
+        [(2 * OUT_ROWS * members, SIDE)],
         (corr, other, results),
         "sum",
         ins=[VMEM] * 3,
         aliases={2: 0},
     )[0]
-    placed = exchange(results, (5, 4))
+    placed = exchange(results, (5, 4), ("near", "line", "core"))
     grad_q, grad_k, grad_v, grad_filter = call(
         functools.partial(unpack_kernel, members),
         [block, block, block, filter_raw.shape],
@@ -348,9 +379,10 @@
 def solution(mesh):
     shards, groups = mesh.devices.shape
     parted = Mesh(
-        mesh.devices.reshape(shards, groups // BLOCKS, BLOCKS), ("seq", "far", "near")
-    )
-    whole, filters = P("seq", ("far", "near")), P("seq", None)
+        mesh.devices.reshape(shards // 2, 2, groups // BLOCKS, BLOCKS),
+        ("line", "core", "far", "near"),
+    )
+    whole, filters = P(("line", "core"), ("far", "near")), P(("line", "core"), None)
     return jax.shard_map(
         local,
         mesh=parted,

time: 99.6 us -> 102 us (1.024)
  blocking collectives: 87.4 us -> 83.3 us
  starting transfers between devices: 2.53 us -> 5.83 us
  waiting for transfers between devices: 0.1 us -> 1.67 us
  Pallas kernels: 7.78 us -> 8.9 us
    all_to_all x2, blocking collectives: 87.4 us -> 83.3 us  [exchange(): return lax.all_to_all(parted, axes, 0, 0, tiled=True).reshape(block.shape)]
    ppermute x1 -> x2, starting transfers between devices: 2.53 us -> 5.83 us  [the longest x1 3.29 us: local(): lax.ppermute(other, 'core', swap)]
    ppermute x1 -> x2, waiting for transfers between devices: 0.1 us -> 1.67 us  [the longest x1 1.58 us: local(): lax.ppermute(other, 'core', swap)]
    pallas_call x5 -> x6, Pallas kernels: 7.78 us -> 8.9 us  [call(): pl.pallas_call(kernel, out_shape=[jax.ShapeDtypeStruct(shape, F32) for sh...]
  transfers between devices with their start and end apart: 1 -> 2, of which waited for: 1 -> 2; matrix products, arithmetic and copies ran while one was open for 0% -> 0% of each run, Pallas kernels for 2% -> 2%
where the time goes in v6:
time: 102 us; the launch traced here: 101 us
  blocking collectives  83.3 us (82%)
  Pallas kernels  8.9 us (9%)
  starting transfers between devices  5.83 us (6%)
  waiting for transfers between devices  1.67 us (2%)
    all_to_all x2, blocking collectives, exchange(): return lax.all_to_all(parted, axes, 0, 0, tiled=True).reshape(block.shape)  83.3 us
    pallas_call x6, Pallas kernels, call(): pl.pallas_call(kernel, out_shape=[jax.ShapeDtypeStruct(shape, F32) for sh...  8.9 us
    ppermute x1, starting transfers between devices, local(): lax.ppermute(other, 'core', swap)  3.29 us
    ppermute x1, starting transfers between devices, local(): other = lax.ppermute(corr, 'far', swap)  2.54 us
  transfers between devices with their start and end apart: 2, of which 2 were waited for; matrix products, arithmetic and copies ran while one was open for 0% of the time, Pallas kernels for 2%

profile of v6, /device:TPU:1, one launch (start us, length us, event | category | flops | bytes accessed | tf_op | source)
XLA Modules:
  0.0 100.6 jit_solution(16118883180089850067)
XLA Ops:
  0.6 0.1 pad_add_fusion.place_ref
  0.7 2.6 %pack.1 = (f32[2176,128]{1,0:T(8,128)S(1)}, f32[1088,128]{1,0:T(8,128)S(1)}) custom-call(s32[2]{0:T(128)S(1)} %pad_add_fusion.place_ref, f32[512,256]{1,0:T(8,128)} %k_ref.1, f32[512,256]{1,0:T(8,128)} %v_ref.1, f32[512,256]{1,0:T(8,128)} %g_ref.1, f32[512,256]{1,0:T(8,128)} %q_hbm.1, f32[512,128]{1,0:T(8,128)} %f_hbm.1), custom_call_target="tpu_custom_call" | custom-call | bytes 4030472 | tf_op jit(solution)/shard_map/pack/pallas_call | solution.py:294
  3.3 3.3 %collective-permute-start = (f32[1088,128]{1,0:T(8,128)S(1)}, f32[1088,128]{1,0:T(8,128)S(1)}, u32[]{:S(2)}, u32[]{:S(2)}) collective-permute-start(f32[1088,128]{1,0:T(8,128)S(1)} %get-tuple-element.9), channel_id=1, source_target_pairs={{0,8},{8,0},{1,9},{9,1},{2,10},{10,2},{3,11},{11,3},{4,12},{12,4},... | collective-permute-start | bytes 1671176 | tf_op jit(solution)/shard_map/ppermute | solution.py:336
  6.6 1.6 %collective-permute-done.other_ref = f32[1088,128]{1,0:T(8,128)S(1)} collective-permute-done((f32[1088,128]{1,0:T(8,128)S(1)}, f32[1088,128]{1,0:T(8,128)S(1)}, u32[]{:S(2)}, u32[]{:S(2)}) %collective-permute-start) | collective-permute-done | bytes 557088 | tf_op jit(solution)/shard_map/ppermute | solution.py:336
  8.2 0.6 merge.1
  8.8 0.0 copy-start.3
  8.8 0.0 copy-start.4
  8.8 0.0 copy-start.5
  8.8 0.0 copy-start.6
  8.9 0.0 copy-start.7
  8.9 39.9 %all_to_all.10 = f32[64,17,2,128]{3,2,1,0:T(2,128)S(1)} all-to-all(f32[64,17,2,128]{3,2,1,0:T(2,128)S(1)} %bitcast.10), channel_id=1, replica_groups=mesh['line'=16,'core'=2,'far'=2,'near'=4] {'near','line'}, dimensions={0} | all-to-all | bytes 2228224 | tf_op jit(solution)/shard_map/all_to_all | solution.py:309
  48.8 0.0 copy-done.3
  48.8 0.0 copy-done.4
  48.8 0.0 copy-done.5
  48.8 0.0 copy-done.6
  48.8 0.0 copy-done.7
  48.8 2.1 %ahead.1 = (f32[128,128]{1,0:T(8,128)S(1)}, f32[1024,256]{1,0:T(8,128)S(1)}, f32[1024,256]{1,0:T(8,128)S(1)}) custom-call(f32[2176,128]{1,0:T(8,128)S(1)} %bitcast.8, bf16[256,384]{1,0:T(8,128)(2,1)S(1)} %copy-done.5, bf16[256,256]{1,0:T(8,128)(2,1)S(1)} %copy-done.7, bf16[768,256]{1,0:T(8,128)(2,1)S(1)} %copy-done.4, bf16[768,256]{1,0:T(8,128)(2,1)S(1)} %copy-done.3, ...), custom_call_target="tpu_custom_call" | custom-call | flops 1000000000 | bytes 4521984 | tf_op jit(solution)/shard_map/ahead/pallas_call | solution.py:294
  50.9 2.5 %collective-permute-start.1 = (f32[128,128]{1,0:T(8,128)S(1)}, f32[128,128]{1,0:T(8,128)S(1)}, u32[]{:S(2)}, u32[]{:S(2)}) collective-permute-start(f32[128,128]{1,0:T(8,128)S(1)} %get-tuple-element.11.own_ref), channel_id=1, source_target_pairs={{0,4},{4,0},{1,5},{5,1},{2,6},{6,2},{3,7},{7,3},{8,12},{12,8},{9,1... | collective-permute-start | bytes 196616 | tf_op jit(solution)/shard_map/ppermute | solution.py:350
  53.4 2.1 %behind.1._ = f32[2560,128]{1,0:T(8,128)S(1)} custom-call(f32[2176,128]{1,0:T(8,128)S(1)} %bitcast.9, f32[1024,256]{1,0:T(8,128)S(1)} %get-tuple-element.12.gated_ref, f32[1024,256]{1,0:T(8,128)S(1)} %get-tuple-element.13.grad_ref, bf16[256,384]{1,0:T(8,128)(2,1)S(1)} %copy-done.5, bf16[256,256]{1,0:T(8,128)(2,1)S(1)} %copy-done.7, ...), custom_call_target="tpu_custom_call" | custom-call | flops 1000000000 | bytes 5767168 | tf_op jit(solution)/shard_map/behind/pallas_call | solution.py:294
  55.5 0.1 collective-permute-done.1.other_ref
  55.6 0.0 copy-start
  55.7 0.0 copy-start.1
  55.7 0.0 copy-start.2
  55.7 43.4 %all_to_all.11 = f32[128,5,4,128]{3,2,1,0:T(4,128)S(1)} all-to-all(f32[128,5,4,128]{3,2,1,0:T(4,128)S(1)} %bitcast.6), channel_id=1, replica_groups=mesh['line'=16,'core'=2,'far'=2,'near'=4] {'near','line','core'}, dimensions={0} | all-to-all | bytes 2621440 | tf_op jit(solution)/shard_map/all_to_all | solution.py:309
  99.1 0.0 copy-done
  99.1 0.0 copy-done.1
  99.1 0.0 copy-done.2
  99.1 1.5 %unpack.1 = (f32[512,256]{1,0:T(8,128)}, f32[512,256]{1,0:T(8,128)}, f32[512,256]{1,0:T(8,128)}, f32[512,128]{1,0:T(8,128)}) custom-call(f32[2560,128]{1,0:T(8,128)S(1)} %bitcast.7, f32[512,256]{1,0:T(8,128)S(1)} %copy-done.2, f32[512,256]{1,0:T(8,128)S(1)} %copy-done.1, f32[512,256]{1,0:T(8,128)S(1)} %copy-done), custom_call_target="tpu_custom_call" | custom-call | bytes 4718592 | tf_op jit(solution)/shard_map/unpack/pallas_call | solution.py:294
  (1 shorter events, 0.0 us)
Async XLA Ops:
  3.3 4.9 %collective-permute-start = (f32[1088,128]{1,0:T(8,128)S(1)}, f32[1088,128]{1,0:T(8,128)S(1)}, u32[]{:S(2)}, u32[]{:S(2)}) collective-permute-start(f32[1088,128]{1,0:T(8,128)S(1)} %get-tuple-element.9), channel_id=1, source_target_pairs={{0,8},{8,0},{1,9},{9,1},{2,10},{10,2},{3,11},{11,3},{4,12},{12,4},... | collective-permute-start | bytes 1671176 | tf_op jit(solution)/shard_map/ppermute | solution.py:336
  8.8 40.0 %copy-start.3 = (bf16[768,256]{1,0:T(8,128)(2,1)S(1)}, bf16[768,256]{1,0:T(8,128)(2,1)}, u32[]{:S(2)}) copy-start(bf16[768,256]{1,0:T(8,128)(2,1)} %constant.22.clone.behind_ref) | copy-start | bytes 1179652
  8.8 39.9 %copy-start.4 = (bf16[768,256]{1,0:T(8,128)(2,1)S(1)}, bf16[768,256]{1,0:T(8,128)(2,1)}, u32[]{:S(2)}) copy-start(bf16[768,256]{1,0:T(8,128)(2,1)} %constant.21.clone.ahead_ref) | copy-start | bytes 1179652
  8.8 39.9 %copy-start.5 = (bf16[256,384]{1,0:T(8,128)(2,1)S(1)}, bf16[256,384]{1,0:T(8,128)(2,1)}, u32[]{:S(2)}) copy-start(bf16[256,384]{1,0:T(8,128)(2,1)} %constant.19.clone.into_ref) | copy-start | bytes 589828
  8.8 39.9 %copy-start.6 = (f32[128,256]{1,0:T(8,128)S(1)}, f32[128,256]{1,0:T(8,128)}, u32[]{:S(2)}) copy-start(f32[128,256]{1,0:T(8,128)} %constant.23.clone.twist_ref) | copy-start | bytes 393220
  8.9 39.9 %copy-start.7 = (bf16[256,256]{1,0:T(8,128)(2,1)S(1)}, bf16[256,256]{1,0:T(8,128)(2,1)}, u32[]{:S(2)}) copy-start(bf16[256,256]{1,0:T(8,128)(2,1)} %constant.20.clone.back_ref) | copy-start | bytes 393220
  50.9 4.7 %collective-permute-start.1 = (f32[128,128]{1,0:T(8,128)S(1)}, f32[128,128]{1,0:T(8,128)S(1)}, u32[]{:S(2)}, u32[]{:S(2)}) collective-permute-start(f32[128,128]{1,0:T(8,128)S(1)} %get-tuple-element.11.own_ref), channel_id=1, source_target_pairs={{0,4},{4,0},{1,5},{5,1},{2,6},{6,2},{3,7},{7,3},{8,12},{12,8},{9,1... | collective-permute-start | bytes 196616 | tf_op jit(solution)/shard_map/ppermute | solution.py:350
  55.6 43.4 %copy-start = (f32[512,256]{1,0:T(8,128)S(1)}, f32[512,256]{1,0:T(8,128)}, u32[]{:S(2)}) copy-start(f32[512,256]{1,0:T(8,128)} %k_ref.1) | copy-start | bytes 1572868
  55.7 43.4 %copy-start.1 = (f32[512,256]{1,0:T(8,128)S(1)}, f32[512,256]{1,0:T(8,128)}, u32[]{:S(2)}) copy-start(f32[512,256]{1,0:T(8,128)} %v_ref.1) | copy-start | bytes 1572868
  55.7 43.4 %copy-start.2 = (f32[512,256]{1,0:T(8,128)S(1)}, f32[512,256]{1,0:T(8,128)}, u32[]{:S(2)}) copy-start(f32[512,256]{1,0:T(8,128)} %g_ref.1) | copy-start | bytes 1572868

commit v7 on v5

--- a/solution.py
+++ b/solution.py
@@ -131,29 +131,30 @@
     k_ref, v_ref, g_ref, q_ref, f_ref, sems,
 ):
     copies = []
-    for q in range(QUARTERS):
-        rows = pl.ds(q * SIDE, SIDE)
+    for part in range(2):
+        rows = pl.ds(part * 2 * SIDE, 2 * SIDE)
         pairs = ((k_hbm, k_ref), (v_hbm, v_ref), (g_hbm, g_ref), (q_hbm, q_ref))
         for at, (source, target) in enumerate(pairs):
-            copy = pltpu.make_async_copy(source.at[rows], target.at[rows], sems.at[q * 4 + at])
+            copy = pltpu.make_async_copy(source.at[rows], target.at[rows], sems.at[part * 4 + at])
             copy.start()
             copies.append(copy)
-        if q == 0:
+        if part == 0:
             start = pl.multiple_of(near_ref[0] * SIDE, SIDE)
             own = pltpu.make_async_copy(f_hbm.at[pl.ds(start, SIDE)], f_ref, sems.at[16])
             own.start()
-    for q in range(QUARTERS):
-        rows = slice(q * SIDE, (q + 1) * SIDE)
+    for part in range(2):
         for array, (left, right) in enumerate(((k_ref, v_ref), (g_ref, q_ref))):
-            copies[q * 4 + array * 2].wait()
-            copies[q * 4 + array * 2 + 1].wait()
-            for h in range(HALVES):
-                cols = slice(h * SIDE, (h + 1) * SIDE)
-                at = array * 8 + h * QUARTERS + q
-                out_ref[pl.ds(at, members, stride=IN_ROWS), :] = (
-                    left[rows, cols] * right[rows, cols]
-                ).T
-        if q == 0:
+            copies[part * 4 + array * 2].wait()
+            copies[part * 4 + array * 2 + 1].wait()
+            for q in (2 * part, 2 * part + 1):
+                rows = slice(q * SIDE, (q + 1) * SIDE)
+                for h in range(HALVES):
+                    cols = slice(h * SIDE, (h + 1) * SIDE)
+                    at = array * 8 + h * QUARTERS + q
+                    out_ref[pl.ds(at, members, stride=IN_ROWS), :] = (
+                        left[rows, cols] * right[rows, cols]
+                    ).T
+        if part == 0:
             own.wait()
             out_ref[pl.ds(16, members, stride=IN_ROWS), :] = f_ref[...].T
 
@@ -240,23 +241,29 @@
     gq_ref, gk_ref, gv_ref, gf_ref, sems,
 ):
     copies = []
+
+    def send(source, target, q):
+        part = pl.ds(q * SIDE, SIDE)
+        copy = pltpu.make_async_copy(source.at[part], target.at[part], sems.at[len(copies)])
+        copy.start()
+        copies.append(copy)
+
     for q in range(QUARTERS):
         rows = slice(q * SIDE, (q + 1) * SIDE)
         for h in range(HALVES):
             cols = slice(h * SIDE, (h + 1) * SIDE)
-            at = h * QUARTERS + q
-            conv = in_ref[pl.ds(at, members, stride=OUT_ROWS), :].T
-            gq_ref[rows, cols] = conv * g_ref[rows, cols]
-            back = in_ref[pl.ds(8 + at, members, stride=OUT_ROWS), :].T
+            back = in_ref[pl.ds(8 + h * QUARTERS + q, members, stride=OUT_ROWS), :].T
             gk_ref[rows, cols] = back * v_ref[rows, cols]
             gv_ref[rows, cols] = back * k_ref[rows, cols]
+        send(gk_ref, gk_hbm, q)
+        send(gv_ref, gv_hbm, q)
+        for h in range(HALVES):
+            cols = slice(h * SIDE, (h + 1) * SIDE)
+            conv = in_ref[pl.ds(h * QUARTERS + q, members, stride=OUT_ROWS), :].T
+            gq_ref[rows, cols] = conv * g_ref[rows, cols]
+        send(gq_ref, gq_hbm, q)
         gf_ref[rows, :] = in_ref[pl.ds(16 + q, members, stride=OUT_ROWS), :].T
-        pairs = ((gq_ref, gq_hbm), (gk_ref, gk_hbm), (gv_ref, gv_hbm), (gf_ref, gf_hbm))
-        for at, (source, target) in enumerate(pairs):
-            part = pl.ds(q * SIDE, SIDE)
-            copy = pltpu.make_async_copy(source.at[part], target.at[part], sems.at[q * 4 + at])
-            copy.start()
-            copies.append(copy)
+        send(gf_ref, gf_hbm, q)
     for copy in copies:
         copy.wait()
 

time: 99.6 us -> 99.3 us (level)
  no operation moved by 1% of the time
where the time goes in v7:
time: 99.3 us; the launch traced here: 98.3 us
  blocking collectives  87.4 us (88%)
  Pallas kernels  7.51 us (8%)
  starting transfers between devices  2.54 us (3%)
    all_to_all x2, blocking collectives, exchange(): lax.all_to_all(parted, ('near', 'seq'), 0, 0, tiled=True)  87.4 us
    pallas_call x5, Pallas kernels, call(): pl.pallas_call(kernel, out_shape=[jax.ShapeDtypeStruct(shape, F32) for sh...  7.51 us
    ppermute x1, starting transfers between devices, local(): other = lax.ppermute(corr, 'far', [(0, 1), (1, 0)])  2.54 us
  transfers between devices with their start and end apart: 1, of which 1 were waited for; matrix products, arithmetic and copies ran while one was open for 0% of the time, Pallas kernels for 2%

profile of v7, /device:TPU:1, one launch (start us, length us, event | category | flops | bytes accessed | tf_op | source)
XLA Modules:
  0.0 98.3 jit_solution(3229744214127984764)
XLA Ops:
  0.6 1.9 %pack.1 = f32[2176,128]{1,0:T(8,128)S(1)} custom-call(s32[1]{0:T(128)} %bitcast.near_ref, f32[512,256]{1,0:T(8,128)} %k_ref.1, f32[512,256]{1,0:T(8,128)} %v_ref.1, f32[512,256]{1,0:T(8,128)} %g_ref.1, f32[512,256]{1,0:T(8,128)} %q_hbm.1, f32[512,128]{1,0:T(8,128)} %f_hbm.1), custom_call_target="tpu_custom_call" | custom-call | bytes 3473412 | tf_op jit(solution)/shard_map/pack/pallas_call | solution.py:280
  2.5 0.0 copy-start.3
  2.5 0.0 copy-start.4
  2.5 0.0 copy-start.5
  2.5 0.0 copy-start.6
  2.5 0.0 copy-start.7
  2.6 44.3 %all_to_all.10 = f32[128,17,1,128]{3,2,1,0:T(1,128)S(1)} all-to-all(f32[128,17,1,128]{3,2,1,0:T(1,128)S(1)} %bitcast.9), channel_id=1, replica_groups=mesh['seq'=32,'far'=2,'near'=4] {'near','seq'}, dimensions={0} | all-to-all | bytes 2228224 | tf_op jit(solution)/shard_map/all_to_all | solution.py:295
  46.9 0.0 copy-done.3
  46.9 0.0 copy-done.4
  46.9 0.0 copy-done.5
  46.9 0.0 copy-done.6
  46.9 0.0 copy-done.7
  46.9 2.1 %ahead.1 = (f32[128,128]{1,0:T(8,128)S(1)}, f32[1024,256]{1,0:T(8,128)S(1)}, f32[1024,256]{1,0:T(8,128)S(1)}) custom-call(f32[2176,128]{1,0:T(8,128)S(1)} %bitcast.7, bf16[256,384]{1,0:T(8,128)(2,1)S(1)} %copy-done.5, bf16[256,256]{1,0:T(8,128)(2,1)S(1)} %copy-done.7, bf16[768,256]{1,0:T(8,128)(2,1)S(1)} %copy-done.4, bf16[768,256]{1,0:T(8,128)(2,1)S(1)} %copy-done.3, ...), custom_call_target="tpu_custom_call" | custom-call | flops 1000000000 | bytes 4521984 | tf_op jit(solution)/shard_map/ahead/pallas_call | solution.py:280
  49.1 2.5 %collective-permute-start = (f32[128,128]{1,0:T(8,128)S(1)}, f32[128,128]{1,0:T(8,128)S(1)}, u32[]{:S(2)}, u32[]{:S(2)}) collective-permute-start(f32[128,128]{1,0:T(8,128)S(1)} %get-tuple-element.7.own_ref), channel_id=1, source_target_pairs={{0,4},{4,0},{1,5},{5,1},{2,6},{6,2},{3,7},{7,3},{8,12},{12,8},{9,1... | collective-permute-start | bytes 196616 | tf_op jit(solution)/shard_map/ppermute | solution.py:326
  51.6 2.1 %behind.1._ = f32[2560,128]{1,0:T(8,128)S(1)} custom-call(f32[2176,128]{1,0:T(8,128)S(1)} %bitcast.8, f32[1024,256]{1,0:T(8,128)S(1)} %get-tuple-element.8.gated_ref, f32[1024,256]{1,0:T(8,128)S(1)} %get-tuple-element.9.grad_ref, bf16[256,384]{1,0:T(8,128)(2,1)S(1)} %copy-done.5, bf16[256,256]{1,0:T(8,128)(2,1)S(1)} %copy-done.7, ...), custom_call_target="tpu_custom_call" | custom-call | flops 1000000000 | bytes 5767168 | tf_op jit(solution)/shard_map/behind/pallas_call | solution.py:280
  53.7 0.1 collective-permute-done.other_ref
  53.8 0.0 copy-start
  53.8 0.0 copy-start.1
  53.8 0.0 copy-start.2
  53.8 43.0 %all_to_all.11 = f32[128,5,4,128]{3,2,1,0:T(4,128)S(1)} all-to-all(f32[128,5,4,128]{3,2,1,0:T(4,128)S(1)} %bitcast.5), channel_id=1, replica_groups=mesh['seq'=32,'far'=2,'near'=4] {'near','seq'}, dimensions={0} | all-to-all | bytes 2621440 | tf_op jit(solution)/shard_map/all_to_all | solution.py:295
  96.9 0.0 copy-done
  96.9 0.0 copy-done.1
  96.9 0.0 copy-done.2
  96.9 1.5 %unpack.1 = (f32[512,256]{1,0:T(8,128)}, f32[512,256]{1,0:T(8,128)}, f32[512,256]{1,0:T(8,128)}, f32[512,128]{1,0:T(8,128)}) custom-call(f32[2560,128]{1,0:T(8,128)S(1)} %bitcast.6, f32[512,256]{1,0:T(8,128)S(1)} %copy-done.2, f32[512,256]{1,0:T(8,128)S(1)} %copy-done.1, f32[512,256]{1,0:T(8,128)S(1)} %copy-done), custom_call_target="tpu_custom_call" | custom-call | bytes 4718592 | tf_op jit(solution)/shard_map/unpack/pallas_call | solution.py:280
  (1 shorter events, 0.0 us)
Async XLA Ops:
  2.5 44.4 %copy-start.3 = (bf16[768,256]{1,0:T(8,128)(2,1)S(1)}, bf16[768,256]{1,0:T(8,128)(2,1)}, u32[]{:S(2)}) copy-start(bf16[768,256]{1,0:T(8,128)(2,1)} %constant.17.clone.behind_ref) | copy-start | bytes 1179652
  2.5 44.4 %copy-start.4 = (bf16[768,256]{1,0:T(8,128)(2,1)S(1)}, bf16[768,256]{1,0:T(8,128)(2,1)}, u32[]{:S(2)}) copy-start(bf16[768,256]{1,0:T(8,128)(2,1)} %constant.16.clone.ahead_ref) | copy-start | bytes 1179652
  2.5 44.4 %copy-start.5 = (bf16[256,384]{1,0:T(8,128)(2,1)S(1)}, bf16[256,384]{1,0:T(8,128)(2,1)}, u32[]{:S(2)}) copy-start(bf16[256,384]{1,0:T(8,128)(2,1)} %constant.14.clone.into_ref) | copy-start | bytes 589828
  2.5 44.4 %copy-start.6 = (f32[128,256]{1,0:T(8,128)S(1)}, f32[128,256]{1,0:T(8,128)}, u32[]{:S(2)}) copy-start(f32[128,256]{1,0:T(8,128)} %constant.18.clone.twist_ref) | copy-start | bytes 393220
  2.5 44.4 %copy-start.7 = (bf16[256,256]{1,0:T(8,128)(2,1)S(1)}, bf16[256,256]{1,0:T(8,128)(2,1)}, u32[]{:S(2)}) copy-start(bf16[256,256]{1,0:T(8,128)(2,1)} %constant.15.clone.back_ref) | copy-start | bytes 393220
  49.1 4.7 %collective-permute-start = (f32[128,128]{1,0:T(8,128)S(1)}, f32[128,128]{1,0:T(8,128)S(1)}, u32[]{:S(2)}, u32[]{:S(2)}) collective-permute-start(f32[128,128]{1,0:T(8,128)S(1)} %get-tuple-element.7.own_ref), channel_id=1, source_target_pairs={{0,4},{4,0},{1,5},{5,1},{2,6},{6,2},{3,7},{7,3},{8,12},{12,8},{9,1... | collective-permute-start | bytes 196616 | tf_op jit(solution)/shard_map/ppermute | solution.py:326
  53.8 43.1 %copy-start = (f32[512,256]{1,0:T(8,128)S(1)}, f32[512,256]{1,0:T(8,128)}, u32[]{:S(2)}) copy-start(f32[512,256]{1,0:T(8,128)} %k_ref.1) | copy-start | bytes 1572868
  53.8 43.1 %copy-start.1 = (f32[512,256]{1,0:T(8,128)S(1)}, f32[512,256]{1,0:T(8,128)}, u32[]{:S(2)}) copy-start(f32[512,256]{1,0:T(8,128)} %v_ref.1) | copy-start | bytes 1572868
  53.8 43.1 %copy-start.2 = (f32[512,256]{1,0:T(8,128)S(1)}, f32[512,256]{1,0:T(8,128)}, u32[]{:S(2)}) copy-start(f32[512,256]{1,0:T(8,128)} %g_ref.1) | copy-start | bytes 1572868

commit v8 on v7

--- a/solution.py
+++ b/solution.py
@@ -131,32 +131,37 @@
     k_ref, v_ref, g_ref, q_ref, f_ref, sems,
 ):
     copies = []
+    plan = ((k_hbm, k_ref, 0, 4), (v_hbm, v_ref, 0, 4))
+    plan += ((g_hbm, g_ref, 0, 2), (q_hbm, q_ref, 0, 2), (g_hbm, g_ref, 2, 2), (q_hbm, q_ref, 2, 2))
+    for at, (source, target, first, count) in enumerate(plan):
+        rows = pl.ds(first * SIDE, count * SIDE)
+        copy = pltpu.make_async_copy(source.at[rows], target.at[rows], sems.at[at])
+        copy.start()
+        copies.append(copy)
+        if at == 1:
+            start = pl.multiple_of(near_ref[0] * SIDE, SIDE)
+            own = pltpu.make_async_copy(f_hbm.at[pl.ds(start, SIDE)], f_ref, sems.at[6])
+            own.start()
+
+    def put(array, left, right, quarters):
+        for q in quarters:
+            rows = slice(q * SIDE, (q + 1) * SIDE)
+            for h in range(HALVES):
+                cols = slice(h * SIDE, (h + 1) * SIDE)
+                at = array * 8 + h * QUARTERS + q
+                out_ref[pl.ds(at, members, stride=IN_ROWS), :] = (
+                    left[rows, cols] * right[rows, cols]
+                ).T
+
+    copies[0].wait()
+    copies[1].wait()
+    put(0, k_ref, v_ref, range(QUARTERS))
+    own.wait()
+    out_ref[pl.ds(16, members, stride=IN_ROWS), :] = f_ref[...].T
     for part in range(2):
-        rows = pl.ds(part * 2 * SIDE, 2 * SIDE)
-        pairs = ((k_hbm, k_ref), (v_hbm, v_ref), (g_hbm, g_ref), (q_hbm, q_ref))
-        for at, (source, target) in enumerate(pairs):
-            copy = pltpu.make_async_copy(source.at[rows], target.at[rows], sems.at[part * 4 + at])
-            copy.start()
-            copies.append(copy)
-        if part == 0:
-            start = pl.multiple_of(near_ref[0] * SIDE, SIDE)
-            own = pltpu.make_async_copy(f_hbm.at[pl.ds(start, SIDE)], f_ref, sems.at[16])
-            own.start()
-    for part in range(2):
-        for array, (left, right) in enumerate(((k_ref, v_ref), (g_ref, q_ref))):
-            copies[part * 4 + array * 2].wait()
-            copies[part * 4 + array * 2 + 1].wait()
-            for q in (2 * part, 2 * part + 1):
-                rows = slice(q * SIDE, (q + 1) * SIDE)
-                for h in range(HALVES):
-                    cols = slice(h * SIDE, (h + 1) * SIDE)
-                    at = array * 8 + h * QUARTERS + q
-                    out_ref[pl.ds(at, members, stride=IN_ROWS), :] = (
-                        left[rows, cols] * right[rows, cols]
-                    ).T
-        if part == 0:
-            own.wait()
-            out_ref[pl.ds(16, members, stride=IN_ROWS), :] = f_ref[...].T
+        copies[2 + part * 2].wait()
+        copies[3 + part * 2].wait()
+        put(1, g_ref, q_ref, (2 * part, 2 * part + 1))
 
 
 def ahead_kernel(
@@ -312,7 +317,7 @@
         (near, *(pltpu.with_memory_space_constraint(a, pltpu.HBM) for a in (k_gate, values, grad_out, q_gate, filter_raw))),
         "pack",
         ins=[SMEM] + [HBM] * 5,
-        scratch=[wide] * 4 + [pltpu.VMEM((SIDE, SIDE), F32), pltpu.SemaphoreType.DMA((17,))],
+        scratch=[wide] * 4 + [pltpu.VMEM((SIDE, SIDE), F32), pltpu.SemaphoreType.DMA((7,))],
     )[0]
     spread = exchange(packed, (17, 1))
     corr, gated_spec, grad_spec = call(

time: 99.3 us -> 99.3 us (level)
  no operation moved by 1% of the time
where the time goes in v8:
time: 99.3 us; the launch traced here: 98.3 us
  blocking collectives  87.4 us (88%)
  Pallas kernels  7.51 us (8%)
  starting transfers between devices  2.54 us (3%)
    all_to_all x2, blocking collectives, exchange(): lax.all_to_all(parted, ('near', 'seq'), 0, 0, tiled=True)  87.4 us
    pallas_call x5, Pallas kernels, call(): pl.pallas_call(kernel, out_shape=[jax.ShapeDtypeStruct(shape, F32) for sh...  7.51 us
    ppermute x1, starting transfers between devices, local(): other = lax.ppermute(corr, 'far', [(0, 1), (1, 0)])  2.54 us
  transfers between devices with their start and end apart: 1, of which 1 were waited for; matrix products, arithmetic and copies ran while one was open for 0% of the time, Pallas kernels for 2%

profile of v8, /device:TPU:1, one launch (start us, length us, event | category | flops | bytes accessed | tf_op | source)
XLA Modules:
  0.0 98.3 jit_solution(16049247349647373350)
XLA Ops:
  0.6 1.8 %pack.1 = f32[2176,128]{1,0:T(8,128)S(1)} custom-call(s32[1]{0:T(128)} %bitcast.near_ref, f32[512,256]{1,0:T(8,128)} %k_ref.1, f32[512,256]{1,0:T(8,128)} %v_ref.1, f32[512,256]{1,0:T(8,128)} %g_ref.1, f32[512,256]{1,0:T(8,128)} %q_hbm.1, f32[512,128]{1,0:T(8,128)} %f_hbm.1), custom_call_target="tpu_custom_call" | custom-call | bytes 3473412 | tf_op jit(solution)/shard_map/pack/pallas_call | solution.py:285
  2.5 0.0 copy-start.3
  2.5 0.0 copy-start.4
  2.5 0.0 copy-start.5
  2.5 0.0 copy-start.6
  2.5 0.0 copy-start.7
  2.5 44.3 %all_to_all.10 = f32[128,17,1,128]{3,2,1,0:T(1,128)S(1)} all-to-all(f32[128,17,1,128]{3,2,1,0:T(1,128)S(1)} %bitcast.9), channel_id=1, replica_groups=mesh['seq'=32,'far'=2,'near'=4] {'near','seq'}, dimensions={0} | all-to-all | bytes 2228224 | tf_op jit(solution)/shard_map/all_to_all | solution.py:300
  46.9 0.0 copy-done.3
  46.9 0.0 copy-done.4
  46.9 0.0 copy-done.5
  46.9 0.0 copy-done.6
  46.9 0.0 copy-done.7
  46.9 2.1 %ahead.1 = (f32[128,128]{1,0:T(8,128)S(1)}, f32[1024,256]{1,0:T(8,128)S(1)}, f32[1024,256]{1,0:T(8,128)S(1)}) custom-call(f32[2176,128]{1,0:T(8,128)S(1)} %bitcast.7, bf16[256,384]{1,0:T(8,128)(2,1)S(1)} %copy-done.5, bf16[256,256]{1,0:T(8,128)(2,1)S(1)} %copy-done.7, bf16[768,256]{1,0:T(8,128)(2,1)S(1)} %copy-done.4, bf16[768,256]{1,0:T(8,128)(2,1)S(1)} %copy-done.3, ...), custom_call_target="tpu_custom_call" | custom-call | flops 1000000000 | bytes 4521984 | tf_op jit(solution)/shard_map/ahead/pallas_call | solution.py:285
  49.0 2.5 %collective-permute-start = (f32[128,128]{1,0:T(8,128)S(1)}, f32[128,128]{1,0:T(8,128)S(1)}, u32[]{:S(2)}, u32[]{:S(2)}) collective-permute-start(f32[128,128]{1,0:T(8,128)S(1)} %get-tuple-element.7.own_ref), channel_id=1, source_target_pairs={{0,4},{4,0},{1,5},{5,1},{2,6},{6,2},{3,7},{7,3},{8,12},{12,8},{9,1... | collective-permute-start | bytes 196616 | tf_op jit(solution)/shard_map/ppermute | solution.py:331
  51.6 2.1 %behind.1._ = f32[2560,128]{1,0:T(8,128)S(1)} custom-call(f32[2176,128]{1,0:T(8,128)S(1)} %bitcast.8, f32[1024,256]{1,0:T(8,128)S(1)} %get-tuple-element.8.gated_ref, f32[1024,256]{1,0:T(8,128)S(1)} %get-tuple-element.9.grad_ref, bf16[256,384]{1,0:T(8,128)(2,1)S(1)} %copy-done.5, bf16[256,256]{1,0:T(8,128)(2,1)S(1)} %copy-done.7, ...), custom_call_target="tpu_custom_call" | custom-call | flops 1000000000 | bytes 5767168 | tf_op jit(solution)/shard_map/behind/pallas_call | solution.py:285
  53.7 0.1 collective-permute-done.other_ref
  53.8 0.0 copy-start
  53.8 0.0 copy-start.1
  53.8 0.0 copy-start.2
  53.8 43.0 %all_to_all.11 = f32[128,5,4,128]{3,2,1,0:T(4,128)S(1)} all-to-all(f32[128,5,4,128]{3,2,1,0:T(4,128)S(1)} %bitcast.5), channel_id=1, replica_groups=mesh['seq'=32,'far'=2,'near'=4] {'near','seq'}, dimensions={0} | all-to-all | bytes 2621440 | tf_op jit(solution)/shard_map/all_to_all | solution.py:300
  96.9 0.0 copy-done
  96.9 0.0 copy-done.1
  96.9 0.0 copy-done.2
  96.9 1.5 %unpack.1 = (f32[512,256]{1,0:T(8,128)}, f32[512,256]{1,0:T(8,128)}, f32[512,256]{1,0:T(8,128)}, f32[512,128]{1,0:T(8,128)}) custom-call(f32[2560,128]{1,0:T(8,128)S(1)} %bitcast.6, f32[512,256]{1,0:T(8,128)S(1)} %copy-done.2, f32[512,256]{1,0:T(8,128)S(1)} %copy-done.1, f32[512,256]{1,0:T(8,128)S(1)} %copy-done), custom_call_target="tpu_custom_call" | custom-call | bytes 4718592 | tf_op jit(solution)/shard_map/unpack/pallas_call | solution.py:285
  (1 shorter events, 0.0 us)
Async XLA Ops:
  2.5 44.4 %copy-start.3 = (bf16[768,256]{1,0:T(8,128)(2,1)S(1)}, bf16[768,256]{1,0:T(8,128)(2,1)}, u32[]{:S(2)}) copy-start(bf16[768,256]{1,0:T(8,128)(2,1)} %constant.17.clone.behind_ref) | copy-start | bytes 1179652
  2.5 44.4 %copy-start.4 = (bf16[768,256]{1,0:T(8,128)(2,1)S(1)}, bf16[768,256]{1,0:T(8,128)(2,1)}, u32[]{:S(2)}) copy-start(bf16[768,256]{1,0:T(8,128)(2,1)} %constant.16.clone.ahead_ref) | copy-start | bytes 1179652
  2.5 44.4 %copy-start.5 = (bf16[256,384]{1,0:T(8,128)(2,1)S(1)}, bf16[256,384]{1,0:T(8,128)(2,1)}, u32[]{:S(2)}) copy-start(bf16[256,384]{1,0:T(8,128)(2,1)} %constant.14.clone.into_ref) | copy-start | bytes 589828
  2.5 44.4 %copy-start.6 = (f32[128,256]{1,0:T(8,128)S(1)}, f32[128,256]{1,0:T(8,128)}, u32[]{:S(2)}) copy-start(f32[128,256]{1,0:T(8,128)} %constant.18.clone.twist_ref) | copy-start | bytes 393220
  2.5 44.4 %copy-start.7 = (bf16[256,256]{1,0:T(8,128)(2,1)S(1)}, bf16[256,256]{1,0:T(8,128)(2,1)}, u32[]{:S(2)}) copy-start(bf16[256,256]{1,0:T(8,128)(2,1)} %constant.15.clone.back_ref) | copy-start | bytes 393220
  49.0 4.7 %collective-permute-start = (f32[128,128]{1,0:T(8,128)S(1)}, f32[128,128]{1,0:T(8,128)S(1)}, u32[]{:S(2)}, u32[]{:S(2)}) collective-permute-start(f32[128,128]{1,0:T(8,128)S(1)} %get-tuple-element.7.own_ref), channel_id=1, source_target_pairs={{0,4},{4,0},{1,5},{5,1},{2,6},{6,2},{3,7},{7,3},{8,12},{12,8},{9,1... | collective-permute-start | bytes 196616 | tf_op jit(solution)/shard_map/ppermute | solution.py:331
  53.8 43.1 %copy-start = (f32[512,256]{1,0:T(8,128)S(1)}, f32[512,256]{1,0:T(8,128)}, u32[]{:S(2)}) copy-start(f32[512,256]{1,0:T(8,128)} %k_ref.1) | copy-start | bytes 1572868
  53.8 43.1 %copy-start.1 = (f32[512,256]{1,0:T(8,128)S(1)}, f32[512,256]{1,0:T(8,128)}, u32[]{:S(2)}) copy-start(f32[512,256]{1,0:T(8,128)} %v_ref.1) | copy-start | bytes 1572868
  53.8 43.1 %copy-start.2 = (f32[512,256]{1,0:T(8,128)S(1)}, f32[512,256]{1,0:T(8,128)}, u32[]{:S(2)}) copy-start(f32[512,256]{1,0:T(8,128)} %g_ref.1) | copy-start | bytes 1572868

commit v9 on v7

--- a/solution.py
+++ b/solution.py
@@ -250,6 +250,8 @@
 
     for q in range(QUARTERS):
         rows = slice(q * SIDE, (q + 1) * SIDE)
+        gf_ref[rows, :] = in_ref[pl.ds(16 + q, members, stride=OUT_ROWS), :].T
+        send(gf_ref, gf_hbm, q)
         for h in range(HALVES):
             cols = slice(h * SIDE, (h + 1) * SIDE)
             back = in_ref[pl.ds(8 + h * QUARTERS + q, members, stride=OUT_ROWS), :].T
@@ -262,8 +264,6 @@
             conv = in_ref[pl.ds(h * QUARTERS + q, members, stride=OUT_ROWS), :].T
             gq_ref[rows, cols] = conv * g_ref[rows, cols]
         send(gq_ref, gq_hbm, q)
-        gf_ref[rows, :] = in_ref[pl.ds(16 + q, members, stride=OUT_ROWS), :].T
-        send(gf_ref, gf_hbm, q)
     for copy in copies:
         copy.wait()
 

time: 99.3 us -> 99.3 us (level)
  no operation moved by 1% of the time
where the time goes in v9:
time: 99.3 us; the launch traced here: 98.3 us
  blocking collectives  87.4 us (88%)
  Pallas kernels  7.53 us (8%)
  starting transfers between devices  2.54 us (3%)
    all_to_all x2, blocking collectives, exchange(): lax.all_to_all(parted, ('near', 'seq'), 0, 0, tiled=True)  87.4 us
    pallas_call x5, Pallas kernels, call(): pl.pallas_call(kernel, out_shape=[jax.ShapeDtypeStruct(shape, F32) for sh...  7.53 us
    ppermute x1, starting transfers between devices, local(): other = lax.ppermute(corr, 'far', [(0, 1), (1, 0)])  2.54 us
  transfers between devices with their start and end apart: 1, of which 1 were waited for; matrix products, arithmetic and copies ran while one was open for 0% of the time, Pallas kernels for 2%

profile of v9, /device:TPU:1, one launch (start us, length us, event | category | flops | bytes accessed | tf_op | source)
XLA Modules:
  0.0 98.3 jit_solution(10528969639478582845)
XLA Ops:
  0.6 1.9 %pack.1 = f32[2176,128]{1,0:T(8,128)S(1)} custom-call(s32[1]{0:T(128)} %bitcast.near_ref, f32[512,256]{1,0:T(8,128)} %k_ref.1, f32[512,256]{1,0:T(8,128)} %v_ref.1, f32[512,256]{1,0:T(8,128)} %g_ref.1, f32[512,256]{1,0:T(8,128)} %q_hbm.1, f32[512,128]{1,0:T(8,128)} %f_hbm.1), custom_call_target="tpu_custom_call" | custom-call | bytes 3473412 | tf_op jit(solution)/shard_map/pack/pallas_call | solution.py:280
  2.5 0.0 copy-start.3
  2.5 0.0 copy-start.4
  2.5 0.0 copy-start.5
  2.5 0.0 copy-start.6
  2.5 0.0 copy-start.7
  2.6 44.3 %all_to_all.10 = f32[128,17,1,128]{3,2,1,0:T(1,128)S(1)} all-to-all(f32[128,17,1,128]{3,2,1,0:T(1,128)S(1)} %bitcast.9), channel_id=1, replica_groups=mesh['seq'=32,'far'=2,'near'=4] {'near','seq'}, dimensions={0} | all-to-all | bytes 2228224 | tf_op jit(solution)/shard_map/all_to_all | solution.py:295
  46.9 0.0 copy-done.3
  46.9 0.0 copy-done.4
  46.9 0.0 copy-done.5
  46.9 0.0 copy-done.6
  46.9 0.0 copy-done.7
  46.9 2.1 %ahead.1 = (f32[128,128]{1,0:T(8,128)S(1)}, f32[1024,256]{1,0:T(8,128)S(1)}, f32[1024,256]{1,0:T(8,128)S(1)}) custom-call(f32[2176,128]{1,0:T(8,128)S(1)} %bitcast.7, bf16[256,384]{1,0:T(8,128)(2,1)S(1)} %copy-done.5, bf16[256,256]{1,0:T(8,128)(2,1)S(1)} %copy-done.7, bf16[768,256]{1,0:T(8,128)(2,1)S(1)} %copy-done.4, bf16[768,256]{1,0:T(8,128)(2,1)S(1)} %copy-done.3, ...), custom_call_target="tpu_custom_call" | custom-call | flops 1000000000 | bytes 4521984 | tf_op jit(solution)/shard_map/ahead/pallas_call | solution.py:280
  49.1 2.5 %collective-permute-start = (f32[128,128]{1,0:T(8,128)S(1)}, f32[128,128]{1,0:T(8,128)S(1)}, u32[]{:S(2)}, u32[]{:S(2)}) collective-permute-start(f32[128,128]{1,0:T(8,128)S(1)} %get-tuple-element.7.own_ref), channel_id=1, source_target_pairs={{0,4},{4,0},{1,5},{5,1},{2,6},{6,2},{3,7},{7,3},{8,12},{12,8},{9,1... | collective-permute-start | bytes 196616 | tf_op jit(solution)/shard_map/ppermute | solution.py:326
  51.6 2.1 %behind.1._ = f32[2560,128]{1,0:T(8,128)S(1)} custom-call(f32[2176,128]{1,0:T(8,128)S(1)} %bitcast.8, f32[1024,256]{1,0:T(8,128)S(1)} %get-tuple-element.8.gated_ref, f32[1024,256]{1,0:T(8,128)S(1)} %get-tuple-element.9.grad_ref, bf16[256,384]{1,0:T(8,128)(2,1)S(1)} %copy-done.5, bf16[256,256]{1,0:T(8,128)(2,1)S(1)} %copy-done.7, ...), custom_call_target="tpu_custom_call" | custom-call | flops 1000000000 | bytes 5767168 | tf_op jit(solution)/shard_map/behind/pallas_call | solution.py:280
  53.7 0.1 collective-permute-done.other_ref
  53.8 0.0 copy-start
  53.8 0.0 copy-start.1
  53.8 0.0 copy-start.2
  53.8 43.0 %all_to_all.11 = f32[128,5,4,128]{3,2,1,0:T(4,128)S(1)} all-to-all(f32[128,5,4,128]{3,2,1,0:T(4,128)S(1)} %bitcast.5), channel_id=1, replica_groups=mesh['seq'=32,'far'=2,'near'=4] {'near','seq'}, dimensions={0} | all-to-all | bytes 2621440 | tf_op jit(solution)/shard_map/all_to_all | solution.py:295
  96.9 0.0 copy-done
  96.9 0.0 copy-done.1
  96.9 0.0 copy-done.2
  96.9 1.5 %unpack.1 = (f32[512,256]{1,0:T(8,128)}, f32[512,256]{1,0:T(8,128)}, f32[512,256]{1,0:T(8,128)}, f32[512,128]{1,0:T(8,128)}) custom-call(f32[2560,128]{1,0:T(8,128)S(1)} %bitcast.6, f32[512,256]{1,0:T(8,128)S(1)} %copy-done.2, f32[512,256]{1,0:T(8,128)S(1)} %copy-done.1, f32[512,256]{1,0:T(8,128)S(1)} %copy-done), custom_call_target="tpu_custom_call" | custom-call | bytes 4718592 | tf_op jit(solution)/shard_map/unpack/pallas_call | solution.py:280
  (1 shorter events, 0.0 us)
Async XLA Ops:
  2.5 44.4 %copy-start.3 = (bf16[768,256]{1,0:T(8,128)(2,1)S(1)}, bf16[768,256]{1,0:T(8,128)(2,1)}, u32[]{:S(2)}) copy-start(bf16[768,256]{1,0:T(8,128)(2,1)} %constant.17.clone.behind_ref) | copy-start | bytes 1179652
  2.5 44.4 %copy-start.4 = (bf16[768,256]{1,0:T(8,128)(2,1)S(1)}, bf16[768,256]{1,0:T(8,128)(2,1)}, u32[]{:S(2)}) copy-start(bf16[768,256]{1,0:T(8,128)(2,1)} %constant.16.clone.ahead_ref) | copy-start | bytes 1179652
  2.5 44.4 %copy-start.5 = (bf16[256,384]{1,0:T(8,128)(2,1)S(1)}, bf16[256,384]{1,0:T(8,128)(2,1)}, u32[]{:S(2)}) copy-start(bf16[256,384]{1,0:T(8,128)(2,1)} %constant.14.clone.into_ref) | copy-start | bytes 589828
  2.5 44.4 %copy-start.6 = (f32[128,256]{1,0:T(8,128)S(1)}, f32[128,256]{1,0:T(8,128)}, u32[]{:S(2)}) copy-start(f32[128,256]{1,0:T(8,128)} %constant.18.clone.twist_ref) | copy-start | bytes 393220
  2.5 44.4 %copy-start.7 = (bf16[256,256]{1,0:T(8,128)(2,1)S(1)}, bf16[256,256]{1,0:T(8,128)(2,1)}, u32[]{:S(2)}) copy-start(bf16[256,256]{1,0:T(8,128)(2,1)} %constant.15.clone.back_ref) | copy-start | bytes 393220
  49.1 4.7 %collective-permute-start = (f32[128,128]{1,0:T(8,128)S(1)}, f32[128,128]{1,0:T(8,128)S(1)}, u32[]{:S(2)}, u32[]{:S(2)}) collective-permute-start(f32[128,128]{1,0:T(8,128)S(1)} %get-tuple-element.7.own_ref), channel_id=1, source_target_pairs={{0,4},{4,0},{1,5},{5,1},{2,6},{6,2},{3,7},{7,3},{8,12},{12,8},{9,1... | collective-permute-start | bytes 196616 | tf_op jit(solution)/shard_map/ppermute | solution.py:326
  53.8 43.1 %copy-start = (f32[512,256]{1,0:T(8,128)S(1)}, f32[512,256]{1,0:T(8,128)}, u32[]{:S(2)}) copy-start(f32[512,256]{1,0:T(8,128)} %k_ref.1) | copy-start | bytes 1572868
  53.8 43.1 %copy-start.1 = (f32[512,256]{1,0:T(8,128)S(1)}, f32[512,256]{1,0:T(8,128)}, u32[]{:S(2)}) copy-start(f32[512,256]{1,0:T(8,128)} %v_ref.1) | copy-start | bytes 1572868
  53.8 43.1 %copy-start.2 = (f32[512,256]{1,0:T(8,128)S(1)}, f32[512,256]{1,0:T(8,128)}, u32[]{:S(2)}) copy-start(f32[512,256]{1,0:T(8,128)} %g_ref.1) | copy-start | bytes 1572868
